TPU v7x, 128 devices: a whole 4x4x4 slice. The times are simulated.
128 devices in a mesh: blk: 64 (over y_lo, x, z, core), feat: 2 (over y_hi).
Axes of the slice: x: 4, y: 4 (y_hi: 2, y_lo: 2; y = y_hi * 2 + y_lo), z: 4, core: 2. Of those that a mesh axis runs over, the one named last changes fastest.
Arguments:
- inputs: bfloat16 [131072, 128], P('blk'), may hold values from -6 to 6
- weight_h: bfloat16 [128, 128], P(None, 'feat'), may hold values from -0.5 to 0.5
- weight_s: bfloat16 [128, 4], replicated, may hold values from -0.75 to 0.75
- cotangent: bfloat16 [131072, 128], P('blk', 'feat'), may hold values from -6 to 6
- ranks: int32 [131072], P('blk'), may hold values from 0 to 2047, as said below
- counts: int32 [64], replicated, may hold values from 1024 to 2048, as said below
Outputs:
- grad_inputs: bfloat16 [131072, 128], P('blk', 'feat')
- grad_weight_h: float32 [128, 128], P(None, 'feat')
- grad_weight_s: float32 [128, 4], replicated
Inputs may be any that keep to these rules, and one draw needn't show every extreme that they name: Within each block of 2048 hits the ranks are a permutation of 0 to 2047. `counts`: some block is full and some block holds exactly 1024 live hits.
All inputs are finite; a program needn't handle non-finite values.
Results may differ from a plain program's by a relative error of at most 0.0054.
Values may be sent and summed in bfloat16 or wider, within the bound.
No kernel may reach another device: no remote copies, remote signals or barrier semaphores. Data moves between devices by JAX's collectives and lax.ppermute only.
A program may use at most 128 MiB of HBM per device.

v0:
```python
import jax
import jax.numpy as jnp
from jax import lax
from jax.sharding import PartitionSpec as P

WINDOW = 2


highest = lax.Precision.HIGHEST


def shifted(block, axis, distance):
    devices = range(lax.axis_size(axis))
    route = [((i - distance) % len(devices), i) for i in devices]
    return lax.ppermute(block, axis, route)


def sides_of(panel, weight_full, weight_s):
    masked = panel[0]
    scaled = panel[1]
    hidden = jnp.dot(masked, weight_full, preferred_element_type=jnp.float32).astype(jnp.bfloat16)
    coords = jnp.einsum("bd,dc->cb", masked, weight_s, preferred_element_type=jnp.float32)
    return (scaled, hidden, coords)


def pair_terms(near, far, col_start, col_count, both):
    scaled_a, hidden_a, coords_a = near
    scaled_b, hidden_b, coords_b = far
    square = jnp.zeros((coords_a.shape[1], coords_b.shape[1]), jnp.float32)
    for component in range(coords_a.shape[0]):
        square = square + (coords_a[component][:, None] - coords_b[component][None, :]) ** 2
    kernel = jnp.exp(-square)
    contract = (((1,), (1,)), ((), ()))
    inner = lax.dot_general(scaled_a, hidden_b, contract, preferred_element_type=jnp.float32)
    inner = inner + lax.dot_general(
        hidden_a, scaled_b, contract, preferred_element_type=jnp.float32
    )
    force = -kernel * inner
    rounded = kernel.astype(jnp.bfloat16)
    half_b = lax.dynamic_slice_in_dim(scaled_b, col_start, col_count, 1)
    hidden_near = jnp.einsum("kj,jf->fk", rounded, half_b, preferred_element_type=jnp.float32)
    coord_near = 2.0 * (
        coords_a * jnp.sum(force, 1)[None, :]
        - jnp.einsum("kj,cj->ck", force, coords_b, precision=highest)
    )
    near_part = jnp.concatenate([hidden_near, coord_near], 0)
    if not both:
        return (near_part, near_part)
    half_a = lax.dynamic_slice_in_dim(scaled_a, col_start, col_count, 1)
    hidden_far = jnp.einsum("kj,kf->fj", rounded, half_a, preferred_element_type=jnp.float32)
    coord_far = 2.0 * (
        coords_b * jnp.sum(force, 0)[None, :]
        - jnp.einsum("kj,ck->cj", force, coords_a, precision=highest)
    )
    far_part = jnp.concatenate([hidden_far, coord_far], 0)
    return (near_part, far_part)


def local(inputs, weight_h, weight_s, cotangent, ranks, counts):
    block_total = lax.axis_size("blk")
    position = lax.axis_index("blk")
    my_half = lax.axis_index("feat")
    width = cotangent.shape[1]
    hit_total = inputs.shape[0]
    blocks = jnp.arange(block_total, dtype=jnp.int32)
    spacing = (blocks - position) % block_total
    loop_gap = jnp.minimum(spacing, block_total - spacing)
    own_count = jnp.sum(jnp.where(blocks == position, counts, 0))
    window_count = jnp.sum(jnp.where(loop_gap <= WINDOW, counts, 0))
    live = (ranks < own_count).astype(jnp.float32)
    scale = 1.0 / jnp.sqrt(window_count.astype(jnp.float32))
    full_grad, weight_full = (
        lax.all_gather(cotangent, "feat", axis=1, tiled=True),
        lax.all_gather(weight_h, "feat", axis=1, tiled=True),
    )
    scaled = (full_grad.astype(jnp.float32) * (live * scale)[:, None]).astype(jnp.bfloat16)
    masked = inputs * live.astype(jnp.bfloat16)[:, None]
    panel = jnp.stack([masked, scaled])
    own_side = sides_of(panel, weight_full, weight_s)
    col_start = my_half * width
    near_rows, unused = pair_terms(own_side, own_side, col_start, width, False)
    far_sum = jnp.zeros((width + weight_s.shape[1], hit_total), jnp.float32)
    for offset in range(1, WINDOW + 1):
        remote = shifted(panel, "blk", -offset)
        near_part, far_part = pair_terms(
            own_side, sides_of(remote, weight_full, weight_s), col_start, width, True
        )
        returned = shifted(far_part, "blk", offset)
        near_rows = near_rows + near_part
        far_sum = far_sum + returned
    totals = near_rows + far_sum
    hidden_grad = (totals[:width] * live[None, :]).astype(jnp.bfloat16)
    coord_grad = totals[width:]
    grad_wh_part = jnp.einsum("bd,fb->df", masked, hidden_grad, preferred_element_type=jnp.float32)
    grad_ws_part = jnp.einsum(
        "bd,cb->dc", masked.astype(jnp.float32), coord_grad, precision=highest
    )
    grad_weight_h, grad_weight_s = lax.psum((grad_wh_part, grad_ws_part), "blk")
    weight_s_wide = weight_s.astype(jnp.float32)
    leading = (my_half == 0).astype(jnp.float32)
    partial_term = jnp.einsum(
        "fb,df->bd", hidden_grad, weight_h, preferred_element_type=jnp.float32
    )
    partial_term = partial_term + leading * jnp.einsum(
        "cb,dc->bd", coord_grad, weight_s_wide, precision=highest
    )
    grad_inputs = lax.psum_scatter(partial_term, "feat", scatter_dimension=1, tiled=True)
    return (grad_inputs.astype(jnp.bfloat16), grad_weight_h, grad_weight_s)


def solution(mesh):
    placed = (P("blk", None), P(None, "feat"), P(), P("blk", "feat"), P("blk"), P())
    return jax.shard_map(
        local,
        mesh=mesh,
        in_specs=placed,
        out_specs=(P("blk", "feat"), P(None, "feat"), P()),
        check_vma=False,
    )
```

profile of v0, /device:TPU:8, one launch (start us, length us, event | category | flops | bytes accessed | tf_op | source)
XLA Modules:
  0.0 518.6 jit_solution(8377369472749263844)
XLA Ops:
  7.2 0.0 copy-start
  7.2 0.0 reduce-scatter.2.cloned.1.call-start
  7.2 1.3 fusion.56
  9.2 1.9 fusion.61
  11.2 1.2 copy.9
  12.4 10.4 %all_gather.6 = bf16[2048,128]{0,1:T(8,128)(2,1)S(1)} all-gather(bf16[2048,64]{0,1:T(8,128)(2,1)} %param.9), channel_id=1, replica_groups=mesh['blk'=64,'feat'=2] {'feat'}, dimensions={1}, use_global_device_ids=true | all-gather | bytes 786432 | tf_op jit(solution)/shard_map/all_gather | solution.py:73
  22.9 0.1 fusion.93
  23.0 1.1 pad_maximum_fusion
  24.1 6.1 %collective-permute-start.1 = (bf16[2,2048,128]{1,2,0:T(8,128)(2,1)}, bf16[2,2048,128]{1,2,0:T(8,128)(2,1)S(1)}, u32[]{:S(2)}, u32[]{:S(2)}) collective-permute-start(bf16[2,2048,128]{1,2,0:T(8,128)(2,1)} %pad_maximum_fusion), channel_id=1, source_target_pairs={{4,0},{6,2},{8,4},{10,6},{12,8},{14,10},{16,12},{18,14},{20,16},{2... | collective-permute-start | bytes 3145736 | tf_op jit(solution)/shard_map/ppermute | solution.py:15
  30.3 0.1 multiply_convert_fusion
  30.4 6.1 %all_gather.7 = bf16[128,128]{0,1:T(8,128)(2,1)S(1)} all-gather(bf16[128,64]{0,1:T(8,128)(2,1)} %param.7), channel_id=1, replica_groups=mesh['blk'=64,'feat'=2] {'feat'}, dimensions={1}, use_global_device_ids=true | all-gather | bytes 49152 | tf_op jit(solution)/shard_map/all_gather | solution.py:74
  36.5 0.2 fusion.31
  36.7 0.3 convolution_convert_fusion.2
  37.1 2.4 fusion.66
  39.5 12.4 %fusion.65 = (f32[2048]{0:T(1024)S(1)}, f32[2048,2048]{0,1:T(8,128)}) fusion(f32[2048,2048]{0,1:T(8,128)S(1)} %fusion.66, bf16[2048,128]{1,0:T(8,128)(2,1)S(1)} %convolution_convert_fusion.2, bf16[2048,128]{0,1:T(8,128)(2,1)S(1)} %multiply_convert_fusion, f32[2048]{0:T(1024)S(1)} %bitcast.87, f32[2048]{0:T(1024)S(1)} %bitcast.95, f32[2048]{0:T(1024)S(1)} %bitcast.103, ...), kind=kOutput, calls=%fused_computation.91 | convolution fusion | flops 1140848640 | bytes 34643968 | tf_op jit(solution)/shard_map/dot_general | solution.py:34
  51.9 8.7 %fusion.3 = f32[64,2048]{1,0:T(8,128)} fusion(f32[2048]{0:T(1024)S(1)} %bitcast.88, f32[2048]{0:T(1024)S(1)} %bitcast.96, f32[2048]{0:T(1024)S(1)} %bitcast.104, f32[2048]{0:T(1024)S(1)} %bitcast.80, bf16[2048,128]{0,1:T(8,128)(2,1)S(1)} %multiply_convert_fusion, s32[]{:T(128)S(6)} %select_n.24), kind=kOutput, calls=%fused_computation.9 | convolution fusion | flops 591396864 | bytes 851972 | tf_op jit(solution)/shard_map/kj,jf->fk/dot_general | solution.py:41
  60.6 12.4 %fusion.16 = f32[4,2048]{1,0:T(4,128)} fusion(f32[2048,4]{0,1:T(4,128)S(1)} %fusion.31, f32[2048,2048]{0,1:T(8,128)} %get-tuple-element.26, f32[2048]{0:T(1024)S(1)} %get-tuple-element.25), kind=kOutput, calls=%fused_computation.24 | convolution fusion | flops 201351168 | bytes 16850944 | tf_op jit(solution)/shard_map/kj,cj->ck/dot_general | solution.py:44
  73.0 0.0 collective-permute-done.1
  73.0 0.2 fusion.25
  73.2 0.6 copy-done.7
  73.8 7.9 %fusion.5 = f32[64,2048]{1,0:T(8,128)S(1)} fusion(f32[2048]{0:T(1024)S(1)} %bitcast.114, f32[2048]{0:T(1024)S(1)} %bitcast.117, f32[2048]{0:T(1024)S(1)} %bitcast.120, f32[2048]{0:T(1024)S(1)} %bitcast.111, f32[2048]{0:T(1024)S(1)} %bitcast.89, f32[2048]{0:T(1024)S(1)} %bitcast.97, f32[2048]{0:T(1024)S(1)} %bitcast.105, f32[2048]{0:T(1024)S(1)} %bitcast.81, ...), kind=kOutput, calls=%fused_computation.10 | convolution fusion | flops 591396864 | bytes 851972 | tf_op jit(solution)/shard_map/kj,kf->fj/dot_general | solution.py:50
  81.7 8.8 %fusion.7 = f32[64,2048]{1,0:T(8,128)} fusion(f32[2048]{0:T(1024)S(1)} %bitcast.115, f32[2048]{0:T(1024)S(1)} %bitcast.118, f32[2048]{0:T(1024)S(1)} %bitcast.121, f32[2048]{0:T(1024)S(1)} %bitcast.112, f32[2048]{0:T(1024)S(1)} %bitcast.90, f32[2048]{0:T(1024)S(1)} %bitcast.98, f32[2048]{0:T(1024)S(1)} %bitcast.106, f32[2048]{0:T(1024)S(1)} %bitcast.82, ...), kind=kOutput, calls=%fused_computation.11 | convolution fusion | flops 591396864 | bytes 851972 | tf_op jit(solution)/shard_map/kj,jf->fk/dot_general | solution.py:41
  90.6 1.2 fusion.24
  91.8 8.9 %fusion.9 = f32[64,2048]{1,0:T(8,128)} fusion(f32[2048]{0:T(1024)S(1)} %bitcast.126, f32[2048]{0:T(1024)S(1)} %bitcast.129, f32[2048]{0:T(1024)S(1)} %bitcast.132, f32[2048]{0:T(1024)S(1)} %bitcast.123, f32[2048]{0:T(1024)S(1)} %bitcast.91, f32[2048]{0:T(1024)S(1)} %bitcast.99, f32[2048]{0:T(1024)S(1)} %bitcast.107, f32[2048]{0:T(1024)S(1)} %bitcast.83, ...), kind=kOutput, calls=%fused_computation.12 | convolution fusion | flops 591396864 | bytes 851972 | tf_op jit(solution)/shard_map/kj,kf->fj/dot_general | solution.py:50
  100.8 1.1 slice.88
  101.9 8.7 %fusion.11 = f32[64,2048]{1,0:T(8,128)} fusion(f32[2048]{0:T(1024)S(1)} %bitcast.127, f32[2048]{0:T(1024)S(1)} %bitcast.130, f32[2048]{0:T(1024)S(1)} %bitcast.133, f32[2048]{0:T(1024)S(1)} %bitcast.124, f32[2048]{0:T(1024)S(1)} %bitcast.92, f32[2048]{0:T(1024)S(1)} %bitcast.100, f32[2048]{0:T(1024)S(1)} %bitcast.108, f32[2048]{0:T(1024)S(1)} %bitcast.84, ...), kind=kOutput, calls=%fused_computation.13 | convolution fusion | flops 591396864 | bytes 851972 | tf_op jit(solution)/shard_map/kj,jf->fk/dot_general | solution.py:41
  110.5 8.3 %fusion.17 = f32[2048,2048]{0,1:T(8,128)} fusion(bf16[2048,128]{0,1:T(8,128)(2,1)S(1)} %multiply_convert_fusion, bf16[128,128]{0,1:T(8,128)(2,1)S(1)} %all_gather.7, bf16[2,2048,128]{1,2,0:T(8,128)(2,1)} %collective-permute-done), kind=kOutput, calls=%fused_computation.25 | convolution fusion | flops 1141112832 | bytes 17858560 | tf_op jit(solution)/shard_map/dot_general | solution.py:34
  118.8 14.6 %fusion.60 = (f32[2048]{0:T(1024)S(1)}, f32[2048]{0:T(1024)S(1)}, f32[2048,2048]{0,1:T(8,128)S(1)}) fusion(f32[2048,2048]{0,1:T(8,128)} %fusion.17, bf16[2048,128]{1,0:T(8,128)(2,1)S(1)} %convolution_convert_fusion.2, bf16[2,2048,128]{1,2,0:T(8,128)(2,1)} %collective-permute-done, f32[2048]{0:T(1024)S(1)} %bitcast.128, f32[2048]{0:T(1024)S(1)} %bitcast.93, ...), kind=kOutput, calls=%fused_computation.86 | convolution fusion | flops 1145040896 | bytes 34684928 | tf_op jit(solution)/shard_map/dot_general | solution.py:35
  133.5 13.8 %subtract_multiply_fusion.1 = f32[4,2048]{1,0:T(4,128)S(1)} fusion(f32[2048]{0:T(1024)S(1)} %get-tuple-element.5, f32[2048,4]{0,1:T(4,128)S(1)} %fusion.24, f32[2048,4]{0,1:T(4,128)S(1)} %fusion.31, f32[2048,2048]{0,1:T(8,128)S(1)} %get-tuple-element.27), kind=kOutput, calls=%fused_computation.63 | convolution fusion | flops 201351168 | bytes 16883712 | tf_op jit(solution)/shard_map/kj,ck->cj/dot_general | solution.py:53
  147.3 8.1 %fusion.15 = f32[4,2048]{1,0:T(4,128)S(1)} fusion(f32[2048,4]{0,1:T(4,128)S(1)} %fusion.24, f32[2048,2048]{0,1:T(8,128)S(1)} %get-tuple-element.27, f32[2048]{0:T(1024)S(1)} %get-tuple-element.6, f32[2048,4]{0,1:T(4,128)S(1)} %fusion.31), kind=kOutput, calls=%fused_computation.22 | convolution fusion | flops 201351168 | bytes 16883712 | tf_op jit(solution)/shard_map/kj,cj->ck/dot_general | solution.py:44
  155.5 0.1 collective-permute-start.2
  155.6 7.2 %fusion.18 = f32[2048,2048]{0,1:T(8,128)} fusion(bf16[2048,128]{0,1:T(8,128)(2,1)S(1)} %multiply_convert_fusion, bf16[128,128]{0,1:T(8,128)(2,1)S(1)} %all_gather.7, bf16[2,2048,128]{1,2,0:T(8,128)(2,1)S(1)} %collective-permute-done.1), kind=kOutput, calls=%fused_computation.26 | convolution fusion | flops 1141112832 | bytes 17858560 | tf_op jit(solution)/shard_map/dot_general | solution.py:34
  162.8 14.5 %fusion.59 = (f32[2048]{0:T(1024)S(1)}, f32[2048]{0:T(1024)S(1)}, f32[2048,2048]{0,1:T(8,128)S(1)}) fusion(f32[2048,2048]{0,1:T(8,128)} %fusion.18, bf16[2048,128]{1,0:T(8,128)(2,1)S(1)} %convolution_convert_fusion.2, bf16[2,2048,128]{1,2,0:T(8,128)(2,1)S(1)} %collective-permute-done.1, f32[2048]{0:T(1024)S(1)} %bitcast.116, f32[2048]{0:T(1024)S(1)} %bitcast.94, ...), kind=kOutput, calls=%fused_computation.85 | convolution fusion | flops 1145040896 | bytes 34684928 | tf_op jit(solution)/shard_map/dot_general | solution.py:35
  177.4 0.0 copy-start.9
  177.4 0.0 copy-start.13
  177.4 13.8 %subtract_multiply_fusion = f32[4,2048]{1,0:T(4,128)S(1)} fusion(f32[2048]{0:T(1024)S(1)} %get-tuple-element.3, f32[2048,4]{0,1:T(4,128)S(1)} %copy-done.8, f32[2048,4]{0,1:T(4,128)S(1)} %fusion.31, f32[2048,2048]{0,1:T(8,128)S(1)} %get-tuple-element.28), kind=kOutput, calls=%fused_computation.62 | convolution fusion | flops 201351168 | bytes 16883712 | tf_op jit(solution)/shard_map/kj,ck->cj/dot_general | solution.py:53
  191.2 0.0 copy-start.11
  191.3 0.7 collective-permute-start.3
  192.0 7.9 %fusion.14 = f32[4,2048]{1,0:T(4,128)S(1)} fusion(f32[2048,4]{0,1:T(4,128)S(1)} %copy-done.8, f32[2048,2048]{0,1:T(8,128)S(1)} %get-tuple-element.28, f32[2048]{0:T(1024)S(1)} %get-tuple-element.4, f32[2048,4]{0,1:T(4,128)S(1)} %fusion.31), kind=kOutput, calls=%fused_computation.20 | convolution fusion | flops 201351168 | bytes 16883712 | tf_op jit(solution)/shard_map/kj,cj->ck/dot_general | solution.py:44
  199.9 11.6 %collective-permute-done.3 = f32[68,2048]{1,0:T(8,128)S(1)} collective-permute-done((f32[68,2048]{1,0:T(8,128)S(1)}, f32[68,2048]{1,0:T(8,128)S(1)}, u32[]{:S(2)}, u32[]{:S(2)}) %collective-permute-start.3) | collective-permute-done | bytes 557088 | tf_op jit(solution)/shard_map/ppermute | solution.py:15
  211.5 1.3 fusion.20
  212.8 0.3 fusion.45
  213.2 1.6 fusion.13
  214.8 0.0 reduce-scatter.2.cloned.1.call-update
  214.9 0.5 fusion.26
  215.4 0.3 fusion.28
  215.7 293.9 %all-reduce = (f32[128,64]{0,1:T(8,128)}, f32[128,4]{0,1:T(4,128)}) all-reduce(f32[128,64]{0,1:T(8,128)S(1)} %fusion.28, f32[128,4]{0,1:T(4,128)S(1)} %fusion.26), channel_id=1, replica_groups=mesh['blk'=64,'feat'=2] {'blk'}, use_global_device_ids=true, to_apply=%region_8.9 | all-reduce | flops 8704 | bytes 69632 | tf_op jit(solution)/shard_map/psum | solution.py:98
  509.6 1.8 convert_element_type.57
  (36 shorter events, 0.3 us)
Async XLA Ops:
  7.2 29.3 %copy-start = (bf16[128,4]{0,1:T(4,128)(2,1)S(1)}, bf16[128,4]{0,1:T(4,128)(2,1)}, u32[]{:S(2)}) copy-start(bf16[128,4]{0,1:T(4,128)(2,1)} %param.8) | copy-start | bytes 3076
  7.2 502.4 %reduce-scatter.2.cloned.1.call-start = ((), (), s32[]{:S(2)}) async-start(), calls=%async_computation.1 | async-start | bytes 1572864 | tf_op jit(solution)/shard_map/reduce_scatter | solution.py:107
  11.2 40.7 %copy-start.10 = (bf16[2048]{0:T(1024)(128)(2,1)}, bf16[2048]{0:T(1024)(128)(2,1)S(1)}, u32[]{:S(2)}) copy-start(bf16[2048]{0:T(1024)(128)(2,1)S(1)} %convert_convert_fusion) | copy-start | bytes 12292
  12.4 39.5 %copy-start.1 = (bf16[2048,128]{0,1:T(8,128)(2,1)}, bf16[2048,128]{0,1:T(8,128)(2,1)S(1)}, u32[]{:S(2)}) copy-start(bf16[2048,128]{0,1:T(8,128)(2,1)S(1)} %copy.9) | copy-start | bytes 1572868
  24.1 48.8 %collective-permute-start.1 = (bf16[2,2048,128]{1,2,0:T(8,128)(2,1)}, bf16[2,2048,128]{1,2,0:T(8,128)(2,1)S(1)}, u32[]{:S(2)}, u32[]{:S(2)}) collective-permute-start(bf16[2,2048,128]{1,2,0:T(8,128)(2,1)} %pad_maximum_fusion), channel_id=1, source_target_pairs={{4,0},{6,2},{8,4},{10,6},{12,8},{14,10},{16,12},{18,14},{20,16},{2... | collective-permute-start | bytes 3145736 | tf_op jit(solution)/shard_map/ppermute | solution.py:15
  30.3 60.3 %collective-permute-start = (bf16[2,2048,128]{1,2,0:T(8,128)(2,1)}, bf16[2,2048,128]{1,2,0:T(8,128)(2,1)}, u32[]{:S(2)}, u32[]{:S(2)}) collective-permute-start(bf16[2,2048,128]{1,2,0:T(8,128)(2,1)} %pad_maximum_fusion), channel_id=1, source_target_pairs={{2,0},{4,2},{6,4},{8,6},{10,8},{12,10},{14,12},{16,14},{18,16},{20... | collective-permute-start | bytes 3145736 | tf_op jit(solution)/shard_map/ppermute | solution.py:15
  73.2 0.6 copy-start.7
  133.5 22.0 %copy-start.3 = (f32[64,2048]{1,0:T(8,128)S(1)}, f32[64,2048]{1,0:T(8,128)}, u32[]{:S(2)}) copy-start(f32[64,2048]{1,0:T(8,128)} %fusion.9) | copy-start | bytes 1572868
  155.5 44.4 %collective-permute-start.2 = (f32[68,2048]{1,0:T(8,128)S(1)}, f32[68,2048]{1,0:T(8,128)}, u32[]{:S(2)}, u32[]{:S(2)}) collective-permute-start(f32[68,2048]{1,0:T(8,128)S(1)} %pad_maximum_fusion.1), channel_id=1, source_target_pairs={{126,0},{0,2},{2,4},{4,6},{6,8},{8,10},{10,12},{12,14},{14,16},{16... | collective-permute-start | bytes 1671176 | tf_op jit(solution)/shard_map/ppermute | solution.py:15
  162.8 14.5 %copy-start.8 = (f32[2048,4]{0,1:T(4,128)S(1)}, f32[2048,4]{0,1:T(4,128)}, u32[]{:S(2)}) copy-start(f32[2048,4]{0,1:T(4,128)} %copy-done.7) | copy-start | bytes 98308
  177.3 34.2 %copy-start.4 = (f32[64,2048]{1,0:T(8,128)S(1)}, f32[64,2048]{1,0:T(8,128)}, u32[]{:S(2)}) copy-start(f32[64,2048]{1,0:T(8,128)} %fusion.3) | copy-start | bytes 1572868
  177.4 34.2 %copy-start.5 = (f32[64,2048]{1,0:T(8,128)S(1)}, f32[64,2048]{1,0:T(8,128)}, u32[]{:S(2)}) copy-start(f32[64,2048]{1,0:T(8,128)} %fusion.7) | copy-start | bytes 1572868
  177.4 34.2 %copy-start.6 = (f32[64,2048]{1,0:T(8,128)S(1)}, f32[64,2048]{1,0:T(8,128)}, u32[]{:S(2)}) copy-start(f32[64,2048]{1,0:T(8,128)} %fusion.11) | copy-start | bytes 1572868
  177.4 34.2 %copy-start.9 = (f32[4,2048]{1,0:T(4,128)S(1)}, f32[4,2048]{1,0:T(4,128)}, u32[]{:S(2)}) copy-start(f32[4,2048]{1,0:T(4,128)} %fusion.16) | copy-start | bytes 98308
  177.4 35.4 %copy-start.12 = (f32[2048]{0:T(1024)S(1)}, f32[2048]{0:T(1024)}, u32[]{:S(2)}) copy-start(f32[2048]{0:T(1024)} %get-tuple-element.11) | copy-start | bytes 24580
  177.4 35.4 %copy-start.13 = (bf16[128,64]{0,1:T(8,128)(2,1)S(1)}, bf16[128,64]{0,1:T(8,128)(2,1)}, u32[]{:S(2)}) copy-start(bf16[128,64]{0,1:T(8,128)(2,1)} %param.7) | copy-start | bytes 49156
  191.2 23.6 %copy-start.2 = (bf16[2048,128]{0,1:T(8,128)(2,1)S(1)}, bf16[2048,128]{0,1:T(8,128)(2,1)}, u32[]{:S(2)}) copy-start(bf16[2048,128]{0,1:T(8,128)(2,1)} %copy-done.1) | copy-start | bytes 1572868
  191.2 23.6 %copy-start.11 = (bf16[2048]{0:T(1024)(128)(2,1)S(1)}, bf16[2048]{0:T(1024)(128)(2,1)}, u32[]{:S(2)}) copy-start(bf16[2048]{0:T(1024)(128)(2,1)} %copy-done.10) | copy-start | bytes 12292
  191.3 20.2 %collective-permute-start.3 = (f32[68,2048]{1,0:T(8,128)S(1)}, f32[68,2048]{1,0:T(8,128)S(1)}, u32[]{:S(2)}, u32[]{:S(2)}) collective-permute-start(f32[68,2048]{1,0:T(8,128)S(1)} %pad_maximum_fusion.2), channel_id=1, source_target_pairs={{124,0},{126,2},{0,4},{2,6},{4,8},{6,10},{8,12},{10,14},{12,16},{1... | collective-permute-start | bytes 1671176 | tf_op jit(solution)/shard_map/ppermute | solution.py:15
Sparse Core Ops, SparseCore 0:
  215.0 48.7 reduce-scatter.1
where the time goes:
time: 529 us; the launch traced here: 519 us
  blocking collectives  310 us (59%)
  matrix products  163 us (31%)
  between operations  15.5 us (3%)
  waiting for transfers between devices  11.6 us (2%)
  other arithmetic  7.74 us (1%)
  starting transfers between devices  6.89 us (1%)
    psum x1, blocking collectives, local(): grad_weight_h, grad_weight_s = lax.psum((grad_wh_part, grad_ws_part), 'blk')  294 us
    dot_general x3, matrix products, pair_terms(): lax.dot_general(hidden_a, scaled_b, contract, preferred_element_type=jnp....  31.5 us
    dot_general x3, matrix products, pair_terms(): jnp.einsum('kj,cj->ck', force, coords_b, precision=highest)  28.5 us
    dot_general x3, matrix products, pair_terms(): lax.dot_general(scaled_a, hidden_b, contract, preferred_element_type=jnp....  27.9 us
    dot_general x2, matrix products, pair_terms(): jnp.einsum('kj,ck->cj', force, coords_a, precision=highest)  27.7 us
    dot_general x3, matrix products, pair_terms(): jnp.einsum('kj,jf->fk', rounded, half_b, preferred_element_type=jnp.float32)  26.2 us
    dot_general x2, matrix products, pair_terms(): jnp.einsum('kj,kf->fj', rounded, half_a, preferred_element_type=jnp.float32)  16.8 us
    ppermute x4, waiting for transfers between devices, shifted(): return lax.ppermute(block, axis, route)  11.6 us
  transfers between devices with their start and end apart: 5, of which 1 were waited for; matrix products, arithmetic and copies ran while one was open for 19% of the time, Pallas kernels for 0%

commit v1 on v0

v1 whole, which is shorter than its diff:
```python
import functools
import math

import jax
import jax.numpy as jnp
from jax import lax
from jax.experimental import pallas as pl
from jax.experimental.pallas import tpu as pltpu
from jax.sharding import PartitionSpec as P

WINDOW = 2
LOG2E = math.log2(math.e)
NT = (((1,), (1,)), ((), ()))
F32 = jnp.float32
BF16 = jnp.bfloat16
highest = lax.Precision.HIGHEST
ROW_TILE = 512
COL_TILE = 1024


def moved(x, target):
    blks, feats = lax.axis_size("blk"), lax.axis_size("feat")
    route = []
    for b in range(blks):
        for f in range(feats):
            to_b, to_f = target(b, f)
            route.append((b * feats + f, (to_b % blks) * feats + to_f))
    return lax.ppermute(x, ("blk", "feat"), route)


def split3(v):
    high = v.astype(BF16).astype(F32)
    rest = v - high
    mid = rest.astype(BF16).astype(F32)
    return high, mid, rest - mid


def norm_rows(v, row, first):
    parts = split3(-LOG2E * jnp.sum(v * v, axis=0, keepdims=True))
    out = jnp.where(row < 6, 1.0, 0.0)
    for i, part in enumerate(parts):
        out = jnp.where(row == first + i, part, out)
    return out


def far_features(coords):
    row = lax.broadcasted_iota(jnp.int32, coords.shape, 0)
    b1, b2, b3 = split3(coords)
    zero = jnp.zeros_like(coords)
    dist = jnp.concatenate([b1, b2, b3, b1, b2, b1, norm_rows(coords, row, 3), zero], 0)
    moment = jnp.concatenate([jnp.where(row == 4, 1.0, b1), b2, b3, zero], 0)
    return dist.astype(BF16), moment.astype(BF16)


def near_features(coords):
    row = lax.broadcasted_iota(jnp.int32, coords.shape, 0)
    a1, a2, a3 = split3((2.0 * LOG2E) * coords)
    zero = jnp.zeros_like(coords)
    dist = jnp.concatenate([a1, a1, a1, a2, a2, a3, norm_rows(coords, row, 0), zero], 0)
    return jnp.transpose(dist).astype(BF16)


def window_terms(near_dist, near_mix, mb, sb, w_t, ws_t, dist_sc, mix_sc, mom_sc, oh, oc, acc):
    dist, moment = far_features(
        lax.dot_general(ws_t[...], mb[...], NT, preferred_element_type=F32)
    )
    dist_sc[...] = dist
    mom_sc[...] = moment
    half = mix_sc.shape[0] // 2
    mix_sc[:half, :] = lax.dot_general(
        w_t[...], mb[...], NT, preferred_element_type=F32
    ).astype(BF16)
    mix_sc[half:, :] = sb[...]
    rows, cols = near_dist.shape[0], mb.shape[0]
    for r in range(0, rows, ROW_TILE):
        rs = slice(r, r + ROW_TILE)
        total_h = total_c = None
        if acc is not None:
            total_h, total_c = acc[0][rs, :], acc[1][rs, :]
        for c in range(0, cols, COL_TILE):
            cs = slice(c, c + COL_TILE)
            power = jnp.dot(near_dist[rs, :], dist_sc[:, cs], preferred_element_type=F32)
            inner = jnp.dot(near_mix[rs, :], mix_sc[:, cs], preferred_element_type=F32)
            kernel = jnp.exp2(power)
            force = (kernel * inner).astype(BF16)
            part_h = lax.dot_general(
                kernel.astype(BF16), sb[:, cs], NT, preferred_element_type=F32
            )
            part_c = lax.dot_general(force, mom_sc[:, cs], NT, preferred_element_type=F32)
            total_h = part_h if total_h is None else total_h + part_h
            total_c = part_c if total_c is None else total_c + part_c
        oh[rs, :] = total_h
        oc[rs, :] = total_c


def first_body(ma, sa, mb, sb, w, w_t, ws_t, oh, oc, near_dist, near_mix, dist_sc, mix_sc, mom_sc):
    near_dist[...] = near_features(
        lax.dot_general(ws_t[...], ma[...], NT, preferred_element_type=F32)
    )
    half = near_mix.shape[1] // 2
    near_mix[:, :half] = jnp.transpose(sa[...].astype(F32)).astype(BF16)
    near_mix[:, half:] = jnp.dot(ma[...], w[...], preferred_element_type=F32).astype(BF16)
    window_terms(near_dist, near_mix, mb, sb, w_t, ws_t, dist_sc, mix_sc, mom_sc, oh, oc, None)


def next_body(near_dist, near_mix, mb, sb, w_t, ws_t, ah, ac, oh, oc, dist_sc, mix_sc, mom_sc):
    window_terms(
        near_dist, near_mix, mb, sb, w_t, ws_t, dist_sc, mix_sc, mom_sc, oh, oc, (ah, ac)
    )


def call(body, operands, outs, cols, feats, **kw):
    vmem = pl.BlockSpec(memory_space=pltpu.VMEM)
    return pl.pallas_call(
        body,
        out_shape=outs,
        in_specs=[vmem] * len(operands),
        out_specs=[vmem] * len(outs),
        scratch_shapes=[
            pltpu.VMEM((64, cols), BF16),
            pltpu.VMEM((2 * feats, cols), BF16),
            pltpu.VMEM((32, cols), BF16),
        ],
        compiler_params=pltpu.CompilerParams(vmem_limit_bytes=48 << 20),
        **kw,
    )(*operands)


def local(inputs, weight_h, weight_s, cotangent, ranks, counts):
    block_total = lax.axis_size("blk")
    position = lax.axis_index("blk")
    my_half = lax.axis_index("feat")
    hits, width = cotangent.shape
    feats = 2 * width
    rows = hits // 2
    dims = weight_s.shape[1]
    blocks = jnp.arange(block_total, dtype=jnp.int32)
    spacing = (blocks - position) % block_total
    loop_gap = jnp.minimum(spacing, block_total - spacing)
    own_count = jnp.sum(jnp.where(blocks == position, counts, 0))
    window_count = jnp.sum(jnp.where(loop_gap <= WINDOW, counts, 0))
    live = (ranks < own_count).astype(F32)
    scale = 1.0 / jnp.sqrt(window_count.astype(F32))
    other_feat = lambda b, f: (b, 1 - f)

    masked = inputs * live.astype(BF16)[:, None]
    scaled_own = (cotangent.T.astype(F32) * (live * scale)[None, :]).astype(BF16)
    offsets = [1, -1, 2, -2][: 2 * WINDOW]
    masked_far = [moved(masked, lambda b, f, d=d: (b - d, f)) for d in offsets]
    scaled_other = moved(scaled_own, other_feat)
    w_own = weight_h
    w_other = moved(weight_h, other_feat)
    scaled = jnp.concatenate([scaled_own, scaled_other], 0)
    w = jnp.concatenate([w_own, w_other], 1)
    scaled_far = [moved(scaled, lambda b, f, d=d: (b - d, f)) for d in offsets]

    w_t = w.T
    ws_t = jnp.zeros((8, weight_s.shape[0]), BF16).at[:dims].set(weight_s.T)
    start = my_half * rows
    ma = lax.dynamic_slice_in_dim(masked, start, rows, 0)
    sa = lax.dynamic_slice_in_dim(scaled, start, rows, 1)
    sums = [
        jax.ShapeDtypeStruct((rows, feats), F32),
        jax.ShapeDtypeStruct((rows, 32), F32),
    ]
    near = [
        jax.ShapeDtypeStruct((rows, 64), BF16),
        jax.ShapeDtypeStruct((rows, 2 * feats), BF16),
    ]
    oh, oc, near_dist, near_mix = call(
        first_body, (ma, sa, masked, scaled, w, w_t, ws_t), sums + near, hits, feats
    )
    for mb, sb in zip(masked_far, scaled_far):
        oh, oc = call(
            next_body,
            (near_dist, near_mix, mb, sb, w_t, ws_t, oh, oc),
            sums,
            hits,
            feats,
            input_output_aliases={6: 0, 7: 1},
        )

    live_rows = lax.dynamic_slice_in_dim(live, start, rows, 0)
    hidden_grad = (oh * live_rows[:, None]).astype(BF16)
    coords = jnp.dot(ma, weight_s, preferred_element_type=F32)
    pulled = oc[:, :dims] + oc[:, 8 : 8 + dims] + oc[:, 16 : 16 + dims]
    coord_grad = 2.0 * (pulled - coords * oc[:, 4:5])
    part_h = lax.dot_general(
        hidden_grad, ma, (((0,), (0,)), ((), ())), preferred_element_type=F32
    )
    part_s = lax.dot_general(
        coord_grad, ma.astype(F32), (((0,), (0,)), ((), ())), precision=highest
    )
    total = jnp.concatenate([part_h[:width], part_s], 0) + moved(
        jnp.concatenate([part_h[width:], part_s], 0), other_feat
    )
    step = 1
    while step < block_total:
        total = total + moved(total, lambda b, f, s=step: (b ^ s, f))
        step *= 2
    grad_rows = lax.dot_general(hidden_grad, w, NT, preferred_element_type=F32) + jnp.dot(
        coord_grad, weight_s.astype(F32).T, precision=highest
    )
    grad_rows = grad_rows.astype(BF16)
    mine = lax.dynamic_slice_in_dim(grad_rows, my_half * width, width, 1)
    theirs = lax.dynamic_slice_in_dim(grad_rows, (1 - my_half) * width, width, 1)
    got = moved(theirs, other_feat)
    grad_inputs = jnp.where(
        my_half == 0, jnp.concatenate([mine, got], 0), jnp.concatenate([got, mine], 0)
    )
    return (grad_inputs, total[:width].T, total[width:].T)


def solution(mesh):
    placed = (P("blk", None), P(None, "feat"), P(), P("blk", "feat"), P("blk"), P())
    return jax.shard_map(
        local,
        mesh=mesh,
        in_specs=placed,
        out_specs=(P("blk", "feat"), P(None, "feat"), P()),
        check_vma=False,
    )
```

time: 529 us -> 97.1 us (0.18)
  the two profiles are of different devices: /device:TPU:8 before, /device:TPU:0 now
where the time goes in v1:
time: 97.1 us; the launch traced here: 96.8 us
  starting transfers between devices  29.9 us (31%)
  Pallas kernels  27.5 us (28%)
  waiting for transfers between devices  26.3 us (27%)
  other arithmetic  5.22 us (5%)
  local copies, waits for them, and re-layouts  3.91 us (4%)
  matrix products  2.36 us (2%)
  between operations  1.61 us (2%)
    ppermute x18, starting transfers between devices, moved(): return lax.ppermute(x, ('blk', 'feat'), route)  29.9 us
    pallas_call x5, Pallas kernels, call(): pl.pallas_call(body, out_shape=outs, in_specs=[vmem] * len(operands), out...  27.5 us
    ppermute x18, waiting for transfers between devices, moved(): return lax.ppermute(x, ('blk', 'feat'), route)  26.3 us
    unnamed x17, local copies, waits for them, and re-layouts  2.16 us
  transfers between devices with their start and end apart: 18, of which 11 were waited for; matrix products, arithmetic and copies ran while one was open for 3% of the time, Pallas kernels for 22%

profile of v1, /device:TPU:0, one launch (start us, length us, event | category | flops | bytes accessed | tf_op | source)
XLA Modules:
  0.0 96.8 jit_solution(15809248363820320571)
XLA Ops:
  0.7 1.4 %fusion.6 = (s32[]{:T(128)}, s32[]{:T(128)}) fusion(s32[64]{0:T(128)} %param.13, s32[]{:T(128)S(6)} %axis_index.25), kind=kLoop, calls=%fused_computation.34 | loop fusion | flops 1278 | bytes 268 | tf_op jit(solution)/shard_map/reduce_sum | solution.py:141
  2.7 0.7 fusion.8
  3.4 1.0 %fusion.1 = bf16[64,2048]{1,0:T(8,128)(2,1)S(1)} fusion(bf16[2048,64]{0,1:T(8,128)(2,1)} %param.11, f32[2048]{0:T(1024)S(1)} %broadcast_select_fusion), kind=kLoop, calls=%fused_computation.9 | loop fusion | flops 393216 | bytes 532480 | tf_op jit(solution)/shard_map/convert_element_type | solution.py:147
  4.4 0.0 copy-start.2
  4.4 3.4 %collective-permute-start = (bf16[64,2048]{1,0:T(8,128)(2,1)S(1)}, bf16[64,2048]{1,0:T(8,128)(2,1)S(1)}, u32[]{:S(2)}, u32[]{:S(2)}) collective-permute-start(bf16[64,2048]{1,0:T(8,128)(2,1)S(1)} %fusion.1), channel_id=1, source_target_pairs={{0,1},{1,0},{2,3},{3,2},{4,5},{5,4},{6,7},{7,6},{8,9},{9,8},{10,11... | collective-permute-start | bytes 786440 | tf_op jit(solution)/shard_map/ppermute | solution.py:28
  7.8 0.3 broadcast_multiply_fusion.mb
  8.1 5.6 %collective-permute-start.8 = (bf16[2048,128]{1,0:T(8,128)(2,1)S(1)}, bf16[2048,128]{1,0:T(8,128)(2,1)S(1)}, u32[]{:S(2)}, u32[]{:S(2)}) collective-permute-start(bf16[2048,128]{1,0:T(8,128)(2,1)S(1)} %broadcast_multiply_fusion.mb), channel_id=1, source_target_pairs={{0,126},{1,127},{2,0},{3,1},{4,2},{5,3},{6,4},{7,5},{8,6},{9,7},{1... | collective-permute-start | bytes 1572872 | tf_op jit(solution)/shard_map/ppermute | solution.py:28
  13.7 0.4 collective-permute-done
  14.1 0.7 copy-done.3
  14.8 5.9 %collective-permute-start.9 = (bf16[128,2048]{1,0:T(8,128)(2,1)S(1)}, bf16[128,2048]{1,0:T(8,128)(2,1)S(1)}, u32[]{:S(2)}, u32[]{:S(2)}) collective-permute-start(bf16[128,2048]{1,0:T(8,128)(2,1)S(1)} %pad_maximum_fusion.sb), channel_id=1, source_target_pairs={{0,126},{1,127},{2,0},{3,1},{4,2},{5,3},{6,4},{7,5},{8,6},{9,7},{1... | collective-permute-start | bytes 1572872 | tf_op jit(solution)/shard_map/ppermute | solution.py:28
  20.6 2.9 %collective-permute-start.1 = (bf16[128,64]{0,1:T(8,128)(2,1)S(1)}, bf16[128,64]{0,1:T(8,128)(2,1)S(1)}, u32[]{:S(2)}, u32[]{:S(2)}) collective-permute-start(bf16[128,64]{0,1:T(8,128)(2,1)S(1)} %copy-done.5), channel_id=1, source_target_pairs={{0,1},{1,0},{2,3},{3,2},{4,5},{5,4},{6,7},{7,6},{8,9},{9,8},{10,11... | collective-permute-start | bytes 49160 | tf_op jit(solution)/shard_map/ppermute | solution.py:28
  23.6 2.3 %collective-permute-done.1 = bf16[128,64]{0,1:T(8,128)(2,1)S(1)} collective-permute-done((bf16[128,64]{0,1:T(8,128)(2,1)S(1)}, bf16[128,64]{0,1:T(8,128)(2,1)S(1)}, u32[]{:S(2)}, u32[]{:S(2)}) %collective-permute-start.1) | collective-permute-done | bytes 16416 | tf_op jit(solution)/shard_map/ppermute | solution.py:28
  25.9 1.4 %collective-permute-start.4 = (bf16[2048,128]{1,0:T(8,128)(2,1)S(1)}, bf16[2048,128]{1,0:T(8,128)(2,1)S(1)}, u32[]{:S(2)}, u32[]{:S(2)}) collective-permute-start(bf16[2048,128]{1,0:T(8,128)(2,1)S(1)} %broadcast_multiply_fusion.mb), channel_id=1, source_target_pairs={{0,124},{1,125},{2,126},{3,127},{4,0},{5,1},{6,2},{7,3},{8,4},{9,5... | collective-permute-start | bytes 1572872 | tf_op jit(solution)/shard_map/ppermute | solution.py:28
  27.3 0.4 collective-permute-start.5
  27.7 1.6 %collective-permute-start.2 = (bf16[2048,128]{1,0:T(8,128)(2,1)S(1)}, bf16[2048,128]{1,0:T(8,128)(2,1)S(1)}, u32[]{:S(2)}, u32[]{:S(2)}) collective-permute-start(bf16[2048,128]{1,0:T(8,128)(2,1)S(1)} %broadcast_multiply_fusion.mb), channel_id=1, source_target_pairs={{0,4},{1,5},{2,6},{3,7},{4,8},{5,9},{6,10},{7,11},{8,12},{9,13},{1... | collective-permute-start | bytes 1572872 | tf_op jit(solution)/shard_map/ppermute | solution.py:28
  29.4 0.8 copy-done
  30.2 0.6 collective-permute-start.3
  30.8 0.7 copy-done.6
  31.5 0.1 copy.19.w
  31.6 1.0 %fusion.2.sa = bf16[128,1024]{1,0:T(8,128)(2,1)S(1)} fusion(s32[]{:T(128)S(6)} %select_n.35, bf16[64,2048]{1,0:T(8,128)(2,1)} %copy-done.2, bf16[64,2048]{1,0:T(8,128)(2,1)} %copy-done.3), kind=kLoop, calls=%fused_computation.10 | loop fusion | flops 524288 | bytes 786436 | tf_op jit(solution)/shard_map/concatenate | solution.py:153
  32.6 4.9 %shard_map.85 = (f32[1024,128]{1,0:T(8,128)S(1)}, f32[1024,32]{1,0:T(8,128)S(1)}, bf16[1024,64]{1,0:T(8,128)(2,1)S(1)}, bf16[1024,256]{1,0:T(8,128)(2,1)S(1)}) custom-call(bf16[1024,128]{1,0:T(8,128)(2,1)S(1)} %constant_dynamic-slice_fusion.2.ma, bf16[128,1024]{1,0:T(8,128)(2,1)S(1)} %fusion.2.sa, bf16[2048,128]{1,0:T(8,128)(2,1)S(1)} %broadcast_multiply_fusion.mb, ...), custom_call_target="tpu_custom_call" | custom-call | tf_op jit(solution)/shard_map/pallas_call | solution.py:114
  37.5 4.8 %shard_map.86 = (f32[1024,128]{1,0:T(8,128)S(1)}, f32[1024,32]{1,0:T(8,128)S(1)}) custom-call(bf16[1024,64]{1,0:T(8,128)(2,1)S(1)} %get-tuple-element.27.near_dist, bf16[1024,256]{1,0:T(8,128)(2,1)S(1)} %get-tuple-element.28.near_mix, bf16[2048,128]{1,0:T(8,128)(2,1)S(1)} %collective-permute-done.8.mb, ...), custom_call_target="tpu_custom_call", output_to_operand_aliasing={{0}: (6, {}), {1}: (7, {})} | custom-call | tf_op jit(solution)/shard_map/pallas_call | solution.py:114
  42.4 6.1 %shard_map.87 = (f32[1024,128]{1,0:T(8,128)S(1)}, f32[1024,32]{1,0:T(8,128)S(1)}) custom-call(bf16[1024,64]{1,0:T(8,128)(2,1)S(1)} %get-tuple-element.27.near_dist, bf16[1024,256]{1,0:T(8,128)(2,1)S(1)} %get-tuple-element.28.near_mix, bf16[2048,128]{1,0:T(8,128)(2,1)S(1)} %collective-permute-done.6.mb, ...), custom_call_target="tpu_custom_call", output_to_operand_aliasing={{0}: (6, {}), {1}: (7, {})} | custom-call | tf_op jit(solution)/shard_map/pallas_call | solution.py:114
  48.5 0.7 collective-permute-done.5.sb
  49.2 5.8 %shard_map.88 = (f32[1024,128]{1,0:T(8,128)S(1)}, f32[1024,32]{1,0:T(8,128)S(1)}) custom-call(bf16[1024,64]{1,0:T(8,128)(2,1)S(1)} %get-tuple-element.27.near_dist, bf16[1024,256]{1,0:T(8,128)(2,1)S(1)} %get-tuple-element.28.near_mix, bf16[2048,128]{1,0:T(8,128)(2,1)S(1)} %collective-permute-done.4.mb, ...), custom_call_target="tpu_custom_call", output_to_operand_aliasing={{0}: (6, {}), {1}: (7, {})} | custom-call | tf_op jit(solution)/shard_map/pallas_call | solution.py:114
  55.1 3.1 %collective-permute-done.3.sb = bf16[128,2048]{1,0:T(8,128)(2,1)} collective-permute-done((bf16[128,2048]{1,0:T(8,128)(2,1)S(1)}, bf16[128,2048]{1,0:T(8,128)(2,1)}, u32[]{:S(2)}, u32[]{:S(2)}) %collective-permute-start.3) | collective-permute-done | bytes 524320 | tf_op jit(solution)/shard_map/ppermute | solution.py:28
  58.2 5.8 %shard_map.89 = (f32[1024,128]{1,0:T(8,128)S(1)}, f32[1024,32]{1,0:T(8,128)S(1)}) custom-call(bf16[1024,64]{1,0:T(8,128)(2,1)S(1)} %get-tuple-element.27.near_dist, bf16[1024,256]{1,0:T(8,128)(2,1)S(1)} %get-tuple-element.28.near_mix, bf16[2048,128]{1,0:T(8,128)(2,1)S(1)} %collective-permute-done.2.mb, ...), custom_call_target="tpu_custom_call", output_to_operand_aliasing={{0}: (6, {}), {1}: (7, {})} | custom-call | tf_op jit(solution)/shard_map/pallas_call | solution.py:114
  64.0 0.4 slice_reduce_fusion
  64.4 0.5 subtract_multiply_fusion
  64.9 0.5 fusion.11
  65.4 0.5 fusion.7
  65.9 1.7 %collective-permute-start.11 = (f32[68,128]{1,0:T(8,128)S(1)}, f32[68,128]{1,0:T(8,128)S(1)}, u32[]{:S(2)}, u32[]{:S(2)}) collective-permute-start(f32[68,128]{1,0:T(8,128)S(1)} %pad_maximum_fusion.1), channel_id=1, source_target_pairs={{0,1},{1,0},{2,3},{3,2},{4,5},{5,4},{6,7},{7,6},{8,9},{9,8},{10,11... | collective-permute-start | bytes 104456 | tf_op jit(solution)/shard_map/ppermute | solution.py:28
  67.6 0.4 fusion.10
  68.0 3.5 %collective-permute-done.11 = f32[68,128]{1,0:T(8,128)S(1)} collective-permute-done((f32[68,128]{1,0:T(8,128)S(1)}, f32[68,128]{1,0:T(8,128)S(1)}, u32[]{:S(2)}, u32[]{:S(2)}) %collective-permute-start.11) | collective-permute-done | bytes 34848 | tf_op jit(solution)/shard_map/ppermute | solution.py:28
  71.5 0.4 fusion
  71.9 0.8 collective-permute-done.12
  72.8 1.6 %collective-permute-start.10 = (bf16[1024,64]{0,1:T(8,128)(2,1)S(1)}, bf16[1024,64]{0,1:T(8,128)(2,1)S(1)}, u32[]{:S(2)}, u32[]{:S(2)}) collective-permute-start(bf16[1024,64]{0,1:T(8,128)(2,1)S(1)} %get-tuple-element.44), channel_id=1, source_target_pairs={{0,1},{1,0},{2,3},{3,2},{4,5},{5,4},{6,7},{7,6},{8,9},{9,8},{10,11... | collective-permute-start | bytes 393224 | tf_op jit(solution)/shard_map/ppermute | solution.py:28
  74.4 2.3 %collective-permute-done.13 = f32[68,128]{1,0:T(8,128)S(1)} collective-permute-done((f32[68,128]{1,0:T(8,128)S(1)}, f32[68,128]{1,0:T(8,128)S(1)}, u32[]{:S(2)}, u32[]{:S(2)}) %collective-permute-start.13) | collective-permute-done | bytes 34848 | tf_op jit(solution)/shard_map/ppermute | solution.py:28
  76.7 3.0 %collective-permute-start.14 = (f32[68,128]{1,0:T(8,128)S(1)}, f32[68,128]{1,0:T(8,128)S(1)}, u32[]{:S(2)}, u32[]{:S(2)}) collective-permute-start(f32[68,128]{1,0:T(8,128)S(1)} %add.60), channel_id=1, source_target_pairs={{0,8},{1,9},{2,10},{3,11},{4,12},{5,13},{6,14},{7,15},{8,0},{9,1},... | collective-permute-start | bytes 104456 | tf_op jit(solution)/shard_map/ppermute | solution.py:28
  79.7 2.5 %collective-permute-done.14 = f32[68,128]{1,0:T(8,128)S(1)} collective-permute-done((f32[68,128]{1,0:T(8,128)S(1)}, f32[68,128]{1,0:T(8,128)S(1)}, u32[]{:S(2)}, u32[]{:S(2)}) %collective-permute-start.14) | collective-permute-done | bytes 34848 | tf_op jit(solution)/shard_map/ppermute | solution.py:28
  82.2 3.9 %collective-permute-done.15 = f32[68,128]{1,0:T(8,128)S(1)} collective-permute-done((f32[68,128]{1,0:T(8,128)S(1)}, f32[68,128]{1,0:T(8,128)S(1)}, u32[]{:S(2)}, u32[]{:S(2)}) %collective-permute-start.15) | collective-permute-done | bytes 34848 | tf_op jit(solution)/shard_map/ppermute | solution.py:28
  86.1 1.4 %collective-permute-start.16 = (f32[68,128]{1,0:T(8,128)S(1)}, f32[68,128]{1,0:T(8,128)S(1)}, u32[]{:S(2)}, u32[]{:S(2)}) collective-permute-start(f32[68,128]{1,0:T(8,128)S(1)} %add.62), channel_id=1, source_target_pairs={{0,32},{1,33},{2,34},{3,35},{4,36},{5,37},{6,38},{7,39},{8,40},{9,... | collective-permute-start | bytes 104456 | tf_op jit(solution)/shard_map/ppermute | solution.py:28
  87.5 4.0 %collective-permute-done.16 = f32[68,128]{1,0:T(8,128)S(1)} collective-permute-done((f32[68,128]{1,0:T(8,128)S(1)}, f32[68,128]{1,0:T(8,128)S(1)}, u32[]{:S(2)}, u32[]{:S(2)}) %collective-permute-start.16) | collective-permute-done | bytes 34848 | tf_op jit(solution)/shard_map/ppermute | solution.py:28
  91.6 0.4 collective-permute-start.17
  92.0 0.8 maximum_select_fusion
  92.8 2.8 %collective-permute-done.17 = f32[68,128]{1,0:T(8,128)S(1)} collective-permute-done((f32[68,128]{1,0:T(8,128)S(1)}, f32[68,128]{1,0:T(8,128)S(1)}, u32[]{:S(2)}, u32[]{:S(2)}) %collective-permute-start.17) | collective-permute-done | bytes 34848 | tf_op jit(solution)/shard_map/ppermute | solution.py:28
  95.6 0.6 slice_bitcast_fusion
  96.2 0.6 slice_bitcast_fusion.1
  (42 shorter events, 0.2 us)
Async XLA Ops:
  0.6 2.1 %copy-start.7 = (s32[2048]{0:T(1024)S(1)}, s32[2048]{0:T(1024)}, u32[]{:S(2)}) copy-start(s32[2048]{0:T(1024)} %param.12) | copy-start | bytes 24580
  0.6 7.1 %copy-start.4 = (bf16[2048,128]{1,0:T(8,128)(2,1)S(1)}, bf16[2048,128]{1,0:T(8,128)(2,1)}, u32[]{:S(2)}) copy-start(bf16[2048,128]{1,0:T(8,128)(2,1)} %param.8) | copy-start | bytes 1572868
  4.4 9.7 %copy-start.2 = (bf16[64,2048]{1,0:T(8,128)(2,1)}, bf16[64,2048]{1,0:T(8,128)(2,1)S(1)}, u32[]{:S(2)}) copy-start(bf16[64,2048]{1,0:T(8,128)(2,1)S(1)} %fusion.1) | copy-start | bytes 786436
  4.4 9.7 %collective-permute-start = (bf16[64,2048]{1,0:T(8,128)(2,1)S(1)}, bf16[64,2048]{1,0:T(8,128)(2,1)S(1)}, u32[]{:S(2)}, u32[]{:S(2)}) collective-permute-start(bf16[64,2048]{1,0:T(8,128)(2,1)S(1)} %fusion.1), channel_id=1, source_target_pairs={{0,1},{1,0},{2,3},{3,2},{4,5},{5,4},{6,7},{7,6},{8,9},{9,8},{10,11... | collective-permute-start | bytes 786440 | tf_op jit(solution)/shard_map/ppermute | solution.py:28
  8.1 12.5 %copy-start.5 = (bf16[128,64]{0,1:T(8,128)(2,1)S(1)}, bf16[128,64]{0,1:T(8,128)(2,1)}, u32[]{:S(2)}) copy-start(bf16[128,64]{0,1:T(8,128)(2,1)} %param.9) | copy-start | bytes 49156
  8.1 19.2 %collective-permute-start.8 = (bf16[2048,128]{1,0:T(8,128)(2,1)S(1)}, bf16[2048,128]{1,0:T(8,128)(2,1)S(1)}, u32[]{:S(2)}, u32[]{:S(2)}) collective-permute-start(bf16[2048,128]{1,0:T(8,128)(2,1)S(1)} %broadcast_multiply_fusion.mb), channel_id=1, source_target_pairs={{0,126},{1,127},{2,0},{3,1},{4,2},{5,3},{6,4},{7,5},{8,6},{9,7},{1... | collective-permute-start | bytes 1572872 | tf_op jit(solution)/shard_map/ppermute | solution.py:28
  13.7 14.0 %collective-permute-start.6 = (bf16[2048,128]{1,0:T(8,128)(2,1)S(1)}, bf16[2048,128]{1,0:T(8,128)(2,1)S(1)}, u32[]{:S(2)}, u32[]{:S(2)}) collective-permute-start(bf16[2048,128]{1,0:T(8,128)(2,1)S(1)} %broadcast_multiply_fusion.mb), channel_id=1, source_target_pairs={{0,2},{1,3},{2,4},{3,5},{4,6},{5,7},{6,8},{7,9},{8,10},{9,11},{10,... | collective-permute-start | bytes 1572872 | tf_op jit(solution)/shard_map/ppermute | solution.py:28
  14.1 0.7 copy-start.3
  14.8 14.6 %collective-permute-start.9 = (bf16[128,2048]{1,0:T(8,128)(2,1)S(1)}, bf16[128,2048]{1,0:T(8,128)(2,1)S(1)}, u32[]{:S(2)}, u32[]{:S(2)}) collective-permute-start(bf16[128,2048]{1,0:T(8,128)(2,1)S(1)} %pad_maximum_fusion.sb), channel_id=1, source_target_pairs={{0,126},{1,127},{2,0},{3,1},{4,2},{5,3},{6,4},{7,5},{8,6},{9,7},{1... | collective-permute-start | bytes 1572872 | tf_op jit(solution)/shard_map/ppermute | solution.py:28
  20.6 5.2 %collective-permute-start.1 = (bf16[128,64]{0,1:T(8,128)(2,1)S(1)}, bf16[128,64]{0,1:T(8,128)(2,1)S(1)}, u32[]{:S(2)}, u32[]{:S(2)}) collective-permute-start(bf16[128,64]{0,1:T(8,128)(2,1)S(1)} %copy-done.5), channel_id=1, source_target_pairs={{0,1},{1,0},{2,3},{3,2},{4,5},{5,4},{6,7},{7,6},{8,9},{9,8},{10,11... | collective-permute-start | bytes 49160 | tf_op jit(solution)/shard_map/ppermute | solution.py:28
  23.6 18.8 %collective-permute-start.7 = (bf16[128,2048]{1,0:T(8,128)(2,1)S(1)}, bf16[128,2048]{1,0:T(8,128)(2,1)}, u32[]{:S(2)}, u32[]{:S(2)}) collective-permute-start(bf16[128,2048]{1,0:T(8,128)(2,1)S(1)} %pad_maximum_fusion.sb), channel_id=1, source_target_pairs={{0,2},{1,3},{2,4},{3,5},{4,6},{5,7},{6,8},{7,9},{8,10},{9,11},{10,... | collective-permute-start | bytes 1572872 | tf_op jit(solution)/shard_map/ppermute | solution.py:28
  25.9 22.6 %collective-permute-start.4 = (bf16[2048,128]{1,0:T(8,128)(2,1)S(1)}, bf16[2048,128]{1,0:T(8,128)(2,1)S(1)}, u32[]{:S(2)}, u32[]{:S(2)}) collective-permute-start(bf16[2048,128]{1,0:T(8,128)(2,1)S(1)} %broadcast_multiply_fusion.mb), channel_id=1, source_target_pairs={{0,124},{1,125},{2,126},{3,127},{4,0},{5,1},{6,2},{7,3},{8,4},{9,5... | collective-permute-start | bytes 1572872 | tf_op jit(solution)/shard_map/ppermute | solution.py:28
  27.3 21.9 %collective-permute-start.5 = (bf16[128,2048]{1,0:T(8,128)(2,1)S(1)}, bf16[128,2048]{1,0:T(8,128)(2,1)}, u32[]{:S(2)}, u32[]{:S(2)}) collective-permute-start(bf16[128,2048]{1,0:T(8,128)(2,1)S(1)} %pad_maximum_fusion.sb), channel_id=1, source_target_pairs={{0,124},{1,125},{2,126},{3,127},{4,0},{5,1},{6,2},{7,3},{8,4},{9,5... | collective-permute-start | bytes 1572872 | tf_op jit(solution)/shard_map/ppermute | solution.py:28
  27.7 27.3 %collective-permute-start.2 = (bf16[2048,128]{1,0:T(8,128)(2,1)S(1)}, bf16[2048,128]{1,0:T(8,128)(2,1)S(1)}, u32[]{:S(2)}, u32[]{:S(2)}) collective-permute-start(bf16[2048,128]{1,0:T(8,128)(2,1)S(1)} %broadcast_multiply_fusion.mb), channel_id=1, source_target_pairs={{0,4},{1,5},{2,6},{3,7},{4,8},{5,9},{6,10},{7,11},{8,12},{9,13},{1... | collective-permute-start | bytes 1572872 | tf_op jit(solution)/shard_map/ppermute | solution.py:28
  29.4 0.8 copy-start
  30.2 28.0 %collective-permute-start.3 = (bf16[128,2048]{1,0:T(8,128)(2,1)S(1)}, bf16[128,2048]{1,0:T(8,128)(2,1)}, u32[]{:S(2)}, u32[]{:S(2)}) collective-permute-start(bf16[128,2048]{1,0:T(8,128)(2,1)S(1)} %pad_maximum_fusion.sb), channel_id=1, source_target_pairs={{0,4},{1,5},{2,6},{3,7},{4,8},{5,9},{6,10},{7,11},{8,12},{9,13},{1... | collective-permute-start | bytes 1572872 | tf_op jit(solution)/shard_map/ppermute | solution.py:28
  30.8 0.7 copy-start.6
  32.6 4.9 %copy-start.1 = (bf16[128,2048]{1,0:T(8,128)(2,1)S(1)}, bf16[128,2048]{1,0:T(8,128)(2,1)}, u32[]{:S(2)}) copy-start(bf16[128,2048]{1,0:T(8,128)(2,1)} %copy-done) | copy-start | bytes 1572868
  65.9 5.6 %collective-permute-start.11 = (f32[68,128]{1,0:T(8,128)S(1)}, f32[68,128]{1,0:T(8,128)S(1)}, u32[]{:S(2)}, u32[]{:S(2)}) collective-permute-start(f32[68,128]{1,0:T(8,128)S(1)} %pad_maximum_fusion.1), channel_id=1, source_target_pairs={{0,1},{1,0},{2,3},{3,2},{4,5},{5,4},{6,7},{7,6},{8,9},{9,8},{10,11... | collective-permute-start | bytes 104456 | tf_op jit(solution)/shard_map/ppermute | solution.py:28
  71.5 1.2 %collective-permute-start.12 = (f32[68,128]{1,0:T(8,128)S(1)}, f32[68,128]{1,0:T(8,128)S(1)}, u32[]{:S(2)}, u32[]{:S(2)}) collective-permute-start(f32[68,128]{1,0:T(8,128)S(1)} %fusion.3), channel_id=1, source_target_pairs={{0,2},{1,3},{2,0},{3,1},{4,6},{5,7},{6,4},{7,5},{8,10},{9,11},{10,... | collective-permute-start | bytes 104456 | tf_op jit(solution)/shard_map/ppermute | solution.py:28
  72.7 4.0 %collective-permute-start.13 = (f32[68,128]{1,0:T(8,128)S(1)}, f32[68,128]{1,0:T(8,128)S(1)}, u32[]{:S(2)}, u32[]{:S(2)}) collective-permute-start(f32[68,128]{1,0:T(8,128)S(1)} %add.59), channel_id=1, source_target_pairs={{0,4},{1,5},{2,6},{3,7},{4,0},{5,1},{6,2},{7,3},{8,12},{9,13},{10,... | collective-permute-start | bytes 104456 | tf_op jit(solution)/shard_map/ppermute | solution.py:28
  72.8 19.3 %collective-permute-start.10 = (bf16[1024,64]{0,1:T(8,128)(2,1)S(1)}, bf16[1024,64]{0,1:T(8,128)(2,1)S(1)}, u32[]{:S(2)}, u32[]{:S(2)}) collective-permute-start(bf16[1024,64]{0,1:T(8,128)(2,1)S(1)} %get-tuple-element.44), channel_id=1, source_target_pairs={{0,1},{1,0},{2,3},{3,2},{4,5},{5,4},{6,7},{7,6},{8,9},{9,8},{10,11... | collective-permute-start | bytes 393224 | tf_op jit(solution)/shard_map/ppermute | solution.py:28
  76.7 5.5 %collective-permute-start.14 = (f32[68,128]{1,0:T(8,128)S(1)}, f32[68,128]{1,0:T(8,128)S(1)}, u32[]{:S(2)}, u32[]{:S(2)}) collective-permute-start(f32[68,128]{1,0:T(8,128)S(1)} %add.60), channel_id=1, source_target_pairs={{0,8},{1,9},{2,10},{3,11},{4,12},{5,13},{6,14},{7,15},{8,0},{9,1},... | collective-permute-start | bytes 104456 | tf_op jit(solution)/shard_map/ppermute | solution.py:28
  82.2 4.0 %collective-permute-start.15 = (f32[68,128]{1,0:T(8,128)S(1)}, f32[68,128]{1,0:T(8,128)S(1)}, u32[]{:S(2)}, u32[]{:S(2)}) collective-permute-start(f32[68,128]{1,0:T(8,128)S(1)} %add.61), channel_id=1, source_target_pairs={{0,16},{1,17},{2,18},{3,19},{4,20},{5,21},{6,22},{7,23},{8,24},{9,... | collective-permute-start | bytes 104456 | tf_op jit(solution)/shard_map/ppermute | solution.py:28
  86.1 5.5 %collective-permute-start.16 = (f32[68,128]{1,0:T(8,128)S(1)}, f32[68,128]{1,0:T(8,128)S(1)}, u32[]{:S(2)}, u32[]{:S(2)}) collective-permute-start(f32[68,128]{1,0:T(8,128)S(1)} %add.62), channel_id=1, source_target_pairs={{0,32},{1,33},{2,34},{3,35},{4,36},{5,37},{6,38},{7,39},{8,40},{9,... | collective-permute-start | bytes 104456 | tf_op jit(solution)/shard_map/ppermute | solution.py:28
  91.6 4.0 %collective-permute-start.17 = (f32[68,128]{1,0:T(8,128)S(1)}, f32[68,128]{1,0:T(8,128)S(1)}, u32[]{:S(2)}, u32[]{:S(2)}) collective-permute-start(f32[68,128]{1,0:T(8,128)S(1)} %add.63), channel_id=1, source_target_pairs={{0,64},{1,65},{2,66},{3,67},{4,68},{5,69},{6,70},{7,71},{8,72},{9,... | collective-permute-start | bytes 104456 | tf_op jit(solution)/shard_map/ppermute | solution.py:28

commit v2 on v1

--- a/solution.py
+++ b/solution.py
@@ -13,7 +13,6 @@
 NT = (((1,), (1,)), ((), ()))
 F32 = jnp.float32
 BF16 = jnp.bfloat16
-highest = lax.Precision.HIGHEST
 ROW_TILE = 512
 COL_TILE = 1024
 
@@ -109,7 +108,40 @@
     )
 
 
-def call(body, operands, outs, cols, feats, **kw):
+def last_body(
+    near_dist, near_mix, mb, sb, w_t, ws_t, ah, ac, ma, live, w_turned, ws_turned,
+    own, other, mine, theirs, dist_sc, mix_sc, mom_sc, oh, oc,
+):
+    window_terms(
+        near_dist, near_mix, mb, sb, w_t, ws_t, dist_sc, mix_sc, mom_sc, oh, oc, (ah, ac)
+    )
+    width = mine.shape[0]
+    hidden_grad = (oh[...]).astype(BF16)
+    sums = jnp.transpose(oc[...])
+    coords = lax.dot_general(ws_t[...], ma[...], NT, preferred_element_type=F32)
+    pulled = sums[0:8] + sums[8:16] + sums[16:24]
+    coord_grad = 2.0 * (pulled - coords * sums[4:5])
+    row = lax.broadcasted_iota(jnp.int32, coord_grad.shape, 0)
+    coord_grad = jnp.where(row < 4, coord_grad, 0.0)
+    g1, g2, g3 = split3(coord_grad)
+    parts = jnp.concatenate([g1, g2, g3, jnp.zeros_like(g1)], 0).astype(BF16)
+    part_h = lax.dot_general(
+        hidden_grad, ma[...], (((0,), (0,)), ((), ())), preferred_element_type=F32
+    )
+    triple = jnp.dot(parts, ma[...], preferred_element_type=F32)
+    part_s = triple[0:8] + triple[8:16] + triple[16:24]
+    own[:width, :] = part_h[:width]
+    own[width:, :] = part_s
+    other[:width, :] = part_h[width:]
+    other[width:, :] = part_s
+    grad = lax.dot_general(w_turned[...], hidden_grad, NT, preferred_element_type=F32)
+    grad = grad + jnp.dot(ws_turned[...], parts, preferred_element_type=F32)
+    grad = (grad * live[...]).astype(BF16)
+    mine[...] = grad[:width]
+    theirs[...] = grad[width:]
+
+
+def call(body, operands, outs, cols, feats, extra=(), **kw):
     vmem = pl.BlockSpec(memory_space=pltpu.VMEM)
     return pl.pallas_call(
         body,
@@ -120,6 +152,7 @@
             pltpu.VMEM((64, cols), BF16),
             pltpu.VMEM((2 * feats, cols), BF16),
             pltpu.VMEM((32, cols), BF16),
+            *extra,
         ],
         compiler_params=pltpu.CompilerParams(vmem_limit_bytes=48 << 20),
         **kw,
@@ -143,22 +176,25 @@
     scale = 1.0 / jnp.sqrt(window_count.astype(F32))
     other_feat = lambda b, f: (b, 1 - f)
 
+    packed = jnp.concatenate([cotangent.T, weight_h.T], 1)
+    arrived = moved(packed, other_feat)
     masked = inputs * live.astype(BF16)[:, None]
-    scaled_own = (cotangent.T.astype(F32) * (live * scale)[None, :]).astype(BF16)
     offsets = [1, -1, 2, -2][: 2 * WINDOW]
     masked_far = [moved(masked, lambda b, f, d=d: (b - d, f)) for d in offsets]
-    scaled_other = moved(scaled_own, other_feat)
-    w_own = weight_h
-    w_other = moved(weight_h, other_feat)
-    scaled = jnp.concatenate([scaled_own, scaled_other], 0)
-    w = jnp.concatenate([w_own, w_other], 1)
-    scaled_far = [moved(scaled, lambda b, f, d=d: (b - d, f)) for d in offsets]
-
-    w_t = w.T
+    both = jnp.concatenate([packed, arrived], 0)
+    scaled = (both[:, :hits].astype(F32) * (live * scale)[None, :]).astype(BF16)
+    w_t = both[:, hits:]
+    w = w_t.T
     ws_t = jnp.zeros((8, weight_s.shape[0]), BF16).at[:dims].set(weight_s.T)
+    turn = my_half * width
+    w_turned = jnp.roll(w, -turn, 0)
+    ws_turned = jnp.roll(
+        jnp.concatenate([ws_t, ws_t, ws_t, jnp.zeros_like(ws_t)], 0).T, -turn, 0
+    )
     start = my_half * rows
     ma = lax.dynamic_slice_in_dim(masked, start, rows, 0)
     sa = lax.dynamic_slice_in_dim(scaled, start, rows, 1)
+    live_rows = lax.dynamic_slice_in_dim(live, start, rows, 0)[None, :]
     sums = [
         jax.ShapeDtypeStruct((rows, feats), F32),
         jax.ShapeDtypeStruct((rows, 32), F32),
@@ -167,10 +203,13 @@
         jax.ShapeDtypeStruct((rows, 64), BF16),
         jax.ShapeDtypeStruct((rows, 2 * feats), BF16),
     ]
+    scaled_far = [moved(scaled, lambda b, f, d=d: (b - d, f)) for d in offsets[:2]]
     oh, oc, near_dist, near_mix = call(
         first_body, (ma, sa, masked, scaled, w, w_t, ws_t), sums + near, hits, feats
     )
-    for mb, sb in zip(masked_far, scaled_far):
+    late, oh, oc = lax.optimization_barrier((scaled, oh, oc))
+    scaled_far += [moved(late, lambda b, f, d=d: (b - d, f)) for d in offsets[2:]]
+    for mb, sb in list(zip(masked_far, scaled_far))[:-1]:
         oh, oc = call(
             next_body,
             (near_dist, near_mix, mb, sb, w_t, ws_t, oh, oc),
@@ -179,36 +218,26 @@
             feats,
             input_output_aliases={6: 0, 7: 1},
         )
-
-    live_rows = lax.dynamic_slice_in_dim(live, start, rows, 0)
-    hidden_grad = (oh * live_rows[:, None]).astype(BF16)
-    coords = jnp.dot(ma, weight_s, preferred_element_type=F32)
-    pulled = oc[:, :dims] + oc[:, 8 : 8 + dims] + oc[:, 16 : 16 + dims]
-    coord_grad = 2.0 * (pulled - coords * oc[:, 4:5])
-    part_h = lax.dot_general(
-        hidden_grad, ma, (((0,), (0,)), ((), ())), preferred_element_type=F32
-    )
-    part_s = lax.dot_general(
-        coord_grad, ma.astype(F32), (((0,), (0,)), ((), ())), precision=highest
-    )
-    total = jnp.concatenate([part_h[:width], part_s], 0) + moved(
-        jnp.concatenate([part_h[width:], part_s], 0), other_feat
-    )
+    own, other, mine, theirs = call(
+        last_body,
+        (near_dist, near_mix, masked_far[-1], scaled_far[-1], w_t, ws_t, oh, oc)
+        + (ma, live_rows, w_turned, ws_turned),
+        [jax.ShapeDtypeStruct((width + 8, inputs.shape[1]), F32)] * 2
+        + [jax.ShapeDtypeStruct((width, rows), BF16)] * 2,
+        hits,
+        feats,
+        [pltpu.VMEM((rows, feats), F32), pltpu.VMEM((rows, 32), F32)],
+    )
+    total = own + moved(other, other_feat)
     step = 1
     while step < block_total:
         total = total + moved(total, lambda b, f, s=step: (b ^ s, f))
         step *= 2
-    grad_rows = lax.dot_general(hidden_grad, w, NT, preferred_element_type=F32) + jnp.dot(
-        coord_grad, weight_s.astype(F32).T, precision=highest
-    )
-    grad_rows = grad_rows.astype(BF16)
-    mine = lax.dynamic_slice_in_dim(grad_rows, my_half * width, width, 1)
-    theirs = lax.dynamic_slice_in_dim(grad_rows, (1 - my_half) * width, width, 1)
     got = moved(theirs, other_feat)
     grad_inputs = jnp.where(
-        my_half == 0, jnp.concatenate([mine, got], 0), jnp.concatenate([got, mine], 0)
-    )
-    return (grad_inputs, total[:width].T, total[width:].T)
+        my_half == 0, jnp.concatenate([mine, got], 1), jnp.concatenate([got, mine], 1)
+    )
+    return (grad_inputs.T, total[:width].T, total[width : width + dims].T)
 
 
 def solution(mesh):

time: 97.1 us -> 110 us (1.13)
  local copies, waits for them, and re-layouts: 3.91 us -> 14.3 us
  waiting for transfers between devices: 26.3 us -> 29.5 us
  matrix products: 2.36 us -> 0 us
  Pallas kernels: 27.5 us -> 29.2 us
    ppermute x0 -> x5, local copies, waits for them, and re-layouts: none -> 7.75 us  [moved(): return lax.ppermute(x, ('blk', 'feat'), route)]
    ppermute x18 -> x17, waiting for transfers between devices: 26.3 us -> 29.5 us  [moved(): return lax.ppermute(x, ('blk', 'feat'), route)]
    dot_general x5 -> x0, matrix products: 2.36 us -> none  [the longest x1 0.54 us: local(): lax.dot_general(coord_grad, ma.astype(F32), (((0,), (0,)), ((), ())), pre...]
    pallas_call x5, Pallas kernels: 27.5 us -> 29.2 us  [call(): pl.pallas_call(body, out_shape=outs, in_specs=[vmem] * len(operands), out...]
    convert_element_type x0 -> x1, local copies, waits for them, and re-layouts: none -> 1.25 us  [local(): scaled = (both[:, :hits].astype(F32) * (live * scale)[None, :]).astype(BF16)]
    ppermute x18 -> x17, starting transfers between devices: 29.9 us -> 30.4 us  [moved(): return lax.ppermute(x, ('blk', 'feat'), route)]
    unnamed x17 -> x19, local copies, waits for them, and re-layouts: 2.16 us -> 2.56 us
  transfers between devices with their start and end apart: 18 -> 17, of which waited for: 11 -> 10; matrix products, arithmetic and copies ran while one was open for 3% -> 10% of each run, Pallas kernels for 22% -> 21%
where the time goes in v2:
time: 110 us
  starting transfers between devices  30.4 us (28%)
  waiting for transfers between devices  29.5 us (27%)
  Pallas kernels  29.2 us (27%)
  local copies, waits for them, and re-layouts  14.3 us (13%)
  other arithmetic  4.41 us (4%)
  between operations  1.63 us (1%)
    ppermute x17, starting transfers between devices, moved(): return lax.ppermute(x, ('blk', 'feat'), route)  30.4 us
    ppermute x17, waiting for transfers between devices, moved(): return lax.ppermute(x, ('blk', 'feat'), route)  29.5 us
    pallas_call x5, Pallas kernels, call(): pl.pallas_call(body, out_shape=outs, in_specs=[vmem] * len(operands), out...  29.2 us
    ppermute x5, local copies, waits for them, and re-layouts, moved(): return lax.ppermute(x, ('blk', 'feat'), route)  7.75 us
    unnamed x19, local copies, waits for them, and re-layouts  2.56 us
  transfers between devices with their start and end apart: 17, of which 10 were waited for; matrix products, arithmetic and copies ran while one was open for 10% of the time, Pallas kernels for 21%

profile of v2, /device:TPU:0, one launch (start us, length us, event | category | flops | bytes accessed | tf_op | source)
XLA Modules:
  0.0 109.5 jit_solution(4675769565076939435)
XLA Ops:
  0.6 1.2 %copy.34 = bf16[2048,64]{1,0:T(8,128)(2,1)S(1)} copy(bf16[2048,64]{0,1:T(8,128)(2,1)} %param.11) | data formatting | bytes 524288 | tf_op args[3]
  1.9 0.1 copy.35
  2.0 0.1 pad_maximum_fusion
  2.2 0.3 copy.36
  2.4 3.4 %collective-permute-start = (bf16[64,2176]{1,0:T(8,128)(2,1)S(1)}, bf16[64,2176]{1,0:T(8,128)(2,1)S(1)}, u32[]{:S(2)}, u32[]{:S(2)}) collective-permute-start(bf16[64,2176]{1,0:T(8,128)(2,1)S(1)} %copy.36), channel_id=1, source_target_pairs={{0,1},{1,0},{2,3},{3,2},{4,5},{5,4},{6,7},{7,6},{8,9},{9,8},{10,11... | collective-permute-start | bytes 835592 | tf_op jit(solution)/shard_map/ppermute | solution.py:27
  5.8 0.6 fusion.5
  6.4 0.6 fusion.6
  7.1 0.3 broadcast_multiply_fusion.mb
  8.2 4.2 %collective-permute-done = bf16[64,2176]{1,0:T(8,128)(2,1)S(1)} collective-permute-done((bf16[64,2176]{1,0:T(8,128)(2,1)S(1)}, bf16[64,2176]{1,0:T(8,128)(2,1)S(1)}, u32[]{:S(2)}, u32[]{:S(2)}) %collective-permute-start) | collective-permute-done | bytes 278560 | tf_op jit(solution)/shard_map/ppermute | solution.py:27
  12.5 0.3 copy.37
  12.8 0.3 pad_maximum_fusion.1
  13.1 1.1 %multiply_convert_fusion = bf16[128,2048]{0,1:T(8,128)(2,1)} fusion(bf16[128,2176]{0,1:T(8,128)(2,1)S(1)} %pad_maximum_fusion.1, f32[2048]{0:T(1024)S(1)} %broadcast_select_fusion), kind=kLoop, calls=%fused_computation | loop fusion | flops 786432 | bytes 1056768 | tf_op jit(solution)/shard_map/convert_element_type | solution.py:185
  14.3 1.0 constant_dynamic-slice_fusion
  15.2 1.2 %copy.39.sb = bf16[128,2048]{1,0:T(8,128)(2,1)S(1)} copy(bf16[128,2048]{0,1:T(8,128)(2,1)} %multiply_convert_fusion) | data formatting | bytes 1048576 | tf_op jit(solution)/shard_map/convert_element_type | solution.py:185
  16.6 5.9 %collective-permute-start.8 = (bf16[128,2048]{0,1:T(8,128)(2,1)}, bf16[128,2048]{0,1:T(8,128)(2,1)}, u32[]{:S(2)}, u32[]{:S(2)}) collective-permute-start(bf16[128,2048]{0,1:T(8,128)(2,1)} %multiply_convert_fusion), channel_id=1, source_target_pairs={{0,126},{1,127},{2,0},{3,1},{4,2},{5,3},{6,4},{7,5},{8,6},{9,7},{1... | collective-permute-start | bytes 1572872 | tf_op jit(solution)/shard_map/ppermute | solution.py:27
  22.5 0.1 copy.38.sa
  22.8 5.0 %shard_map.85 = (f32[1024,128]{1,0:T(8,128)S(1)}, f32[1024,32]{1,0:T(8,128)S(1)}, bf16[1024,64]{1,0:T(8,128)(2,1)S(1)}, bf16[1024,256]{1,0:T(8,128)(2,1)S(1)}) custom-call(bf16[1024,128]{1,0:T(8,128)(2,1)S(1)} %constant_dynamic-slice_fusion.1.ma, bf16[128,1024]{1,0:T(8,128)(2,1)S(1)} %copy.38.sa, bf16[2048,128]{1,0:T(8,128)(2,1)S(1)} %broadcast_multiply_fusion.mb, ...), custom_call_target="tpu_custom_call" | custom-call | tf_op jit(solution)/shard_map/pallas_call | solution.py:146
  27.8 2.0 %collective-permute-start.4 = (bf16[128,2048]{0,1:T(8,128)(2,1)}, bf16[128,2048]{0,1:T(8,128)(2,1)}, u32[]{:S(2)}, u32[]{:S(2)}) collective-permute-start(bf16[128,2048]{0,1:T(8,128)(2,1)} %multiply_convert_fusion), channel_id=1, source_target_pairs={{0,124},{1,125},{2,126},{3,127},{4,0},{5,1},{6,2},{7,3},{8,4},{9,5... | collective-permute-start | bytes 1572872 | tf_op jit(solution)/shard_map/ppermute | solution.py:27
  29.9 9.6 %collective-permute-start.7 = (bf16[2048,128]{1,0:T(8,128)(2,1)S(1)}, bf16[2048,128]{1,0:T(8,128)(2,1)}, u32[]{:S(2)}, u32[]{:S(2)}) collective-permute-start(bf16[2048,128]{1,0:T(8,128)(2,1)S(1)} %broadcast_multiply_fusion.mb), channel_id=1, source_target_pairs={{0,126},{1,127},{2,0},{3,1},{4,2},{5,3},{6,4},{7,5},{8,6},{9,7},{1... | collective-permute-start | bytes 1572872 | tf_op jit(solution)/shard_map/ppermute | solution.py:27
  39.5 0.4 collective-permute-start.3
  39.9 1.7 %collective-permute-start.1 = (bf16[2048,128]{1,0:T(8,128)(2,1)S(1)}, bf16[2048,128]{1,0:T(8,128)(2,1)}, u32[]{:S(2)}, u32[]{:S(2)}) collective-permute-start(bf16[2048,128]{1,0:T(8,128)(2,1)S(1)} %broadcast_multiply_fusion.mb), channel_id=1, source_target_pairs={{0,4},{1,5},{2,6},{3,7},{4,8},{5,9},{6,10},{7,11},{8,12},{9,13},{1... | collective-permute-start | bytes 1572872 | tf_op jit(solution)/shard_map/ppermute | solution.py:27
  41.8 0.1 copy.50.ws_turned
  42.0 0.1 fusion.1.w_turned
  42.1 2.1 %copy.41.sb = bf16[128,2048]{1,0:T(8,128)(2,1)} copy(bf16[128,2048]{0,1:T(8,128)(2,1)} %collective-permute-done.8) | data formatting | bytes 1048576 | tf_op jit(solution)/shard_map/ppermute | solution.py:27
  44.2 2.1 %copy.43.sb = bf16[128,2048]{1,0:T(8,128)(2,1)} copy(bf16[128,2048]{0,1:T(8,128)(2,1)} %collective-permute-done.6) | data formatting | bytes 1048576 | tf_op jit(solution)/shard_map/ppermute | solution.py:27
  46.2 1.2 %copy.45.sb = bf16[128,2048]{1,0:T(8,128)(2,1)S(1)} copy(bf16[128,2048]{0,1:T(8,128)(2,1)} %collective-permute-done.4) | data formatting | bytes 1048576 | tf_op jit(solution)/shard_map/ppermute | solution.py:27
  47.5 2.1 %copy.48.sb = bf16[128,2048]{1,0:T(8,128)(2,1)} copy(bf16[128,2048]{0,1:T(8,128)(2,1)} %collective-permute-done.2) | data formatting | bytes 1048576 | tf_op jit(solution)/shard_map/ppermute | solution.py:27
  49.5 0.3 collective-permute-done.7.mb
  49.8 1.0 copy-done.1
  50.9 5.9 %shard_map.86 = (f32[1024,128]{1,0:T(8,128)S(1)}, f32[1024,32]{1,0:T(8,128)S(1)}) custom-call(bf16[1024,64]{1,0:T(8,128)(2,1)S(1)} %get-tuple-element.32.near_dist, bf16[1024,256]{1,0:T(8,128)(2,1)S(1)} %get-tuple-element.33.near_mix, bf16[2048,128]{1,0:T(8,128)(2,1)} %collective-permute-done.7.mb, ...), custom_call_target="tpu_custom_call", output_to_operand_aliasing={{0}: (6, {}), {1}: (7, {})} | custom-call | tf_op jit(solution)/shard_map/pallas_call | solution.py:146
  56.8 3.6 %collective-permute-done.5.mb = bf16[2048,128]{1,0:T(8,128)(2,1)} collective-permute-done((bf16[2048,128]{1,0:T(8,128)(2,1)S(1)}, bf16[2048,128]{1,0:T(8,128)(2,1)}, u32[]{:S(2)}, u32[]{:S(2)}) %collective-permute-start.5) | collective-permute-done | bytes 524320 | tf_op jit(solution)/shard_map/ppermute | solution.py:27
  60.4 5.9 %shard_map.87 = (f32[1024,128]{1,0:T(8,128)S(1)}, f32[1024,32]{1,0:T(8,128)S(1)}) custom-call(bf16[1024,64]{1,0:T(8,128)(2,1)S(1)} %get-tuple-element.32.near_dist, bf16[1024,256]{1,0:T(8,128)(2,1)S(1)} %get-tuple-element.33.near_mix, bf16[2048,128]{1,0:T(8,128)(2,1)} %collective-permute-done.5.mb, ...), custom_call_target="tpu_custom_call", output_to_operand_aliasing={{0}: (6, {}), {1}: (7, {})} | custom-call | tf_op jit(solution)/shard_map/pallas_call | solution.py:146
  66.2 6.2 %shard_map.88 = (f32[1024,128]{1,0:T(8,128)S(1)}, f32[1024,32]{1,0:T(8,128)S(1)}) custom-call(bf16[1024,64]{1,0:T(8,128)(2,1)S(1)} %get-tuple-element.32.near_dist, bf16[1024,256]{1,0:T(8,128)(2,1)S(1)} %get-tuple-element.33.near_mix, bf16[2048,128]{1,0:T(8,128)(2,1)} %collective-permute-done.3.mb, ...), custom_call_target="tpu_custom_call", output_to_operand_aliasing={{0}: (6, {}), {1}: (7, {})} | custom-call | tf_op jit(solution)/shard_map/pallas_call | solution.py:146
  72.4 6.3 %shard_map.89 = (f32[72,128]{1,0:T(8,128)S(1)}, f32[72,128]{1,0:T(8,128)S(1)}, bf16[64,1024]{1,0:T(8,128)(2,1)S(1)}, bf16[64,1024]{1,0:T(8,128)(2,1)S(1)}) custom-call(bf16[1024,64]{1,0:T(8,128)(2,1)S(1)} %get-tuple-element.32.near_dist, bf16[1024,256]{1,0:T(8,128)(2,1)S(1)} %get-tuple-element.33.near_mix, bf16[2048,128]{1,0:T(8,128)(2,1)} %collective-permute-done.1.mb, ...), custom_call_target="tpu_custom_call" | custom-call | tf_op jit(solution)/shard_map/pallas_call | solution.py:146
  78.7 3.0 %collective-permute-start.10 = (f32[72,128]{1,0:T(8,128)S(1)}, f32[72,128]{1,0:T(8,128)S(1)}, u32[]{:S(2)}, u32[]{:S(2)}) collective-permute-start(f32[72,128]{1,0:T(8,128)S(1)} %get-tuple-element.48), channel_id=1, source_target_pairs={{0,1},{1,0},{2,3},{3,2},{4,5},{5,4},{6,7},{7,6},{8,9},{9,8},{10,11... | collective-permute-start | bytes 110600 | tf_op jit(solution)/shard_map/ppermute | solution.py:27
  81.7 2.6 %collective-permute-done.10 = f32[72,128]{1,0:T(8,128)S(1)} collective-permute-done((f32[72,128]{1,0:T(8,128)S(1)}, f32[72,128]{1,0:T(8,128)S(1)}, u32[]{:S(2)}, u32[]{:S(2)}) %collective-permute-start.10) | collective-permute-done | bytes 36896 | tf_op jit(solution)/shard_map/ppermute | solution.py:27
  84.3 1.2 %collective-permute-done.11 = f32[72,128]{1,0:T(8,128)S(1)} collective-permute-done((f32[72,128]{1,0:T(8,128)S(1)}, f32[72,128]{1,0:T(8,128)S(1)}, u32[]{:S(2)}, u32[]{:S(2)}) %collective-permute-start.11) | collective-permute-done | bytes 36896 | tf_op jit(solution)/shard_map/ppermute | solution.py:27
  85.5 3.0 %collective-permute-start.9 = (bf16[64,1024]{1,0:T(8,128)(2,1)S(1)}, bf16[64,1024]{1,0:T(8,128)(2,1)S(1)}, u32[]{:S(2)}, u32[]{:S(2)}) collective-permute-start(bf16[64,1024]{1,0:T(8,128)(2,1)S(1)} %get-tuple-element.46), channel_id=1, source_target_pairs={{0,1},{1,0},{2,3},{3,2},{4,5},{5,4},{6,7},{7,6},{8,9},{9,8},{10,11... | collective-permute-start | bytes 393224 | tf_op jit(solution)/shard_map/ppermute | solution.py:27
  88.5 1.0 collective-permute-done.12
  89.5 5.5 %collective-permute-done.13 = f32[72,128]{1,0:T(8,128)S(1)} collective-permute-done((f32[72,128]{1,0:T(8,128)S(1)}, f32[72,128]{1,0:T(8,128)S(1)}, u32[]{:S(2)}, u32[]{:S(2)}) %collective-permute-start.13) | collective-permute-done | bytes 36896 | tf_op jit(solution)/shard_map/ppermute | solution.py:27
  95.0 3.9 %collective-permute-done.14 = f32[72,128]{1,0:T(8,128)S(1)} collective-permute-done((f32[72,128]{1,0:T(8,128)S(1)}, f32[72,128]{1,0:T(8,128)S(1)}, u32[]{:S(2)}, u32[]{:S(2)}) %collective-permute-start.14) | collective-permute-done | bytes 36896 | tf_op jit(solution)/shard_map/ppermute | solution.py:27
  98.9 0.9 collective-permute-start.15
  99.8 4.6 %collective-permute-done.15 = f32[72,128]{1,0:T(8,128)S(1)} collective-permute-done((f32[72,128]{1,0:T(8,128)S(1)}, f32[72,128]{1,0:T(8,128)S(1)}, u32[]{:S(2)}, u32[]{:S(2)}) %collective-permute-start.15) | collective-permute-done | bytes 36896 | tf_op jit(solution)/shard_map/ppermute | solution.py:27
  104.4 0.4 collective-permute-start.16
  104.8 0.8 fusion
  105.6 2.7 %collective-permute-done.16 = f32[72,128]{1,0:T(8,128)S(1)} collective-permute-done((f32[72,128]{1,0:T(8,128)S(1)}, f32[72,128]{1,0:T(8,128)S(1)}, u32[]{:S(2)}, u32[]{:S(2)}) %collective-permute-start.16) | collective-permute-done | bytes 36896 | tf_op jit(solution)/shard_map/ppermute | solution.py:27
  108.4 0.6 slice_bitcast_fusion
  109.0 0.6 slice_bitcast_fusion.1
  (47 shorter events, 0.7 us)
Async XLA Ops:
  0.6 1.3 %copy-start.4 = (bf16[128,64]{0,1:T(8,128)(2,1)S(1)}, bf16[128,64]{0,1:T(8,128)(2,1)}, u32[]{:S(2)}) copy-start(bf16[128,64]{0,1:T(8,128)(2,1)} %param.9) | copy-start | bytes 49156
  2.1 3.7 %copy-start.7 = (s32[64]{0:T(128)S(1)}, s32[64]{0:T(128)}, u32[]{:S(2)}) copy-start(s32[64]{0:T(128)} %param.13) | copy-start | bytes 772
  2.2 4.3 %copy-start.5 = (s32[2048]{0:T(1024)S(1)}, s32[2048]{0:T(1024)}, u32[]{:S(2)}) copy-start(s32[2048]{0:T(1024)} %param.12) | copy-start | bytes 24580
  2.2 4.9 %copy-start.3 = (bf16[2048,128]{1,0:T(8,128)(2,1)S(1)}, bf16[2048,128]{1,0:T(8,128)(2,1)}, u32[]{:S(2)}) copy-start(bf16[2048,128]{1,0:T(8,128)(2,1)} %param.8) | copy-start | bytes 1572868
  2.4 10.0 %collective-permute-start = (bf16[64,2176]{1,0:T(8,128)(2,1)S(1)}, bf16[64,2176]{1,0:T(8,128)(2,1)S(1)}, u32[]{:S(2)}, u32[]{:S(2)}) collective-permute-start(bf16[64,2176]{1,0:T(8,128)(2,1)S(1)} %copy.36), channel_id=1, source_target_pairs={{0,1},{1,0},{2,3},{3,2},{4,5},{5,4},{6,7},{7,6},{8,9},{9,8},{10,11... | collective-permute-start | bytes 835592 | tf_op jit(solution)/shard_map/ppermute | solution.py:27
  7.1 1.1 copy-start.6
  16.6 22.9 %collective-permute-start.8 = (bf16[128,2048]{0,1:T(8,128)(2,1)}, bf16[128,2048]{0,1:T(8,128)(2,1)}, u32[]{:S(2)}, u32[]{:S(2)}) collective-permute-start(bf16[128,2048]{0,1:T(8,128)(2,1)} %multiply_convert_fusion), channel_id=1, source_target_pairs={{0,126},{1,127},{2,0},{3,1},{4,2},{5,3},{6,4},{7,5},{8,6},{9,7},{1... | collective-permute-start | bytes 1572872 | tf_op jit(solution)/shard_map/ppermute | solution.py:27
  22.5 17.0 %collective-permute-start.6 = (bf16[128,2048]{0,1:T(8,128)(2,1)}, bf16[128,2048]{0,1:T(8,128)(2,1)}, u32[]{:S(2)}, u32[]{:S(2)}) collective-permute-start(bf16[128,2048]{0,1:T(8,128)(2,1)} %multiply_convert_fusion), channel_id=1, source_target_pairs={{0,2},{1,3},{2,4},{3,5},{4,6},{5,7},{6,8},{7,9},{8,10},{9,11},{10,... | collective-permute-start | bytes 1572872 | tf_op jit(solution)/shard_map/ppermute | solution.py:27
  27.8 12.1 %collective-permute-start.4 = (bf16[128,2048]{0,1:T(8,128)(2,1)}, bf16[128,2048]{0,1:T(8,128)(2,1)}, u32[]{:S(2)}, u32[]{:S(2)}) collective-permute-start(bf16[128,2048]{0,1:T(8,128)(2,1)} %multiply_convert_fusion), channel_id=1, source_target_pairs={{0,124},{1,125},{2,126},{3,127},{4,0},{5,1},{6,2},{7,3},{8,4},{9,5... | collective-permute-start | bytes 1572872 | tf_op jit(solution)/shard_map/ppermute | solution.py:27
  29.8 17.7 %collective-permute-start.2 = (bf16[128,2048]{0,1:T(8,128)(2,1)}, bf16[128,2048]{0,1:T(8,128)(2,1)}, u32[]{:S(2)}, u32[]{:S(2)}) collective-permute-start(bf16[128,2048]{0,1:T(8,128)(2,1)} %multiply_convert_fusion), channel_id=1, source_target_pairs={{0,4},{1,5},{2,6},{3,7},{4,8},{5,9},{6,10},{7,11},{8,12},{9,13},{1... | collective-permute-start | bytes 1572872 | tf_op jit(solution)/shard_map/ppermute | solution.py:27
  29.9 19.9 %collective-permute-start.7 = (bf16[2048,128]{1,0:T(8,128)(2,1)S(1)}, bf16[2048,128]{1,0:T(8,128)(2,1)}, u32[]{:S(2)}, u32[]{:S(2)}) collective-permute-start(bf16[2048,128]{1,0:T(8,128)(2,1)S(1)} %broadcast_multiply_fusion.mb), channel_id=1, source_target_pairs={{0,126},{1,127},{2,0},{3,1},{4,2},{5,3},{6,4},{7,5},{8,6},{9,7},{1... | collective-permute-start | bytes 1572872 | tf_op jit(solution)/shard_map/ppermute | solution.py:27
  39.5 20.9 %collective-permute-start.5 = (bf16[2048,128]{1,0:T(8,128)(2,1)S(1)}, bf16[2048,128]{1,0:T(8,128)(2,1)}, u32[]{:S(2)}, u32[]{:S(2)}) collective-permute-start(bf16[2048,128]{1,0:T(8,128)(2,1)S(1)} %broadcast_multiply_fusion.mb), channel_id=1, source_target_pairs={{0,2},{1,3},{2,4},{3,5},{4,6},{5,7},{6,8},{7,9},{8,10},{9,11},{10,... | collective-permute-start | bytes 1572872 | tf_op jit(solution)/shard_map/ppermute | solution.py:27
  39.5 26.7 %collective-permute-start.3 = (bf16[2048,128]{1,0:T(8,128)(2,1)S(1)}, bf16[2048,128]{1,0:T(8,128)(2,1)}, u32[]{:S(2)}, u32[]{:S(2)}) collective-permute-start(bf16[2048,128]{1,0:T(8,128)(2,1)S(1)} %broadcast_multiply_fusion.mb), channel_id=1, source_target_pairs={{0,124},{1,125},{2,126},{3,127},{4,0},{5,1},{6,2},{7,3},{8,4},{9,5... | collective-permute-start | bytes 1572872 | tf_op jit(solution)/shard_map/ppermute | solution.py:27
  39.9 32.5 %collective-permute-start.1 = (bf16[2048,128]{1,0:T(8,128)(2,1)S(1)}, bf16[2048,128]{1,0:T(8,128)(2,1)}, u32[]{:S(2)}, u32[]{:S(2)}) collective-permute-start(bf16[2048,128]{1,0:T(8,128)(2,1)S(1)} %broadcast_multiply_fusion.mb), channel_id=1, source_target_pairs={{0,4},{1,5},{2,6},{3,7},{4,8},{5,9},{6,10},{7,11},{8,12},{9,13},{1... | collective-permute-start | bytes 1572872 | tf_op jit(solution)/shard_map/ppermute | solution.py:27
  49.8 1.0 copy-start.1
  50.9 9.5 %copy-start = (bf16[128,2048]{1,0:T(8,128)(2,1)S(1)}, bf16[128,2048]{1,0:T(8,128)(2,1)}, u32[]{:S(2)}) copy-start(bf16[128,2048]{1,0:T(8,128)(2,1)} %copy.43.sb) | copy-start | bytes 1572868
  66.2 6.2 %copy-start.2 = (bf16[128,2048]{1,0:T(8,128)(2,1)S(1)}, bf16[128,2048]{1,0:T(8,128)(2,1)}, u32[]{:S(2)}) copy-start(bf16[128,2048]{1,0:T(8,128)(2,1)} %copy.48.sb) | copy-start | bytes 1572868
  78.7 5.5 %collective-permute-start.10 = (f32[72,128]{1,0:T(8,128)S(1)}, f32[72,128]{1,0:T(8,128)S(1)}, u32[]{:S(2)}, u32[]{:S(2)}) collective-permute-start(f32[72,128]{1,0:T(8,128)S(1)} %get-tuple-element.48), channel_id=1, source_target_pairs={{0,1},{1,0},{2,3},{3,2},{4,5},{5,4},{6,7},{7,6},{8,9},{9,8},{10,11... | collective-permute-start | bytes 110600 | tf_op jit(solution)/shard_map/ppermute | solution.py:27
  84.3 1.2 %collective-permute-start.11 = (f32[72,128]{1,0:T(8,128)S(1)}, f32[72,128]{1,0:T(8,128)S(1)}, u32[]{:S(2)}, u32[]{:S(2)}) collective-permute-start(f32[72,128]{1,0:T(8,128)S(1)} %add.54), channel_id=1, source_target_pairs={{0,2},{1,3},{2,0},{3,1},{4,6},{5,7},{6,4},{7,5},{8,10},{9,11},{10,... | collective-permute-start | bytes 110600 | tf_op jit(solution)/shard_map/ppermute | solution.py:27
  85.5 4.0 %collective-permute-start.12 = (f32[72,128]{1,0:T(8,128)S(1)}, f32[72,128]{1,0:T(8,128)S(1)}, u32[]{:S(2)}, u32[]{:S(2)}) collective-permute-start(f32[72,128]{1,0:T(8,128)S(1)} %add.55), channel_id=1, source_target_pairs={{0,4},{1,5},{2,6},{3,7},{4,0},{5,1},{6,2},{7,3},{8,12},{9,13},{10,... | collective-permute-start | bytes 110600 | tf_op jit(solution)/shard_map/ppermute | solution.py:27
  85.5 19.3 %collective-permute-start.9 = (bf16[64,1024]{1,0:T(8,128)(2,1)S(1)}, bf16[64,1024]{1,0:T(8,128)(2,1)S(1)}, u32[]{:S(2)}, u32[]{:S(2)}) collective-permute-start(bf16[64,1024]{1,0:T(8,128)(2,1)S(1)} %get-tuple-element.46), channel_id=1, source_target_pairs={{0,1},{1,0},{2,3},{3,2},{4,5},{5,4},{6,7},{7,6},{8,9},{9,8},{10,11... | collective-permute-start | bytes 393224 | tf_op jit(solution)/shard_map/ppermute | solution.py:27
  89.5 5.5 %collective-permute-start.13 = (f32[72,128]{1,0:T(8,128)S(1)}, f32[72,128]{1,0:T(8,128)S(1)}, u32[]{:S(2)}, u32[]{:S(2)}) collective-permute-start(f32[72,128]{1,0:T(8,128)S(1)} %add.56), channel_id=1, source_target_pairs={{0,8},{1,9},{2,10},{3,11},{4,12},{5,13},{6,14},{7,15},{8,0},{9,1},... | collective-permute-start | bytes 110600 | tf_op jit(solution)/shard_map/ppermute | solution.py:27
  94.9 4.0 %collective-permute-start.14 = (f32[72,128]{1,0:T(8,128)S(1)}, f32[72,128]{1,0:T(8,128)S(1)}, u32[]{:S(2)}, u32[]{:S(2)}) collective-permute-start(f32[72,128]{1,0:T(8,128)S(1)} %add.57), channel_id=1, source_target_pairs={{0,16},{1,17},{2,18},{3,19},{4,20},{5,21},{6,22},{7,23},{8,24},{9,... | collective-permute-start | bytes 110600 | tf_op jit(solution)/shard_map/ppermute | solution.py:27
  98.9 5.5 %collective-permute-start.15 = (f32[72,128]{1,0:T(8,128)S(1)}, f32[72,128]{1,0:T(8,128)S(1)}, u32[]{:S(2)}, u32[]{:S(2)}) collective-permute-start(f32[72,128]{1,0:T(8,128)S(1)} %add.58), channel_id=1, source_target_pairs={{0,32},{1,33},{2,34},{3,35},{4,36},{5,37},{6,38},{7,39},{8,40},{9,... | collective-permute-start | bytes 110600 | tf_op jit(solution)/shard_map/ppermute | solution.py:27
  104.4 4.0 %collective-permute-start.16 = (f32[72,128]{1,0:T(8,128)S(1)}, f32[72,128]{1,0:T(8,128)S(1)}, u32[]{:S(2)}, u32[]{:S(2)}) collective-permute-start(f32[72,128]{1,0:T(8,128)S(1)} %add.59), channel_id=1, source_target_pairs={{0,64},{1,65},{2,66},{3,67},{4,68},{5,69},{6,70},{7,71},{8,72},{9,... | collective-permute-start | bytes 110600 | tf_op jit(solution)/shard_map/ppermute | solution.py:27

commit v3 on v2

--- a/solution.py
+++ b/solution.py
@@ -108,6 +108,45 @@
     )
 
 
+def pack_body(cot_t, wh_t, out):
+    hits = cot_t.shape[1]
+    out[:, :hits] = cot_t[...]
+    out[:, hits:] = wh_t[...]
+
+
+def spread_body(half, packed, arrived, factor, ws_t, scaled, sa, w, w_t, w_turned, ws_turned):
+    width = packed.shape[0]
+    hits, rows = factor.shape[1], sa.shape[1]
+    for i, ref in enumerate((packed, arrived)):
+        rs = slice(i * width, (i + 1) * width)
+        value = (ref[:, :hits].astype(F32) * factor[...]).astype(BF16)
+        scaled[rs, :] = value
+        w_t[rs, :] = ref[:, hits:]
+
+        @pl.when(half[0] == 0)
+        def _():
+            sa[rs, :] = value[:, :rows]
+
+        @pl.when(half[0] == 1)
+        def _():
+            sa[rs, :] = value[:, rows:]
+
+    full = jnp.transpose(w_t[...].astype(F32))
+    w[...] = full.astype(BF16)
+    triple = jnp.concatenate([ws_t[...].astype(F32)] * 3 + [jnp.zeros(ws_t.shape, F32)], 0)
+    sides = jnp.transpose(triple)
+
+    @pl.when(half[0] == 0)
+    def _():
+        w_turned[...] = full.astype(BF16)
+        ws_turned[...] = sides.astype(BF16)
+
+    @pl.when(half[0] == 1)
+    def _():
+        w_turned[...] = jnp.concatenate([full[width:], full[:width]], 0).astype(BF16)
+        ws_turned[...] = jnp.concatenate([sides[width:], sides[:width]], 0).astype(BF16)
+
+
 def last_body(
     near_dist, near_mix, mb, sb, w_t, ws_t, ah, ac, ma, live, w_turned, ws_turned,
     own, other, mine, theirs, dist_sc, mix_sc, mom_sc, oh, oc,
@@ -155,6 +194,9 @@
             *extra,
         ],
         compiler_params=pltpu.CompilerParams(vmem_limit_bytes=48 << 20),
+        cost_estimate=pl.CostEstimate(
+            flops=4 * cols * cols * feats, transcendentals=cols * cols // 2, bytes_accessed=4 * cols * feats
+        ),
         **kw,
     )(*operands)
 
@@ -176,24 +218,29 @@
     scale = 1.0 / jnp.sqrt(window_count.astype(F32))
     other_feat = lambda b, f: (b, 1 - f)
 
-    packed = jnp.concatenate([cotangent.T, weight_h.T], 1)
+    vmem = pl.BlockSpec(memory_space=pltpu.VMEM)
+    depth = inputs.shape[1]
+    packed = pl.pallas_call(
+        pack_body,
+        out_shape=jax.ShapeDtypeStruct((width, hits + depth), BF16),
+        in_specs=[vmem] * 2,
+        out_specs=vmem,
+    )(cotangent.T, weight_h.T)
     arrived = moved(packed, other_feat)
     masked = inputs * live.astype(BF16)[:, None]
     offsets = [1, -1, 2, -2][: 2 * WINDOW]
     masked_far = [moved(masked, lambda b, f, d=d: (b - d, f)) for d in offsets]
-    both = jnp.concatenate([packed, arrived], 0)
-    scaled = (both[:, :hits].astype(F32) * (live * scale)[None, :]).astype(BF16)
-    w_t = both[:, hits:]
-    w = w_t.T
-    ws_t = jnp.zeros((8, weight_s.shape[0]), BF16).at[:dims].set(weight_s.T)
-    turn = my_half * width
-    w_turned = jnp.roll(w, -turn, 0)
-    ws_turned = jnp.roll(
-        jnp.concatenate([ws_t, ws_t, ws_t, jnp.zeros_like(ws_t)], 0).T, -turn, 0
-    )
+    ws_t = jnp.zeros((8, depth), BF16).at[:dims].set(weight_s.T)
+    shapes = [(feats, hits), (feats, rows), (depth, feats), (feats, depth), (depth, feats)]
+    scaled, sa, w, w_t, w_turned, ws_turned = pl.pallas_call(
+        spread_body,
+        out_shape=[jax.ShapeDtypeStruct(shape, BF16) for shape in shapes + [(depth, 32)]],
+        in_specs=[pl.BlockSpec(memory_space=pltpu.SMEM)] + [vmem] * 4,
+        out_specs=[vmem] * 6,
+        compiler_params=pltpu.CompilerParams(vmem_limit_bytes=32 << 20),
+    )(my_half[None], packed, arrived, (live * scale)[None, :], ws_t)
     start = my_half * rows
     ma = lax.dynamic_slice_in_dim(masked, start, rows, 0)
-    sa = lax.dynamic_slice_in_dim(scaled, start, rows, 1)
     live_rows = lax.dynamic_slice_in_dim(live, start, rows, 0)[None, :]
     sums = [
         jax.ShapeDtypeStruct((rows, feats), F32),
@@ -203,12 +250,10 @@
         jax.ShapeDtypeStruct((rows, 64), BF16),
         jax.ShapeDtypeStruct((rows, 2 * feats), BF16),
     ]
-    scaled_far = [moved(scaled, lambda b, f, d=d: (b - d, f)) for d in offsets[:2]]
+    scaled_far = [moved(scaled, lambda b, f, d=d: (b - d, f)) for d in offsets]
     oh, oc, near_dist, near_mix = call(
         first_body, (ma, sa, masked, scaled, w, w_t, ws_t), sums + near, hits, feats
     )
-    late, oh, oc = lax.optimization_barrier((scaled, oh, oc))
-    scaled_far += [moved(late, lambda b, f, d=d: (b - d, f)) for d in offsets[2:]]
     for mb, sb in list(zip(masked_far, scaled_far))[:-1]:
         oh, oc = call(
             next_body,

time: 110 us -> 92.2 us (0.84)
  local copies, waits for them, and re-layouts: 14.3 us -> 3.14 us
  starting transfers between devices: 30.4 us -> 27.2 us
  other arithmetic: 4.41 us -> 2.46 us
  Pallas kernels: 29.2 us -> 27.7 us
    ppermute x5 -> x0, local copies, waits for them, and re-layouts: 7.75 us -> none  [moved(): return lax.ppermute(x, ('blk', 'feat'), route)]
    pallas_call x5, Pallas kernels: 29.2 us -> 25.8 us  [call(): pl.pallas_call(body, out_shape=outs, in_specs=[vmem] * len(operands), out...]
    ppermute x17, starting transfers between devices: 30.4 us -> 27.2 us  [moved(): return lax.ppermute(x, ('blk', 'feat'), route)]
    pallas_call x0 -> x2, Pallas kernels: none -> 1.96 us  [the longest x1 1.74 us: local(): pl.pallas_call(pack_body, out_shape=jax.ShapeDtypeStruct((width, hits + d...]
    convert_element_type x1 -> x0, local copies, waits for them, and re-layouts: 1.25 us -> none  [local(): scaled = (both[:, :hits].astype(F32) * (live * scale)[None, :]).astype(BF16)]
    convert_element_type x1 -> x0, other arithmetic: 1.14 us -> none  [local(): scaled = (both[:, :hits].astype(F32) * (live * scale)[None, :]).astype(BF16)]
    dynamic_slice x2 -> x0, local copies, waits for them, and re-layouts: 1.11 us -> none  [local(): sa = lax.dynamic_slice_in_dim(scaled, start, rows, 1)]
    unnamed x19 -> x14, local copies, waits for them, and re-layouts: 2.56 us -> 1.91 us
  transfers between devices with their start and end apart: 17 -> 17, of which waited for: 10 -> 8; matrix products, arithmetic and copies ran while one was open for 10% -> 3% of each run, Pallas kernels for 21% -> 23%
where the time goes in v3:
time: 92.2 us; the launch traced here: 91.9 us
  waiting for transfers between devices  29.8 us (32%)
  Pallas kernels  27.7 us (30%)
  starting transfers between devices  27.2 us (30%)
  local copies, waits for them, and re-layouts  3.14 us (3%)
  other arithmetic  2.46 us (3%)
  between operations  1.54 us (2%)
    ppermute x17, waiting for transfers between devices, moved(): return lax.ppermute(x, ('blk', 'feat'), route)  29.8 us
    ppermute x17, starting transfers between devices, moved(): return lax.ppermute(x, ('blk', 'feat'), route)  27.2 us
    pallas_call x5, Pallas kernels, call(): pl.pallas_call(body, out_shape=outs, in_specs=[vmem] * len(operands), out...  25.8 us
    unnamed x14, local copies, waits for them, and re-layouts  1.91 us
  transfers between devices with their start and end apart: 17, of which 8 were waited for; matrix products, arithmetic and copies ran while one was open for 3% of the time, Pallas kernels for 23%

profile of v3, /device:TPU:0, one launch (start us, length us, event | category | flops | bytes accessed | tf_op | source)
XLA Modules:
  0.0 91.9 jit_solution(15009415968363041892)
XLA Ops:
  0.7 1.7 %shard_map.85.packed = bf16[64,2176]{1,0:T(8,128)(2,1)} custom-call(bf16[64,2048]{1,0:T(8,128)(2,1)} %bitcast.14, bf16[64,128]{1,0:T(8,128)(2,1)} %bitcast.15), custom_call_target="tpu_custom_call" | custom-call | tf_op jit(solution)/shard_map/pallas_call | solution.py:223
  2.4 3.3 %collective-permute-start = (bf16[64,2176]{1,0:T(8,128)(2,1)}, bf16[64,2176]{1,0:T(8,128)(2,1)S(1)}, u32[]{:S(2)}, u32[]{:S(2)}) collective-permute-start(bf16[64,2176]{1,0:T(8,128)(2,1)} %shard_map.85.packed), channel_id=1, source_target_pairs={{0,1},{1,0},{2,3},{3,2},{4,5},{5,4},{6,7},{7,6},{8,9},{9,8},{10,11... | collective-permute-start | bytes 835592 | tf_op jit(solution)/shard_map/ppermute | solution.py:27
  5.7 0.6 fusion.3
  6.3 0.6 fusion.4
  7.0 0.3 broadcast_multiply_fusion.mb
  7.3 5.6 %collective-permute-start.7 = (bf16[2048,128]{1,0:T(8,128)(2,1)S(1)}, bf16[2048,128]{1,0:T(8,128)(2,1)S(1)}, u32[]{:S(2)}, u32[]{:S(2)}) collective-permute-start(bf16[2048,128]{1,0:T(8,128)(2,1)S(1)} %broadcast_multiply_fusion.mb), channel_id=1, source_target_pairs={{0,126},{1,127},{2,0},{3,1},{4,2},{5,3},{6,4},{7,5},{8,6},{9,7},{1... | collective-permute-start | bytes 1572872 | tf_op jit(solution)/shard_map/ppermute | solution.py:27
  12.9 0.0 collective-permute-start.5
  13.6 0.0 copy-start.5
  13.6 0.7 copy-done.5
  14.3 0.0 collective-permute-done.arrived
  14.3 0.2 shard_map.86
  14.6 0.0 copy-start.1
  14.6 0.6 copy-done.1
  15.2 6.0 %collective-permute-start.8 = (bf16[128,2048]{1,0:T(8,128)(2,1)S(1)}, bf16[128,2048]{1,0:T(8,128)(2,1)}, u32[]{:S(2)}, u32[]{:S(2)}) collective-permute-start(bf16[128,2048]{1,0:T(8,128)(2,1)S(1)} %get-tuple-element.36.sb), channel_id=1, source_target_pairs={{0,126},{1,127},{2,0},{3,1},{4,2},{5,3},{6,4},{7,5},{8,6},{9,7},{1... | collective-permute-start | bytes 1572872 | tf_op jit(solution)/shard_map/ppermute | solution.py:27
  21.1 0.0 collective-permute-start.6
  21.1 0.4 collective-permute-start.3
  21.6 0.0 collective-permute-done.7.mb
  21.6 0.1 collective-permute-start.4
  21.7 0.6 copy-done.2
  22.3 4.9 %shard_map.87 = (f32[1024,128]{1,0:T(8,128)S(1)}, f32[1024,32]{1,0:T(8,128)S(1)}, bf16[1024,64]{1,0:T(8,128)(2,1)S(1)}, bf16[1024,256]{1,0:T(8,128)(2,1)S(1)}) custom-call(bf16[1024,128]{1,0:T(8,128)(2,1)S(1)} %constant_dynamic-slice_fusion.ma, bf16[128,1024]{1,0:T(8,128)(2,1)S(1)} %get-tuple-element.35.sa, bf16[2048,128]{1,0:T(8,128)(2,1)S(1)} %broadcast_multiply_fusion.mb, ...), custom_call_target="tpu_custom_call" | custom-call | flops 2147483648 | bytes 1048576 | tf_op jit(solution)/shard_map/pallas_call | solution.py:185
  27.2 0.0 collective-permute-done.5.mb
  27.2 1.7 %collective-permute-start.1 = (bf16[2048,128]{1,0:T(8,128)(2,1)S(1)}, bf16[2048,128]{1,0:T(8,128)(2,1)S(1)}, u32[]{:S(2)}, u32[]{:S(2)}) collective-permute-start(bf16[2048,128]{1,0:T(8,128)(2,1)S(1)} %broadcast_multiply_fusion.mb), channel_id=1, source_target_pairs={{0,4},{1,5},{2,6},{3,7},{4,8},{5,9},{6,10},{7,11},{8,12},{9,13},{1... | collective-permute-start | bytes 1572872 | tf_op jit(solution)/shard_map/ppermute | solution.py:27
  28.9 0.0 collective-permute-done.8.sb
  28.9 1.4 %collective-permute-start.2 = (bf16[128,2048]{1,0:T(8,128)(2,1)S(1)}, bf16[128,2048]{1,0:T(8,128)(2,1)S(1)}, u32[]{:S(2)}, u32[]{:S(2)}) collective-permute-start(bf16[128,2048]{1,0:T(8,128)(2,1)S(1)} %get-tuple-element.36.sb), channel_id=1, source_target_pairs={{0,4},{1,5},{2,6},{3,7},{4,8},{5,9},{6,10},{7,11},{8,12},{9,13},{1... | collective-permute-start | bytes 1572872 | tf_op jit(solution)/shard_map/ppermute | solution.py:27
  30.3 5.8 %shard_map.88 = (f32[1024,128]{1,0:T(8,128)S(1)}, f32[1024,32]{1,0:T(8,128)S(1)}) custom-call(bf16[1024,64]{1,0:T(8,128)(2,1)S(1)} %get-tuple-element.39.near_dist, bf16[1024,256]{1,0:T(8,128)(2,1)S(1)} %get-tuple-element.40.near_mix, bf16[2048,128]{1,0:T(8,128)(2,1)S(1)} %collective-permute-done.7.mb, ...), custom_call_target="tpu_custom_call", output_to_operand_aliasing={{0}: (6, {}), {1}: (7, {})} | custom-call | flops 2147483648 | bytes 1048576 | tf_op jit(solution)/shard_map/pallas_call | solution.py:185
  36.2 4.8 %shard_map.89 = (f32[1024,128]{1,0:T(8,128)S(1)}, f32[1024,32]{1,0:T(8,128)S(1)}) custom-call(bf16[1024,64]{1,0:T(8,128)(2,1)S(1)} %get-tuple-element.39.near_dist, bf16[1024,256]{1,0:T(8,128)(2,1)S(1)} %get-tuple-element.40.near_mix, bf16[2048,128]{1,0:T(8,128)(2,1)S(1)} %collective-permute-done.5.mb, ...), custom_call_target="tpu_custom_call", output_to_operand_aliasing={{0}: (6, {}), {1}: (7, {})} | custom-call | flops 2147483648 | bytes 1048576 | tf_op jit(solution)/shard_map/pallas_call | solution.py:185
  41.0 0.0 collective-permute-done.3.mb
  41.0 9.3 %collective-permute-done.4.sb = bf16[128,2048]{1,0:T(8,128)(2,1)S(1)} collective-permute-done((bf16[128,2048]{1,0:T(8,128)(2,1)S(1)}, bf16[128,2048]{1,0:T(8,128)(2,1)S(1)}, u32[]{:S(2)}, u32[]{:S(2)}) %collective-permute-start.4) | collective-permute-done | bytes 524320 | tf_op jit(solution)/shard_map/ppermute | solution.py:27
  50.3 5.0 %shard_map.90 = (f32[1024,128]{1,0:T(8,128)S(1)}, f32[1024,32]{1,0:T(8,128)S(1)}) custom-call(bf16[1024,64]{1,0:T(8,128)(2,1)S(1)} %get-tuple-element.39.near_dist, bf16[1024,256]{1,0:T(8,128)(2,1)S(1)} %get-tuple-element.40.near_mix, bf16[2048,128]{1,0:T(8,128)(2,1)S(1)} %collective-permute-done.3.mb, ...), custom_call_target="tpu_custom_call", output_to_operand_aliasing={{0}: (6, {}), {1}: (7, {})} | custom-call | flops 2147483648 | bytes 1048576 | tf_op jit(solution)/shard_map/pallas_call | solution.py:185
  55.3 0.0 collective-permute-done.2.sb
  55.3 5.2 %shard_map.91 = (f32[72,128]{1,0:T(8,128)S(1)}, f32[72,128]{1,0:T(8,128)S(1)}, bf16[64,1024]{1,0:T(8,128)(2,1)S(1)}, bf16[64,1024]{1,0:T(8,128)(2,1)S(1)}) custom-call(bf16[1024,64]{1,0:T(8,128)(2,1)S(1)} %get-tuple-element.39.near_dist, bf16[1024,256]{1,0:T(8,128)(2,1)S(1)} %get-tuple-element.40.near_mix, bf16[2048,128]{1,0:T(8,128)(2,1)S(1)} %collective-permute-done.1.mb, ...), custom_call_target="tpu_custom_call" | custom-call | flops 2147483648 | bytes 1048576 | tf_op jit(solution)/shard_map/pallas_call | solution.py:185
  60.5 1.9 %collective-permute-start.10 = (f32[72,128]{1,0:T(8,128)S(1)}, f32[72,128]{1,0:T(8,128)S(1)}, u32[]{:S(2)}, u32[]{:S(2)}) collective-permute-start(f32[72,128]{1,0:T(8,128)S(1)} %get-tuple-element.54), channel_id=1, source_target_pairs={{0,1},{1,0},{2,3},{3,2},{4,5},{5,4},{6,7},{7,6},{8,9},{9,8},{10,11... | collective-permute-start | bytes 110600 | tf_op jit(solution)/shard_map/ppermute | solution.py:27
  62.5 3.6 %collective-permute-done.10 = f32[72,128]{1,0:T(8,128)S(1)} collective-permute-done((f32[72,128]{1,0:T(8,128)S(1)}, f32[72,128]{1,0:T(8,128)S(1)}, u32[]{:S(2)}, u32[]{:S(2)}) %collective-permute-start.10) | collective-permute-done | bytes 36896 | tf_op jit(solution)/shard_map/ppermute | solution.py:27
  66.1 0.9 collective-permute-start.11
  67.0 0.9 collective-permute-done.11
  67.9 2.6 %collective-permute-start.9 = (bf16[64,1024]{1,0:T(8,128)(2,1)S(1)}, bf16[64,1024]{1,0:T(8,128)(2,1)S(1)}, u32[]{:S(2)}, u32[]{:S(2)}) collective-permute-start(bf16[64,1024]{1,0:T(8,128)(2,1)S(1)} %get-tuple-element.52), channel_id=1, source_target_pairs={{0,1},{1,0},{2,3},{3,2},{4,5},{5,4},{6,7},{7,6},{8,9},{9,8},{10,11... | collective-permute-start | bytes 393224 | tf_op jit(solution)/shard_map/ppermute | solution.py:27
  70.5 1.3 %collective-permute-done.12 = f32[72,128]{1,0:T(8,128)S(1)} collective-permute-done((f32[72,128]{1,0:T(8,128)S(1)}, f32[72,128]{1,0:T(8,128)S(1)}, u32[]{:S(2)}, u32[]{:S(2)}) %collective-permute-start.12) | collective-permute-done | bytes 36896 | tf_op jit(solution)/shard_map/ppermute | solution.py:27
  71.8 0.0 collective-permute-start.13
  71.8 5.5 %collective-permute-done.13 = f32[72,128]{1,0:T(8,128)S(1)} collective-permute-done((f32[72,128]{1,0:T(8,128)S(1)}, f32[72,128]{1,0:T(8,128)S(1)}, u32[]{:S(2)}, u32[]{:S(2)}) %collective-permute-start.13) | collective-permute-done | bytes 36896 | tf_op jit(solution)/shard_map/ppermute | solution.py:27
  77.3 0.0 collective-permute-start.14
  77.3 3.9 %collective-permute-done.14 = f32[72,128]{1,0:T(8,128)S(1)} collective-permute-done((f32[72,128]{1,0:T(8,128)S(1)}, f32[72,128]{1,0:T(8,128)S(1)}, u32[]{:S(2)}, u32[]{:S(2)}) %collective-permute-start.14) | collective-permute-done | bytes 36896 | tf_op jit(solution)/shard_map/ppermute | solution.py:27
  81.3 2.0 %collective-permute-start.15 = (f32[72,128]{1,0:T(8,128)S(1)}, f32[72,128]{1,0:T(8,128)S(1)}, u32[]{:S(2)}, u32[]{:S(2)}) collective-permute-start(f32[72,128]{1,0:T(8,128)S(1)} %add.41), channel_id=1, source_target_pairs={{0,32},{1,33},{2,34},{3,35},{4,36},{5,37},{6,38},{7,39},{8,40},{9,... | collective-permute-start | bytes 110600 | tf_op jit(solution)/shard_map/ppermute | solution.py:27
  83.2 3.5 %collective-permute-done.15 = f32[72,128]{1,0:T(8,128)S(1)} collective-permute-done((f32[72,128]{1,0:T(8,128)S(1)}, f32[72,128]{1,0:T(8,128)S(1)}, u32[]{:S(2)}, u32[]{:S(2)}) %collective-permute-start.15) | collective-permute-done | bytes 36896 | tf_op jit(solution)/shard_map/ppermute | solution.py:27
  86.7 1.3 %collective-permute-start.16 = (f32[72,128]{1,0:T(8,128)S(1)}, f32[72,128]{1,0:T(8,128)S(1)}, u32[]{:S(2)}, u32[]{:S(2)}) collective-permute-start(f32[72,128]{1,0:T(8,128)S(1)} %add.42), channel_id=1, source_target_pairs={{0,64},{1,65},{2,66},{3,67},{4,68},{5,69},{6,70},{7,71},{8,72},{9,... | collective-permute-start | bytes 110600 | tf_op jit(solution)/shard_map/ppermute | solution.py:27
  88.1 0.8 fusion
  88.9 1.8 %collective-permute-done.16 = f32[72,128]{1,0:T(8,128)S(1)} collective-permute-done((f32[72,128]{1,0:T(8,128)S(1)}, f32[72,128]{1,0:T(8,128)S(1)}, u32[]{:S(2)}, u32[]{:S(2)}) %collective-permute-start.16) | collective-permute-done | bytes 36896 | tf_op jit(solution)/shard_map/ppermute | solution.py:27
  90.7 0.6 slice_bitcast_fusion
  91.3 0.6 slice_bitcast_fusion.1
  (25 shorter events, 0.1 us)
Async XLA Ops:
  0.6 6.4 %copy-start.3 = (bf16[2048,128]{1,0:T(8,128)(2,1)S(1)}, bf16[2048,128]{1,0:T(8,128)(2,1)}, u32[]{:S(2)}) copy-start(bf16[2048,128]{1,0:T(8,128)(2,1)} %param.8) | copy-start | bytes 1572868
  0.6 5.0 %copy-start.6 = (s32[64]{0:T(128)S(1)}, s32[64]{0:T(128)}, u32[]{:S(2)}) copy-start(s32[64]{0:T(128)} %param.13) | copy-start | bytes 772
  2.4 3.9 %copy-start.4 = (s32[2048]{0:T(1024)S(1)}, s32[2048]{0:T(1024)}, u32[]{:S(2)}) copy-start(s32[2048]{0:T(1024)} %param.12) | copy-start | bytes 24580
  2.4 11.9 %collective-permute-start = (bf16[64,2176]{1,0:T(8,128)(2,1)}, bf16[64,2176]{1,0:T(8,128)(2,1)S(1)}, u32[]{:S(2)}, u32[]{:S(2)}) collective-permute-start(bf16[64,2176]{1,0:T(8,128)(2,1)} %shard_map.85.packed), channel_id=1, source_target_pairs={{0,1},{1,0},{2,3},{3,2},{4,5},{5,4},{6,7},{7,6},{8,9},{9,8},{10,11... | collective-permute-start | bytes 835592 | tf_op jit(solution)/shard_map/ppermute | solution.py:27
  7.0 7.3 %copy-start = (bf16[64,2176]{1,0:T(8,128)(2,1)S(1)}, bf16[64,2176]{1,0:T(8,128)(2,1)}, u32[]{:S(2)}) copy-start(bf16[64,2176]{1,0:T(8,128)(2,1)} %shard_map.85.packed) | copy-start | bytes 835588
  7.3 14.2 %collective-permute-start.7 = (bf16[2048,128]{1,0:T(8,128)(2,1)S(1)}, bf16[2048,128]{1,0:T(8,128)(2,1)S(1)}, u32[]{:S(2)}, u32[]{:S(2)}) collective-permute-start(bf16[2048,128]{1,0:T(8,128)(2,1)S(1)} %broadcast_multiply_fusion.mb), channel_id=1, source_target_pairs={{0,126},{1,127},{2,0},{3,1},{4,2},{5,3},{6,4},{7,5},{8,6},{9,7},{1... | collective-permute-start | bytes 1572872 | tf_op jit(solution)/shard_map/ppermute | solution.py:27
  12.9 14.3 %collective-permute-start.5 = (bf16[2048,128]{1,0:T(8,128)(2,1)S(1)}, bf16[2048,128]{1,0:T(8,128)(2,1)S(1)}, u32[]{:S(2)}, u32[]{:S(2)}) collective-permute-start(bf16[2048,128]{1,0:T(8,128)(2,1)S(1)} %broadcast_multiply_fusion.mb), channel_id=1, source_target_pairs={{0,2},{1,3},{2,4},{3,5},{4,6},{5,7},{6,8},{7,9},{8,10},{9,11},{10,... | collective-permute-start | bytes 1572872 | tf_op jit(solution)/shard_map/ppermute | solution.py:27
  13.6 0.7 copy-start.5
  14.6 0.6 copy-start.1
  15.2 13.8 %collective-permute-start.8 = (bf16[128,2048]{1,0:T(8,128)(2,1)S(1)}, bf16[128,2048]{1,0:T(8,128)(2,1)}, u32[]{:S(2)}, u32[]{:S(2)}) collective-permute-start(bf16[128,2048]{1,0:T(8,128)(2,1)S(1)} %get-tuple-element.36.sb), channel_id=1, source_target_pairs={{0,126},{1,127},{2,0},{3,1},{4,2},{5,3},{6,4},{7,5},{8,6},{9,7},{1... | collective-permute-start | bytes 1572872 | tf_op jit(solution)/shard_map/ppermute | solution.py:27
  21.1 15.0 %collective-permute-start.6 = (bf16[128,2048]{1,0:T(8,128)(2,1)S(1)}, bf16[128,2048]{1,0:T(8,128)(2,1)S(1)}, u32[]{:S(2)}, u32[]{:S(2)}) collective-permute-start(bf16[128,2048]{1,0:T(8,128)(2,1)S(1)} %get-tuple-element.36.sb), channel_id=1, source_target_pairs={{0,2},{1,3},{2,4},{3,5},{4,6},{5,7},{6,8},{7,9},{8,10},{9,11},{10,... | collective-permute-start | bytes 1572872 | tf_op jit(solution)/shard_map/ppermute | solution.py:27
  21.1 19.9 %collective-permute-start.3 = (bf16[2048,128]{1,0:T(8,128)(2,1)S(1)}, bf16[2048,128]{1,0:T(8,128)(2,1)S(1)}, u32[]{:S(2)}, u32[]{:S(2)}) collective-permute-start(bf16[2048,128]{1,0:T(8,128)(2,1)S(1)} %broadcast_multiply_fusion.mb), channel_id=1, source_target_pairs={{0,124},{1,125},{2,126},{3,127},{4,0},{5,1},{6,2},{7,3},{8,4},{9,5... | collective-permute-start | bytes 1572872 | tf_op jit(solution)/shard_map/ppermute | solution.py:27
  21.5 0.8 copy-start.2
  21.6 28.7 %collective-permute-start.4 = (bf16[128,2048]{1,0:T(8,128)(2,1)S(1)}, bf16[128,2048]{1,0:T(8,128)(2,1)S(1)}, u32[]{:S(2)}, u32[]{:S(2)}) collective-permute-start(bf16[128,2048]{1,0:T(8,128)(2,1)S(1)} %get-tuple-element.36.sb), channel_id=1, source_target_pairs={{0,124},{1,125},{2,126},{3,127},{4,0},{5,1},{6,2},{7,3},{8,4},{9,5... | collective-permute-start | bytes 1572872 | tf_op jit(solution)/shard_map/ppermute | solution.py:27
  27.2 28.1 %collective-permute-start.1 = (bf16[2048,128]{1,0:T(8,128)(2,1)S(1)}, bf16[2048,128]{1,0:T(8,128)(2,1)S(1)}, u32[]{:S(2)}, u32[]{:S(2)}) collective-permute-start(bf16[2048,128]{1,0:T(8,128)(2,1)S(1)} %broadcast_multiply_fusion.mb), channel_id=1, source_target_pairs={{0,4},{1,5},{2,6},{3,7},{4,8},{5,9},{6,10},{7,11},{8,12},{9,13},{1... | collective-permute-start | bytes 1572872 | tf_op jit(solution)/shard_map/ppermute | solution.py:27
  28.9 26.4 %collective-permute-start.2 = (bf16[128,2048]{1,0:T(8,128)(2,1)S(1)}, bf16[128,2048]{1,0:T(8,128)(2,1)S(1)}, u32[]{:S(2)}, u32[]{:S(2)}) collective-permute-start(bf16[128,2048]{1,0:T(8,128)(2,1)S(1)} %get-tuple-element.36.sb), channel_id=1, source_target_pairs={{0,4},{1,5},{2,6},{3,7},{4,8},{5,9},{6,10},{7,11},{8,12},{9,13},{1... | collective-permute-start | bytes 1572872 | tf_op jit(solution)/shard_map/ppermute | solution.py:27
  60.5 5.5 %collective-permute-start.10 = (f32[72,128]{1,0:T(8,128)S(1)}, f32[72,128]{1,0:T(8,128)S(1)}, u32[]{:S(2)}, u32[]{:S(2)}) collective-permute-start(f32[72,128]{1,0:T(8,128)S(1)} %get-tuple-element.54), channel_id=1, source_target_pairs={{0,1},{1,0},{2,3},{3,2},{4,5},{5,4},{6,7},{7,6},{8,9},{9,8},{10,11... | collective-permute-start | bytes 110600 | tf_op jit(solution)/shard_map/ppermute | solution.py:27
  66.1 1.8 %collective-permute-start.11 = (f32[72,128]{1,0:T(8,128)S(1)}, f32[72,128]{1,0:T(8,128)S(1)}, u32[]{:S(2)}, u32[]{:S(2)}) collective-permute-start(f32[72,128]{1,0:T(8,128)S(1)} %add.37), channel_id=1, source_target_pairs={{0,2},{1,3},{2,0},{3,1},{4,6},{5,7},{6,4},{7,5},{8,10},{9,11},{10,... | collective-permute-start | bytes 110600 | tf_op jit(solution)/shard_map/ppermute | solution.py:27
  67.9 4.0 %collective-permute-start.12 = (f32[72,128]{1,0:T(8,128)S(1)}, f32[72,128]{1,0:T(8,128)S(1)}, u32[]{:S(2)}, u32[]{:S(2)}) collective-permute-start(f32[72,128]{1,0:T(8,128)S(1)} %add.38), channel_id=1, source_target_pairs={{0,4},{1,5},{2,6},{3,7},{4,0},{5,1},{6,2},{7,3},{8,12},{9,13},{10,... | collective-permute-start | bytes 110600 | tf_op jit(solution)/shard_map/ppermute | solution.py:27
  67.9 20.2 %collective-permute-start.9 = (bf16[64,1024]{1,0:T(8,128)(2,1)S(1)}, bf16[64,1024]{1,0:T(8,128)(2,1)S(1)}, u32[]{:S(2)}, u32[]{:S(2)}) collective-permute-start(bf16[64,1024]{1,0:T(8,128)(2,1)S(1)} %get-tuple-element.52), channel_id=1, source_target_pairs={{0,1},{1,0},{2,3},{3,2},{4,5},{5,4},{6,7},{7,6},{8,9},{9,8},{10,11... | collective-permute-start | bytes 393224 | tf_op jit(solution)/shard_map/ppermute | solution.py:27
  71.8 5.5 %collective-permute-start.13 = (f32[72,128]{1,0:T(8,128)S(1)}, f32[72,128]{1,0:T(8,128)S(1)}, u32[]{:S(2)}, u32[]{:S(2)}) collective-permute-start(f32[72,128]{1,0:T(8,128)S(1)} %add.39), channel_id=1, source_target_pairs={{0,8},{1,9},{2,10},{3,11},{4,12},{5,13},{6,14},{7,15},{8,0},{9,1},... | collective-permute-start | bytes 110600 | tf_op jit(solution)/shard_map/ppermute | solution.py:27
  77.3 4.0 %collective-permute-start.14 = (f32[72,128]{1,0:T(8,128)S(1)}, f32[72,128]{1,0:T(8,128)S(1)}, u32[]{:S(2)}, u32[]{:S(2)}) collective-permute-start(f32[72,128]{1,0:T(8,128)S(1)} %add.40), channel_id=1, source_target_pairs={{0,16},{1,17},{2,18},{3,19},{4,20},{5,21},{6,22},{7,23},{8,24},{9,... | collective-permute-start | bytes 110600 | tf_op jit(solution)/shard_map/ppermute | solution.py:27
  81.3 5.5 %collective-permute-start.15 = (f32[72,128]{1,0:T(8,128)S(1)}, f32[72,128]{1,0:T(8,128)S(1)}, u32[]{:S(2)}, u32[]{:S(2)}) collective-permute-start(f32[72,128]{1,0:T(8,128)S(1)} %add.41), channel_id=1, source_target_pairs={{0,32},{1,33},{2,34},{3,35},{4,36},{5,37},{6,38},{7,39},{8,40},{9,... | collective-permute-start | bytes 110600 | tf_op jit(solution)/shard_map/ppermute | solution.py:27
  86.7 4.0 %collective-permute-start.16 = (f32[72,128]{1,0:T(8,128)S(1)}, f32[72,128]{1,0:T(8,128)S(1)}, u32[]{:S(2)}, u32[]{:S(2)}) collective-permute-start(f32[72,128]{1,0:T(8,128)S(1)} %add.42), channel_id=1, source_target_pairs={{0,64},{1,65},{2,66},{3,67},{4,68},{5,69},{6,70},{7,71},{8,72},{9,... | collective-permute-start | bytes 110600 | tf_op jit(solution)/shard_map/ppermute | solution.py:27

commit v4 on v3

--- a/solution.py
+++ b/solution.py
@@ -226,10 +226,20 @@
         in_specs=[vmem] * 2,
         out_specs=vmem,
     )(cotangent.T, weight_h.T)
+    packed, inputs = lax.optimization_barrier((packed, inputs))
     arrived = moved(packed, other_feat)
     masked = inputs * live.astype(BF16)[:, None]
-    offsets = [1, -1, 2, -2][: 2 * WINDOW]
-    masked_far = [moved(masked, lambda b, f, d=d: (b - d, f)) for d in offsets]
+    partner = lambda b, f: (b ^ 1, f)
+
+    def spread_out(x):
+        steps = (partner, lambda b, f: (b - 2, f), lambda b, f: (b + 2, f))
+        return [moved(x, step) for step in steps]
+
+    def passed_on(after, before):
+        return moved(jnp.where(position % 2 == 0, after, before), partner)
+
+    masked_far = spread_out(masked)
+    masked_far.append(passed_on(*masked_far[1:]))
     ws_t = jnp.zeros((8, depth), BF16).at[:dims].set(weight_s.T)
     shapes = [(feats, hits), (feats, rows), (depth, feats), (feats, depth), (depth, feats)]
     scaled, sa, w, w_t, w_turned, ws_turned = pl.pallas_call(
@@ -250,19 +260,22 @@
         jax.ShapeDtypeStruct((rows, 64), BF16),
         jax.ShapeDtypeStruct((rows, 2 * feats), BF16),
     ]
-    scaled_far = [moved(scaled, lambda b, f, d=d: (b - d, f)) for d in offsets]
+    scaled_far = spread_out(scaled)
     oh, oc, near_dist, near_mix = call(
         first_body, (ma, sa, masked, scaled, w, w_t, ws_t), sums + near, hits, feats
     )
-    for mb, sb in list(zip(masked_far, scaled_far))[:-1]:
+    for i in range(3):
         oh, oc = call(
             next_body,
-            (near_dist, near_mix, mb, sb, w_t, ws_t, oh, oc),
+            (near_dist, near_mix, masked_far[i], scaled_far[i], w_t, ws_t, oh, oc),
             sums,
             hits,
             feats,
             input_output_aliases={6: 0, 7: 1},
         )
+        if i == 0:
+            oh, oc, *scaled_far[1:] = lax.optimization_barrier((oh, oc, *scaled_far[1:]))
+            scaled_far.append(passed_on(*scaled_far[1:]))
     own, other, mine, theirs = call(
         last_body,
         (near_dist, near_mix, masked_far[-1], scaled_far[-1], w_t, ws_t, oh, oc)

time: 92.2 us -> 110 us (1.19); the launches traced: 91.9 us -> 108 us
  starting transfers between devices: 27.2 us -> 42.8 us
  waiting for transfers between devices: 29.8 us -> 32 us
  local copies, waits for them, and re-layouts: 3.14 us -> 1.92 us
    ppermute x17, starting transfers between devices: 27.2 us -> 42.8 us  [moved(): return lax.ppermute(x, ('blk', 'feat'), route)]
    ppermute x17, waiting for transfers between devices: 29.8 us -> 32 us  [moved(): return lax.ppermute(x, ('blk', 'feat'), route)]
    unnamed x14 -> x10, local copies, waits for them, and re-layouts: 1.91 us -> 0.69 us
  transfers between devices with their start and end apart: 17 -> 17, of which waited for: 8 -> 10; matrix products, arithmetic and copies ran while one was open for 3% -> 1% of each run, Pallas kernels for 23% -> 18%
where the time goes in v4:
time: 110 us; the launch traced here: 108 us
  starting transfers between devices  42.8 us (39%)
  waiting for transfers between devices  32 us (29%)
  Pallas kernels  27.1 us (25%)
  other arithmetic  2.57 us (2%)
  local copies, waits for them, and re-layouts  1.92 us (2%)
  between operations  1.57 us (1%)
    ppermute x17, starting transfers between devices, moved(): return lax.ppermute(x, ('blk', 'feat'), route)  42.8 us
    ppermute x17, waiting for transfers between devices, moved(): return lax.ppermute(x, ('blk', 'feat'), route)  32 us
    pallas_call x5, Pallas kernels, call(): pl.pallas_call(body, out_shape=outs, in_specs=[vmem] * len(operands), out...  25.2 us
  transfers between devices with their start and end apart: 17, of which 10 were waited for; matrix products, arithmetic and copies ran while one was open for 1% of the time, Pallas kernels for 18%

profile of v4, /device:TPU:0, one launch (start us, length us, event | category | flops | bytes accessed | tf_op | source)
XLA Modules:
  0.0 108.0 jit_solution(5139435003892344842)
XLA Ops:
  0.7 1.7 %shard_map.85.packed = bf16[64,2176]{1,0:T(8,128)(2,1)} custom-call(bf16[64,2048]{1,0:T(8,128)(2,1)} %bitcast.14, bf16[64,128]{1,0:T(8,128)(2,1)} %bitcast.15), custom_call_target="tpu_custom_call" | custom-call | tf_op jit(solution)/shard_map/pallas_call | solution.py:223
  2.4 0.6 fusion.3
  3.1 0.6 fusion.4
  3.7 0.3 broadcast_multiply_fusion.mb
  4.1 0.1 collective-permute-start.4
  4.2 7.4 %collective-permute-start.1 = (bf16[2048,128]{1,0:T(8,128)(2,1)S(1)}, bf16[2048,128]{1,0:T(8,128)(2,1)S(1)}, u32[]{:S(2)}, u32[]{:S(2)}) collective-permute-start(bf16[2048,128]{1,0:T(8,128)(2,1)S(1)} %broadcast_multiply_fusion.mb), channel_id=1, source_target_pairs={{0,124},{1,125},{2,126},{3,127},{4,0},{5,1},{6,2},{7,3},{8,4},{9,5... | collective-permute-start | bytes 1572872 | tf_op jit(solution)/shard_map/ppermute | solution.py:27
  11.6 0.0 collective-permute-start.2
  11.6 2.9 %collective-permute-start = (bf16[64,2176]{1,0:T(8,128)(2,1)S(1)}, bf16[64,2176]{1,0:T(8,128)(2,1)S(1)}, u32[]{:S(2)}, u32[]{:S(2)}) collective-permute-start(bf16[64,2176]{1,0:T(8,128)(2,1)S(1)} %copy-done), channel_id=1, source_target_pairs={{0,1},{1,0},{2,3},{3,2},{4,5},{5,4},{6,7},{7,6},{8,9},{9,8},{10,11... | collective-permute-start | bytes 835592 | tf_op jit(solution)/shard_map/ppermute | solution.py:27
  15.2 0.0 copy-start.3
  15.2 0.7 copy-done.3
  15.9 5.9 %collective-permute-done.arrived = bf16[64,2176]{1,0:T(8,128)(2,1)S(1)} collective-permute-done((bf16[64,2176]{1,0:T(8,128)(2,1)S(1)}, bf16[64,2176]{1,0:T(8,128)(2,1)S(1)}, u32[]{:S(2)}, u32[]{:S(2)}) %collective-permute-start) | collective-permute-done | bytes 278560 | tf_op jit(solution)/shard_map/ppermute | solution.py:27
  21.8 0.2 shard_map.86
  22.0 0.1 collective-permute-start.5
  22.1 6.0 %collective-permute-start.6 = (bf16[128,2048]{1,0:T(8,128)(2,1)S(1)}, bf16[128,2048]{1,0:T(8,128)(2,1)S(1)}, u32[]{:S(2)}, u32[]{:S(2)}) collective-permute-start(bf16[128,2048]{1,0:T(8,128)(2,1)S(1)} %get-tuple-element.44.sb), channel_id=1, source_target_pairs={{0,124},{1,125},{2,126},{3,127},{4,0},{5,1},{6,2},{7,3},{8,4},{9,5... | collective-permute-start | bytes 1572872 | tf_op jit(solution)/shard_map/ppermute | solution.py:27
  28.2 5.0 %shard_map.87 = (f32[1024,128]{1,0:T(8,128)S(1)}, f32[1024,32]{1,0:T(8,128)S(1)}, bf16[1024,64]{1,0:T(8,128)(2,1)S(1)}, bf16[1024,256]{1,0:T(8,128)(2,1)S(1)}) custom-call(bf16[1024,128]{1,0:T(8,128)(2,1)S(1)} %constant_dynamic-slice_fusion.ma, bf16[128,1024]{1,0:T(8,128)(2,1)S(1)} %get-tuple-element.43.sa, bf16[2048,128]{1,0:T(8,128)(2,1)S(1)} %broadcast_multiply_fusion.mb, ...), custom_call_target="tpu_custom_call" | custom-call | flops 2147483648 | bytes 1048576 | tf_op jit(solution)/shard_map/pallas_call | solution.py:185
  33.2 0.0 collective-permute-done.1.mb
  33.2 0.1 collective-permute-start.7
  33.3 0.0 collective-permute-done.2.mb
  33.3 0.1 broadcast_select_fusion.1
  33.3 0.4 collective-permute-start.3
  33.8 0.0 collective-permute-done.4.mb
  33.8 4.9 %shard_map.88 = (f32[1024,128]{1,0:T(8,128)S(1)}, f32[1024,32]{1,0:T(8,128)S(1)}) custom-call(bf16[1024,64]{1,0:T(8,128)(2,1)S(1)} %get-tuple-element.47.near_dist, bf16[1024,256]{1,0:T(8,128)(2,1)S(1)} %get-tuple-element.48.near_mix, bf16[2048,128]{1,0:T(8,128)(2,1)S(1)} %collective-permute-done.4.mb, ...), custom_call_target="tpu_custom_call", output_to_operand_aliasing={{0}: (6, {}), {1}: (7, {})} | custom-call | flops 2147483648 | bytes 1048576 | tf_op jit(solution)/shard_map/pallas_call | solution.py:185
  38.6 1.3 %collective-permute-done.6.sb = bf16[128,2048]{1,0:T(8,128)(2,1)S(1)} collective-permute-done((bf16[128,2048]{1,0:T(8,128)(2,1)S(1)}, bf16[128,2048]{1,0:T(8,128)(2,1)S(1)}, u32[]{:S(2)}, u32[]{:S(2)}) %collective-permute-start.6) | collective-permute-done | bytes 524320 | tf_op jit(solution)/shard_map/ppermute | solution.py:27
  40.0 11.5 %collective-permute-done.7.sb = bf16[128,2048]{1,0:T(8,128)(2,1)S(1)} collective-permute-done((bf16[128,2048]{1,0:T(8,128)(2,1)S(1)}, bf16[128,2048]{1,0:T(8,128)(2,1)S(1)}, u32[]{:S(2)}, u32[]{:S(2)}) %collective-permute-start.7) | collective-permute-done | bytes 524320 | tf_op jit(solution)/shard_map/ppermute | solution.py:27
  51.5 0.1 broadcast_select_fusion
  51.5 0.1 collective-permute-start.8
  51.6 4.9 %shard_map.89 = (f32[1024,128]{1,0:T(8,128)S(1)}, f32[1024,32]{1,0:T(8,128)S(1)}) custom-call(bf16[1024,64]{1,0:T(8,128)(2,1)S(1)} %get-tuple-element.47.near_dist, bf16[1024,256]{1,0:T(8,128)(2,1)S(1)} %get-tuple-element.48.near_mix, bf16[2048,128]{1,0:T(8,128)(2,1)S(1)} %collective-permute-done.1.mb, ...), custom_call_target="tpu_custom_call", output_to_operand_aliasing={{0}: (6, {}), {1}: (7, {})} | custom-call | flops 2147483648 | bytes 1048576 | tf_op jit(solution)/shard_map/pallas_call | solution.py:185
  56.5 4.9 %shard_map.90 = (f32[1024,128]{1,0:T(8,128)S(1)}, f32[1024,32]{1,0:T(8,128)S(1)}) custom-call(bf16[1024,64]{1,0:T(8,128)(2,1)S(1)} %get-tuple-element.47.near_dist, bf16[1024,256]{1,0:T(8,128)(2,1)S(1)} %get-tuple-element.48.near_mix, bf16[2048,128]{1,0:T(8,128)(2,1)S(1)} %collective-permute-done.2.mb, ...), custom_call_target="tpu_custom_call", output_to_operand_aliasing={{0}: (6, {}), {1}: (7, {})} | custom-call | flops 2147483648 | bytes 1048576 | tf_op jit(solution)/shard_map/pallas_call | solution.py:185
  61.4 0.0 collective-permute-done.8.sb
  61.4 5.5 %shard_map.91 = (f32[72,128]{1,0:T(8,128)S(1)}, f32[72,128]{1,0:T(8,128)S(1)}, bf16[64,1024]{1,0:T(8,128)(2,1)S(1)}, bf16[64,1024]{1,0:T(8,128)(2,1)S(1)}) custom-call(bf16[1024,64]{1,0:T(8,128)(2,1)S(1)} %get-tuple-element.47.near_dist, bf16[1024,256]{1,0:T(8,128)(2,1)S(1)} %get-tuple-element.48.near_mix, bf16[2048,128]{1,0:T(8,128)(2,1)S(1)} %collective-permute-done.3.mb, ...), custom_call_target="tpu_custom_call" | custom-call | flops 2147483648 | bytes 1048576 | tf_op jit(solution)/shard_map/pallas_call | solution.py:185
  67.0 3.0 %collective-permute-start.10 = (f32[72,128]{1,0:T(8,128)S(1)}, f32[72,128]{1,0:T(8,128)S(1)}, u32[]{:S(2)}, u32[]{:S(2)}) collective-permute-start(f32[72,128]{1,0:T(8,128)S(1)} %get-tuple-element.66), channel_id=1, source_target_pairs={{0,1},{1,0},{2,3},{3,2},{4,5},{5,4},{6,7},{7,6},{8,9},{9,8},{10,11... | collective-permute-start | bytes 110600 | tf_op jit(solution)/shard_map/ppermute | solution.py:27
  70.0 2.6 %collective-permute-done.10 = f32[72,128]{1,0:T(8,128)S(1)} collective-permute-done((f32[72,128]{1,0:T(8,128)S(1)}, f32[72,128]{1,0:T(8,128)S(1)}, u32[]{:S(2)}, u32[]{:S(2)}) %collective-permute-start.10) | collective-permute-done | bytes 36896 | tf_op jit(solution)/shard_map/ppermute | solution.py:27
  72.5 0.0 collective-permute-start.11
  72.5 1.2 %collective-permute-done.11 = f32[72,128]{1,0:T(8,128)S(1)} collective-permute-done((f32[72,128]{1,0:T(8,128)S(1)}, f32[72,128]{1,0:T(8,128)S(1)}, u32[]{:S(2)}, u32[]{:S(2)}) %collective-permute-start.11) | collective-permute-done | bytes 36896 | tf_op jit(solution)/shard_map/ppermute | solution.py:27
  73.8 3.0 %collective-permute-start.9 = (bf16[64,1024]{1,0:T(8,128)(2,1)S(1)}, bf16[64,1024]{1,0:T(8,128)(2,1)S(1)}, u32[]{:S(2)}, u32[]{:S(2)}) collective-permute-start(bf16[64,1024]{1,0:T(8,128)(2,1)S(1)} %get-tuple-element.64), channel_id=1, source_target_pairs={{0,1},{1,0},{2,3},{3,2},{4,5},{5,4},{6,7},{7,6},{8,9},{9,8},{10,11... | collective-permute-start | bytes 393224 | tf_op jit(solution)/shard_map/ppermute | solution.py:27
  76.7 1.0 collective-permute-done.12
  77.7 4.1 %collective-permute-start.13 = (f32[72,128]{1,0:T(8,128)S(1)}, f32[72,128]{1,0:T(8,128)S(1)}, u32[]{:S(2)}, u32[]{:S(2)}) collective-permute-start(f32[72,128]{1,0:T(8,128)S(1)} %add.45), channel_id=1, source_target_pairs={{0,8},{1,9},{2,10},{3,11},{4,12},{5,13},{6,14},{7,15},{8,0},{9,1},... | collective-permute-start | bytes 110600 | tf_op jit(solution)/shard_map/ppermute | solution.py:27
  81.8 1.9 %collective-permute-done.13 = f32[72,128]{1,0:T(8,128)S(1)} collective-permute-done((f32[72,128]{1,0:T(8,128)S(1)}, f32[72,128]{1,0:T(8,128)S(1)}, u32[]{:S(2)}, u32[]{:S(2)}) %collective-permute-start.13) | collective-permute-done | bytes 36896 | tf_op jit(solution)/shard_map/ppermute | solution.py:27
  83.8 4.7 %collective-permute-start.14 = (f32[72,128]{1,0:T(8,128)S(1)}, f32[72,128]{1,0:T(8,128)S(1)}, u32[]{:S(2)}, u32[]{:S(2)}) collective-permute-start(f32[72,128]{1,0:T(8,128)S(1)} %add.46), channel_id=1, source_target_pairs={{0,16},{1,17},{2,18},{3,19},{4,20},{5,21},{6,22},{7,23},{8,24},{9,... | collective-permute-start | bytes 110600 | tf_op jit(solution)/shard_map/ppermute | solution.py:27
  88.5 1.9 %collective-permute-done.14 = f32[72,128]{1,0:T(8,128)S(1)} collective-permute-done((f32[72,128]{1,0:T(8,128)S(1)}, f32[72,128]{1,0:T(8,128)S(1)}, u32[]{:S(2)}, u32[]{:S(2)}) %collective-permute-start.14) | collective-permute-done | bytes 36896 | tf_op jit(solution)/shard_map/ppermute | solution.py:27
  90.4 10.5 %collective-permute-start.15 = (f32[72,128]{1,0:T(8,128)S(1)}, f32[72,128]{1,0:T(8,128)S(1)}, u32[]{:S(2)}, u32[]{:S(2)}) collective-permute-start(f32[72,128]{1,0:T(8,128)S(1)} %add.47), channel_id=1, source_target_pairs={{0,32},{1,33},{2,34},{3,35},{4,36},{5,37},{6,38},{7,39},{8,40},{9,... | collective-permute-start | bytes 110600 | tf_op jit(solution)/shard_map/ppermute | solution.py:27
  100.9 1.9 %collective-permute-done.15 = f32[72,128]{1,0:T(8,128)S(1)} collective-permute-done((f32[72,128]{1,0:T(8,128)S(1)}, f32[72,128]{1,0:T(8,128)S(1)}, u32[]{:S(2)}, u32[]{:S(2)}) %collective-permute-start.15) | collective-permute-done | bytes 36896 | tf_op jit(solution)/shard_map/ppermute | solution.py:27
  102.8 0.5 collective-permute-start.16
  103.3 0.0 collective-permute-done.9
  103.3 0.8 fusion
  104.1 2.7 %collective-permute-done.16 = f32[72,128]{1,0:T(8,128)S(1)} collective-permute-done((f32[72,128]{1,0:T(8,128)S(1)}, f32[72,128]{1,0:T(8,128)S(1)}, u32[]{:S(2)}, u32[]{:S(2)}) %collective-permute-start.16) | collective-permute-done | bytes 36896 | tf_op jit(solution)/shard_map/ppermute | solution.py:27
  106.8 0.6 slice_bitcast_fusion
  107.4 0.6 slice_bitcast_fusion.1
  (23 shorter events, 0.1 us)
Async XLA Ops:
  0.6 3.1 %copy-start.1 = (bf16[2048,128]{1,0:T(8,128)(2,1)S(1)}, bf16[2048,128]{1,0:T(8,128)(2,1)}, u32[]{:S(2)}) copy-start(bf16[2048,128]{1,0:T(8,128)(2,1)} %param.8) | copy-start | bytes 1572868
  0.6 1.8 %copy-start.4 = (s32[64]{0:T(128)S(1)}, s32[64]{0:T(128)}, u32[]{:S(2)}) copy-start(s32[64]{0:T(128)} %param.13) | copy-start | bytes 772
  0.7 2.4 %copy-start.2 = (s32[2048]{0:T(1024)S(1)}, s32[2048]{0:T(1024)}, u32[]{:S(2)}) copy-start(s32[2048]{0:T(1024)} %param.12) | copy-start | bytes 24580
  3.7 7.8 %copy-start = (bf16[64,2176]{1,0:T(8,128)(2,1)S(1)}, bf16[64,2176]{1,0:T(8,128)(2,1)}, u32[]{:S(2)}) copy-start(bf16[64,2176]{1,0:T(8,128)(2,1)} %shard_map.85.packed) | copy-start | bytes 835588
  4.1 29.7 %collective-permute-start.4 = (bf16[2048,128]{1,0:T(8,128)(2,1)S(1)}, bf16[2048,128]{1,0:T(8,128)(2,1)S(1)}, u32[]{:S(2)}, u32[]{:S(2)}) collective-permute-start(bf16[2048,128]{1,0:T(8,128)(2,1)S(1)} %broadcast_multiply_fusion.mb), channel_id=1, source_target_pairs={{0,2},{1,3},{2,0},{3,1},{4,6},{5,7},{6,4},{7,5},{8,10},{9,11},{10,... | collective-permute-start | bytes 1572872 | tf_op jit(solution)/shard_map/ppermute | solution.py:27
  4.2 29.0 %collective-permute-start.1 = (bf16[2048,128]{1,0:T(8,128)(2,1)S(1)}, bf16[2048,128]{1,0:T(8,128)(2,1)S(1)}, u32[]{:S(2)}, u32[]{:S(2)}) collective-permute-start(bf16[2048,128]{1,0:T(8,128)(2,1)S(1)} %broadcast_multiply_fusion.mb), channel_id=1, source_target_pairs={{0,124},{1,125},{2,126},{3,127},{4,0},{5,1},{6,2},{7,3},{8,4},{9,5... | collective-permute-start | bytes 1572872 | tf_op jit(solution)/shard_map/ppermute | solution.py:27
  11.6 21.7 %collective-permute-start.2 = (bf16[2048,128]{1,0:T(8,128)(2,1)S(1)}, bf16[2048,128]{1,0:T(8,128)(2,1)S(1)}, u32[]{:S(2)}, u32[]{:S(2)}) collective-permute-start(bf16[2048,128]{1,0:T(8,128)(2,1)S(1)} %broadcast_multiply_fusion.mb), channel_id=1, source_target_pairs={{0,4},{1,5},{2,6},{3,7},{4,8},{5,9},{6,10},{7,11},{8,12},{9,13},{1... | collective-permute-start | bytes 1572872 | tf_op jit(solution)/shard_map/ppermute | solution.py:27
  11.6 10.2 %collective-permute-start = (bf16[64,2176]{1,0:T(8,128)(2,1)S(1)}, bf16[64,2176]{1,0:T(8,128)(2,1)S(1)}, u32[]{:S(2)}, u32[]{:S(2)}) collective-permute-start(bf16[64,2176]{1,0:T(8,128)(2,1)S(1)} %copy-done), channel_id=1, source_target_pairs={{0,1},{1,0},{2,3},{3,2},{4,5},{5,4},{6,7},{7,6},{8,9},{9,8},{10,11... | collective-permute-start | bytes 835592 | tf_op jit(solution)/shard_map/ppermute | solution.py:27
  15.2 0.7 copy-start.3
  22.0 11.7 %collective-permute-start.5 = (bf16[128,2048]{1,0:T(8,128)(2,1)S(1)}, bf16[128,2048]{1,0:T(8,128)(2,1)S(1)}, u32[]{:S(2)}, u32[]{:S(2)}) collective-permute-start(bf16[128,2048]{1,0:T(8,128)(2,1)S(1)} %get-tuple-element.44.sb), channel_id=1, source_target_pairs={{0,2},{1,3},{2,0},{3,1},{4,6},{5,7},{6,4},{7,5},{8,10},{9,11},{10,... | collective-permute-start | bytes 1572872 | tf_op jit(solution)/shard_map/ppermute | solution.py:27
  22.1 17.9 %collective-permute-start.6 = (bf16[128,2048]{1,0:T(8,128)(2,1)S(1)}, bf16[128,2048]{1,0:T(8,128)(2,1)S(1)}, u32[]{:S(2)}, u32[]{:S(2)}) collective-permute-start(bf16[128,2048]{1,0:T(8,128)(2,1)S(1)} %get-tuple-element.44.sb), channel_id=1, source_target_pairs={{0,124},{1,125},{2,126},{3,127},{4,0},{5,1},{6,2},{7,3},{8,4},{9,5... | collective-permute-start | bytes 1572872 | tf_op jit(solution)/shard_map/ppermute | solution.py:27
  33.2 18.3 %collective-permute-start.7 = (bf16[128,2048]{1,0:T(8,128)(2,1)S(1)}, bf16[128,2048]{1,0:T(8,128)(2,1)S(1)}, u32[]{:S(2)}, u32[]{:S(2)}) collective-permute-start(bf16[128,2048]{1,0:T(8,128)(2,1)S(1)} %get-tuple-element.44.sb), channel_id=1, source_target_pairs={{0,4},{1,5},{2,6},{3,7},{4,8},{5,9},{6,10},{7,11},{8,12},{9,13},{1... | collective-permute-start | bytes 1572872 | tf_op jit(solution)/shard_map/ppermute | solution.py:27
  33.3 28.1 %collective-permute-start.3 = (bf16[2048,128]{1,0:T(8,128)(2,1)S(1)}, bf16[2048,128]{1,0:T(8,128)(2,1)S(1)}, u32[]{:S(2)}, u32[]{:S(2)}) collective-permute-start(bf16[2048,128]{1,0:T(8,128)(2,1)S(1)} %broadcast_select_fusion.1), channel_id=1, source_target_pairs={{0,2},{1,3},{2,0},{3,1},{4,6},{5,7},{6,4},{7,5},{8,10},{9,11},{10,... | collective-permute-start | bytes 1572872 | tf_op jit(solution)/shard_map/ppermute | solution.py:27
  51.5 9.9 %collective-permute-start.8 = (bf16[128,2048]{1,0:T(8,128)(2,1)S(1)}, bf16[128,2048]{1,0:T(8,128)(2,1)S(1)}, u32[]{:S(2)}, u32[]{:S(2)}) collective-permute-start(bf16[128,2048]{1,0:T(8,128)(2,1)S(1)} %broadcast_select_fusion), channel_id=1, source_target_pairs={{0,2},{1,3},{2,0},{3,1},{4,6},{5,7},{6,4},{7,5},{8,10},{9,11},{10,... | collective-permute-start | bytes 1572872 | tf_op jit(solution)/shard_map/ppermute | solution.py:27
  67.0 5.5 %collective-permute-start.10 = (f32[72,128]{1,0:T(8,128)S(1)}, f32[72,128]{1,0:T(8,128)S(1)}, u32[]{:S(2)}, u32[]{:S(2)}) collective-permute-start(f32[72,128]{1,0:T(8,128)S(1)} %get-tuple-element.66), channel_id=1, source_target_pairs={{0,1},{1,0},{2,3},{3,2},{4,5},{5,4},{6,7},{7,6},{8,9},{9,8},{10,11... | collective-permute-start | bytes 110600 | tf_op jit(solution)/shard_map/ppermute | solution.py:27
  72.5 1.2 %collective-permute-start.11 = (f32[72,128]{1,0:T(8,128)S(1)}, f32[72,128]{1,0:T(8,128)S(1)}, u32[]{:S(2)}, u32[]{:S(2)}) collective-permute-start(f32[72,128]{1,0:T(8,128)S(1)} %add.43), channel_id=1, source_target_pairs={{0,2},{1,3},{2,0},{3,1},{4,6},{5,7},{6,4},{7,5},{8,10},{9,11},{10,... | collective-permute-start | bytes 110600 | tf_op jit(solution)/shard_map/ppermute | solution.py:27
  73.7 4.0 %collective-permute-start.12 = (f32[72,128]{1,0:T(8,128)S(1)}, f32[72,128]{1,0:T(8,128)S(1)}, u32[]{:S(2)}, u32[]{:S(2)}) collective-permute-start(f32[72,128]{1,0:T(8,128)S(1)} %add.44), channel_id=1, source_target_pairs={{0,4},{1,5},{2,6},{3,7},{4,0},{5,1},{6,2},{7,3},{8,12},{9,13},{10,... | collective-permute-start | bytes 110600 | tf_op jit(solution)/shard_map/ppermute | solution.py:27
  73.8 29.5 %collective-permute-start.9 = (bf16[64,1024]{1,0:T(8,128)(2,1)S(1)}, bf16[64,1024]{1,0:T(8,128)(2,1)S(1)}, u32[]{:S(2)}, u32[]{:S(2)}) collective-permute-start(bf16[64,1024]{1,0:T(8,128)(2,1)S(1)} %get-tuple-element.64), channel_id=1, source_target_pairs={{0,1},{1,0},{2,3},{3,2},{4,5},{5,4},{6,7},{7,6},{8,9},{9,8},{10,11... | collective-permute-start | bytes 393224 | tf_op jit(solution)/shard_map/ppermute | solution.py:27
  77.7 6.1 %collective-permute-start.13 = (f32[72,128]{1,0:T(8,128)S(1)}, f32[72,128]{1,0:T(8,128)S(1)}, u32[]{:S(2)}, u32[]{:S(2)}) collective-permute-start(f32[72,128]{1,0:T(8,128)S(1)} %add.45), channel_id=1, source_target_pairs={{0,8},{1,9},{2,10},{3,11},{4,12},{5,13},{6,14},{7,15},{8,0},{9,1},... | collective-permute-start | bytes 110600 | tf_op jit(solution)/shard_map/ppermute | solution.py:27
  83.8 6.6 %collective-permute-start.14 = (f32[72,128]{1,0:T(8,128)S(1)}, f32[72,128]{1,0:T(8,128)S(1)}, u32[]{:S(2)}, u32[]{:S(2)}) collective-permute-start(f32[72,128]{1,0:T(8,128)S(1)} %add.46), channel_id=1, source_target_pairs={{0,16},{1,17},{2,18},{3,19},{4,20},{5,21},{6,22},{7,23},{8,24},{9,... | collective-permute-start | bytes 110600 | tf_op jit(solution)/shard_map/ppermute | solution.py:27
  90.4 12.4 %collective-permute-start.15 = (f32[72,128]{1,0:T(8,128)S(1)}, f32[72,128]{1,0:T(8,128)S(1)}, u32[]{:S(2)}, u32[]{:S(2)}) collective-permute-start(f32[72,128]{1,0:T(8,128)S(1)} %add.47), channel_id=1, source_target_pairs={{0,32},{1,33},{2,34},{3,35},{4,36},{5,37},{6,38},{7,39},{8,40},{9,... | collective-permute-start | bytes 110600 | tf_op jit(solution)/shard_map/ppermute | solution.py:27
  102.8 4.0 %collective-permute-start.16 = (f32[72,128]{1,0:T(8,128)S(1)}, f32[72,128]{1,0:T(8,128)S(1)}, u32[]{:S(2)}, u32[]{:S(2)}) collective-permute-start(f32[72,128]{1,0:T(8,128)S(1)} %add.48), channel_id=1, source_target_pairs={{0,64},{1,65},{2,66},{3,67},{4,68},{5,69},{6,70},{7,71},{8,72},{9,... | collective-permute-start | bytes 110600 | tf_op jit(solution)/shard_map/ppermute | solution.py:27

commit v5 on v3

--- a/solution.py
+++ b/solution.py
@@ -149,7 +149,7 @@
 
 def last_body(
     near_dist, near_mix, mb, sb, w_t, ws_t, ah, ac, ma, live, w_turned, ws_turned,
-    own, other, mine, theirs, dist_sc, mix_sc, mom_sc, oh, oc,
+    pair, mine, theirs, dist_sc, mix_sc, mom_sc, oh, oc,
 ):
     window_terms(
         near_dist, near_mix, mb, sb, w_t, ws_t, dist_sc, mix_sc, mom_sc, oh, oc, (ah, ac)
@@ -169,10 +169,10 @@
     )
     triple = jnp.dot(parts, ma[...], preferred_element_type=F32)
     part_s = triple[0:8] + triple[8:16] + triple[16:24]
-    own[:width, :] = part_h[:width]
-    own[width:, :] = part_s
-    other[:width, :] = part_h[width:]
-    other[width:, :] = part_s
+    for i in range(2):
+        top = i * (width + 8)
+        pair[top : top + width, :] = part_h[i * width : (i + 1) * width]
+        pair[top + width : top + width + 8, :] = part_s
     grad = lax.dot_general(w_turned[...], hidden_grad, NT, preferred_element_type=F32)
     grad = grad + jnp.dot(ws_turned[...], parts, preferred_element_type=F32)
     grad = (grad * live[...]).astype(BF16)
@@ -229,7 +229,7 @@
     arrived = moved(packed, other_feat)
     masked = inputs * live.astype(BF16)[:, None]
     offsets = [1, -1, 2, -2][: 2 * WINDOW]
-    masked_far = [moved(masked, lambda b, f, d=d: (b - d, f)) for d in offsets]
+    masked_far = [moved(masked, lambda b, f, d=d: (b - d, f)) for d in offsets[:2]]
     ws_t = jnp.zeros((8, depth), BF16).at[:dims].set(weight_s.T)
     shapes = [(feats, hits), (feats, rows), (depth, feats), (feats, depth), (depth, feats)]
     scaled, sa, w, w_t, w_turned, ws_turned = pl.pallas_call(
@@ -250,10 +250,14 @@
         jax.ShapeDtypeStruct((rows, 64), BF16),
         jax.ShapeDtypeStruct((rows, 2 * feats), BF16),
     ]
-    scaled_far = [moved(scaled, lambda b, f, d=d: (b - d, f)) for d in offsets]
+    scaled_far = [moved(scaled, lambda b, f, d=d: (b - d, f)) for d in offsets[:2]]
     oh, oc, near_dist, near_mix = call(
         first_body, (ma, sa, masked, scaled, w, w_t, ws_t), sums + near, hits, feats
     )
+    late_m, late_s, oh, oc = lax.optimization_barrier((masked, scaled, oh, oc))
+    for d in offsets[2:]:
+        masked_far.append(moved(late_m, lambda b, f, d=d: (b - d, f)))
+        scaled_far.append(moved(late_s, lambda b, f, d=d: (b - d, f)))
     for mb, sb in list(zip(masked_far, scaled_far))[:-1]:
         oh, oc = call(
             next_body,
@@ -263,20 +267,25 @@
             feats,
             input_output_aliases={6: 0, 7: 1},
         )
-    own, other, mine, theirs = call(
+    pair, mine, theirs = call(
         last_body,
         (near_dist, near_mix, masked_far[-1], scaled_far[-1], w_t, ws_t, oh, oc)
         + (ma, live_rows, w_turned, ws_turned),
-        [jax.ShapeDtypeStruct((width + 8, inputs.shape[1]), F32)] * 2
+        [jax.ShapeDtypeStruct((2 * (width + 8), inputs.shape[1]), F32)]
         + [jax.ShapeDtypeStruct((width, rows), BF16)] * 2,
         hits,
         feats,
         [pltpu.VMEM((rows, feats), F32), pltpu.VMEM((rows, 32), F32)],
     )
-    total = own + moved(other, other_feat)
+    far_half = block_total // 2
+    swap = lambda mask: lambda b, f: (b ^ mask, f)
+    pair = pair + moved(pair, swap(far_half))
+    high = width + 8
+    total = pair[:high] + moved(pair[high:], lambda b, f: (b ^ far_half, 1 - f))
     step = 1
-    while step < block_total:
-        total = total + moved(total, lambda b, f, s=step: (b ^ s, f))
+    while step < far_half:
+        mask = step | (step >> 1) if step in (4, 16) else step
+        total = total + moved(total, swap(mask))
         step *= 2
     got = moved(theirs, other_feat)
     grad_inputs = jnp.where(

time: 92.2 us -> 91.2 us (0.989)
  starting transfers between devices: 27.2 us -> 29.8 us
  waiting for transfers between devices: 29.8 us -> 27.3 us
  Pallas kernels: 27.7 us -> 26.7 us
    ppermute x17, starting transfers between devices: 27.2 us -> 29.8 us  [moved(): return lax.ppermute(x, ('blk', 'feat'), route)]
    ppermute x17, waiting for transfers between devices: 29.8 us -> 27.3 us  [moved(): return lax.ppermute(x, ('blk', 'feat'), route)]
    pallas_call x5, Pallas kernels: 25.8 us -> 24.7 us  [call(): pl.pallas_call(body, out_shape=outs, in_specs=[vmem] * len(operands), out...]
  transfers between devices with their start and end apart: 17 -> 17, of which waited for: 8 -> 8; matrix products, arithmetic and copies ran while one was open for 3% -> 3% of each run, Pallas kernels for 23% -> 21%
where the time goes in v5:
time: 91.2 us; the launch traced here: 91 us
  starting transfers between devices  29.8 us (33%)
  waiting for transfers between devices  27.3 us (30%)
  Pallas kernels  26.7 us (29%)
  local copies, waits for them, and re-layouts  3.19 us (3%)
  other arithmetic  2.46 us (3%)
  between operations  1.58 us (2%)
    ppermute x17, starting transfers between devices, moved(): return lax.ppermute(x, ('blk', 'feat'), route)  29.8 us
    ppermute x17, waiting for transfers between devices, moved(): return lax.ppermute(x, ('blk', 'feat'), route)  27.3 us
    pallas_call x5, Pallas kernels, call(): pl.pallas_call(body, out_shape=outs, in_specs=[vmem] * len(operands), out...  24.7 us
    unnamed x14, local copies, waits for them, and re-layouts  1.95 us
  transfers between devices with their start and end apart: 17, of which 8 were waited for; matrix products, arithmetic and copies ran while one was open for 3% of the time, Pallas kernels for 21%

profile of v5, /device:TPU:0, one launch (start us, length us, event | category | flops | bytes accessed | tf_op | source)
XLA Modules:
  0.0 91.0 jit_solution(12978477870713206791)
XLA Ops:
  0.7 1.7 %shard_map.85.packed = bf16[64,2176]{1,0:T(8,128)(2,1)} custom-call(bf16[64,2048]{1,0:T(8,128)(2,1)} %bitcast.14, bf16[64,128]{1,0:T(8,128)(2,1)} %bitcast.15), custom_call_target="tpu_custom_call" | custom-call | tf_op jit(solution)/shard_map/pallas_call | solution.py:223
  2.4 3.3 %collective-permute-start = (bf16[64,2176]{1,0:T(8,128)(2,1)}, bf16[64,2176]{1,0:T(8,128)(2,1)S(1)}, u32[]{:S(2)}, u32[]{:S(2)}) collective-permute-start(bf16[64,2176]{1,0:T(8,128)(2,1)} %shard_map.85.packed), channel_id=1, source_target_pairs={{0,1},{1,0},{2,3},{3,2},{4,5},{5,4},{6,7},{7,6},{8,9},{9,8},{10,11... | collective-permute-start | bytes 835592 | tf_op jit(solution)/shard_map/ppermute | solution.py:27
  5.7 0.6 fusion.3
  6.3 0.6 fusion.4
  7.0 0.3 broadcast_multiply_fusion.mb
  7.3 5.6 %collective-permute-start.7 = (bf16[2048,128]{1,0:T(8,128)(2,1)S(1)}, bf16[2048,128]{1,0:T(8,128)(2,1)S(1)}, u32[]{:S(2)}, u32[]{:S(2)}) collective-permute-start(bf16[2048,128]{1,0:T(8,128)(2,1)S(1)} %broadcast_multiply_fusion.mb), channel_id=1, source_target_pairs={{0,126},{1,127},{2,0},{3,1},{4,2},{5,3},{6,4},{7,5},{8,6},{9,7},{1... | collective-permute-start | bytes 1572872 | tf_op jit(solution)/shard_map/ppermute | solution.py:27
  12.9 0.0 collective-permute-start.5
  13.6 0.0 copy-start.5
  13.6 0.7 copy-done.5
  14.3 0.0 collective-permute-done.arrived
  14.3 0.2 shard_map.86
  14.6 0.0 copy-start.1
  14.6 0.6 copy-done.1
  15.2 6.0 %collective-permute-start.8 = (bf16[128,2048]{1,0:T(8,128)(2,1)S(1)}, bf16[128,2048]{1,0:T(8,128)(2,1)S(1)}, u32[]{:S(2)}, u32[]{:S(2)}) collective-permute-start(bf16[128,2048]{1,0:T(8,128)(2,1)S(1)} %get-tuple-element.47.sb), channel_id=1, source_target_pairs={{0,126},{1,127},{2,0},{3,1},{4,2},{5,3},{6,4},{7,5},{8,6},{9,7},{1... | collective-permute-start | bytes 1572872 | tf_op jit(solution)/shard_map/ppermute | solution.py:27
  21.2 0.1 collective-permute-start.6
  21.2 0.7 copy-done.2
  21.9 4.9 %shard_map.87 = (f32[1024,128]{1,0:T(8,128)S(1)}, f32[1024,32]{1,0:T(8,128)S(1)}, bf16[1024,64]{1,0:T(8,128)(2,1)S(1)}, bf16[1024,256]{1,0:T(8,128)(2,1)S(1)}) custom-call(bf16[1024,128]{1,0:T(8,128)(2,1)S(1)} %constant_dynamic-slice_fusion.ma, bf16[128,1024]{1,0:T(8,128)(2,1)S(1)} %get-tuple-element.38.sa, bf16[2048,128]{1,0:T(8,128)(2,1)S(1)} %broadcast_multiply_fusion.mb, ...), custom_call_target="tpu_custom_call" | custom-call | flops 2147483648 | bytes 1048576 | tf_op jit(solution)/shard_map/pallas_call | solution.py:185
  26.8 0.1 collective-permute-start.3
  26.9 0.0 collective-permute-done.7.mb
  26.9 0.1 collective-permute-start.4
  27.0 0.0 collective-permute-done.5.mb
  27.0 2.0 %collective-permute-start.1 = (bf16[2048,128]{1,0:T(8,128)(2,1)S(1)}, bf16[2048,128]{1,0:T(8,128)(2,1)S(1)}, u32[]{:S(2)}, u32[]{:S(2)}) collective-permute-start(bf16[2048,128]{1,0:T(8,128)(2,1)S(1)} %broadcast_multiply_fusion.mb), channel_id=1, source_target_pairs={{0,4},{1,5},{2,6},{3,7},{4,8},{5,9},{6,10},{7,11},{8,12},{9,13},{1... | collective-permute-start | bytes 1572872 | tf_op jit(solution)/shard_map/ppermute | solution.py:27
  29.0 0.0 collective-permute-done.8.sb
  29.0 1.9 %collective-permute-start.2 = (bf16[128,2048]{1,0:T(8,128)(2,1)S(1)}, bf16[128,2048]{1,0:T(8,128)(2,1)S(1)}, u32[]{:S(2)}, u32[]{:S(2)}) collective-permute-start(bf16[128,2048]{1,0:T(8,128)(2,1)S(1)} %get-tuple-element.47.sb), channel_id=1, source_target_pairs={{0,4},{1,5},{2,6},{3,7},{4,8},{5,9},{6,10},{7,11},{8,12},{9,13},{1... | collective-permute-start | bytes 1572872 | tf_op jit(solution)/shard_map/ppermute | solution.py:27
  31.0 4.8 %shard_map.88 = (f32[1024,128]{1,0:T(8,128)S(1)}, f32[1024,32]{1,0:T(8,128)S(1)}) custom-call(bf16[1024,64]{1,0:T(8,128)(2,1)S(1)} %get-tuple-element.42.near_dist, bf16[1024,256]{1,0:T(8,128)(2,1)S(1)} %get-tuple-element.43.near_mix, bf16[2048,128]{1,0:T(8,128)(2,1)S(1)} %collective-permute-done.7.mb, ...), custom_call_target="tpu_custom_call", output_to_operand_aliasing={{0}: (6, {}), {1}: (7, {})} | custom-call | flops 2147483648 | bytes 1048576 | tf_op jit(solution)/shard_map/pallas_call | solution.py:185
  35.8 0.0 collective-permute-done.6.sb
  35.8 4.8 %shard_map.89 = (f32[1024,128]{1,0:T(8,128)S(1)}, f32[1024,32]{1,0:T(8,128)S(1)}) custom-call(bf16[1024,64]{1,0:T(8,128)(2,1)S(1)} %get-tuple-element.42.near_dist, bf16[1024,256]{1,0:T(8,128)(2,1)S(1)} %get-tuple-element.43.near_mix, bf16[2048,128]{1,0:T(8,128)(2,1)S(1)} %collective-permute-done.5.mb, ...), custom_call_target="tpu_custom_call", output_to_operand_aliasing={{0}: (6, {}), {1}: (7, {})} | custom-call | flops 2147483648 | bytes 1048576 | tf_op jit(solution)/shard_map/pallas_call | solution.py:185
  40.6 6.7 %collective-permute-done.4.sb = bf16[128,2048]{1,0:T(8,128)(2,1)S(1)} collective-permute-done((bf16[128,2048]{1,0:T(8,128)(2,1)S(1)}, bf16[128,2048]{1,0:T(8,128)(2,1)S(1)}, u32[]{:S(2)}, u32[]{:S(2)}) %collective-permute-start.4) | collective-permute-done | bytes 524320 | tf_op jit(solution)/shard_map/ppermute | solution.py:27
  47.3 4.8 %shard_map.90 = (f32[1024,128]{1,0:T(8,128)S(1)}, f32[1024,32]{1,0:T(8,128)S(1)}) custom-call(bf16[1024,64]{1,0:T(8,128)(2,1)S(1)} %get-tuple-element.42.near_dist, bf16[1024,256]{1,0:T(8,128)(2,1)S(1)} %get-tuple-element.43.near_mix, bf16[2048,128]{1,0:T(8,128)(2,1)S(1)} %collective-permute-done.3.mb, ...), custom_call_target="tpu_custom_call", output_to_operand_aliasing={{0}: (6, {}), {1}: (7, {})} | custom-call | flops 2147483648 | bytes 1048576 | tf_op jit(solution)/shard_map/pallas_call | solution.py:185
  52.1 0.0 collective-permute-done.1.mb
  52.1 0.8 collective-permute-done.2.sb
  52.9 5.4 %shard_map.91 = (f32[144,128]{1,0:T(8,128)S(1)}, bf16[64,1024]{1,0:T(8,128)(2,1)S(1)}, bf16[64,1024]{1,0:T(8,128)(2,1)S(1)}) custom-call(bf16[1024,64]{1,0:T(8,128)(2,1)S(1)} %get-tuple-element.42.near_dist, bf16[1024,256]{1,0:T(8,128)(2,1)S(1)} %get-tuple-element.43.near_mix, bf16[2048,128]{1,0:T(8,128)(2,1)S(1)} %collective-permute-done.1.mb, ...), custom_call_target="tpu_custom_call" | custom-call | flops 2147483648 | bytes 1048576 | tf_op jit(solution)/shard_map/pallas_call | solution.py:185
  58.4 1.4 %collective-permute-start.10 = (f32[144,128]{1,0:T(8,128)S(1)}, f32[144,128]{1,0:T(8,128)S(1)}, u32[]{:S(2)}, u32[]{:S(2)}) collective-permute-start(f32[144,128]{1,0:T(8,128)S(1)} %get-tuple-element.60), channel_id=1, source_target_pairs={{0,64},{1,65},{2,66},{3,67},{4,68},{5,69},{6,70},{7,71},{8,72},{9,... | collective-permute-start | bytes 221192 | tf_op jit(solution)/shard_map/ppermute | solution.py:27
  59.8 3.0 %collective-permute-done.10 = f32[144,128]{1,0:T(8,128)S(1)} collective-permute-done((f32[144,128]{1,0:T(8,128)S(1)}, f32[144,128]{1,0:T(8,128)S(1)}, u32[]{:S(2)}, u32[]{:S(2)}) %collective-permute-start.10) | collective-permute-done | bytes 73760 | tf_op jit(solution)/shard_map/ppermute | solution.py:27
  62.8 3.7 %collective-permute-start.11 = (f32[72,128]{1,0:T(8,128)S(1)}, f32[72,128]{1,0:T(8,128)S(1)}, u32[]{:S(2)}, u32[]{:S(2)}) collective-permute-start(f32[72,128]{1,0:T(8,128)S(1)} %slice.33), channel_id=1, source_target_pairs={{0,65},{1,64},{2,67},{3,66},{4,69},{5,68},{6,71},{7,70},{8,73},{9,... | collective-permute-start | bytes 110600 | tf_op jit(solution)/shard_map/ppermute | solution.py:27
  66.5 1.9 %collective-permute-done.11 = f32[72,128]{1,0:T(8,128)S(1)} collective-permute-done((f32[72,128]{1,0:T(8,128)S(1)}, f32[72,128]{1,0:T(8,128)S(1)}, u32[]{:S(2)}, u32[]{:S(2)}) %collective-permute-start.11) | collective-permute-done | bytes 36896 | tf_op jit(solution)/shard_map/ppermute | solution.py:27
  68.4 1.6 %collective-permute-start.12 = (f32[72,128]{1,0:T(8,128)S(1)}, f32[72,128]{1,0:T(8,128)S(1)}, u32[]{:S(2)}, u32[]{:S(2)}) collective-permute-start(f32[72,128]{1,0:T(8,128)S(1)} %slice_add_fusion), channel_id=1, source_target_pairs={{0,2},{1,3},{2,0},{3,1},{4,6},{5,7},{6,4},{7,5},{8,10},{9,11},{10,... | collective-permute-start | bytes 110600 | tf_op jit(solution)/shard_map/ppermute | solution.py:27
  70.0 1.4 %collective-permute-start.9 = (bf16[64,1024]{1,0:T(8,128)(2,1)S(1)}, bf16[64,1024]{1,0:T(8,128)(2,1)S(1)}, u32[]{:S(2)}, u32[]{:S(2)}) collective-permute-start(bf16[64,1024]{1,0:T(8,128)(2,1)S(1)} %get-tuple-element.59), channel_id=1, source_target_pairs={{0,1},{1,0},{2,3},{3,2},{4,5},{5,4},{6,7},{7,6},{8,9},{9,8},{10,11... | collective-permute-start | bytes 393224 | tf_op jit(solution)/shard_map/ppermute | solution.py:27
  71.4 0.1 collective-permute-start.13
  71.5 3.9 %collective-permute-done.13 = f32[72,128]{1,0:T(8,128)S(1)} collective-permute-done((f32[72,128]{1,0:T(8,128)S(1)}, f32[72,128]{1,0:T(8,128)S(1)}, u32[]{:S(2)}, u32[]{:S(2)}) %collective-permute-start.13) | collective-permute-done | bytes 36896 | tf_op jit(solution)/shard_map/ppermute | solution.py:27
  75.5 1.5 %collective-permute-start.14 = (f32[72,128]{1,0:T(8,128)S(1)}, f32[72,128]{1,0:T(8,128)S(1)}, u32[]{:S(2)}, u32[]{:S(2)}) collective-permute-start(f32[72,128]{1,0:T(8,128)S(1)} %add.40), channel_id=1, source_target_pairs={{0,12},{1,13},{2,14},{3,15},{4,8},{5,9},{6,10},{7,11},{8,4},{9,5},... | collective-permute-start | bytes 110600 | tf_op jit(solution)/shard_map/ppermute | solution.py:27
  77.0 3.7 %collective-permute-done.14 = f32[72,128]{1,0:T(8,128)S(1)} collective-permute-done((f32[72,128]{1,0:T(8,128)S(1)}, f32[72,128]{1,0:T(8,128)S(1)}, u32[]{:S(2)}, u32[]{:S(2)}) %collective-permute-start.14) | collective-permute-done | bytes 36896 | tf_op jit(solution)/shard_map/ppermute | solution.py:27
  80.7 3.9 %collective-permute-done.15 = f32[72,128]{1,0:T(8,128)S(1)} collective-permute-done((f32[72,128]{1,0:T(8,128)S(1)}, f32[72,128]{1,0:T(8,128)S(1)}, u32[]{:S(2)}, u32[]{:S(2)}) %collective-permute-start.15) | collective-permute-done | bytes 36896 | tf_op jit(solution)/shard_map/ppermute | solution.py:27
  84.6 1.2 %collective-permute-start.16 = (f32[72,128]{1,0:T(8,128)S(1)}, f32[72,128]{1,0:T(8,128)S(1)}, u32[]{:S(2)}, u32[]{:S(2)}) collective-permute-start(f32[72,128]{1,0:T(8,128)S(1)} %add.42), channel_id=1, source_target_pairs={{0,48},{1,49},{2,50},{3,51},{4,52},{5,53},{6,54},{7,55},{8,56},{9,... | collective-permute-start | bytes 110600 | tf_op jit(solution)/shard_map/ppermute | solution.py:27
  85.8 0.8 fusion
  86.6 3.2 %collective-permute-done.16 = f32[72,128]{1,0:T(8,128)S(1)} collective-permute-done((f32[72,128]{1,0:T(8,128)S(1)}, f32[72,128]{1,0:T(8,128)S(1)}, u32[]{:S(2)}, u32[]{:S(2)}) %collective-permute-start.16) | collective-permute-done | bytes 36896 | tf_op jit(solution)/shard_map/ppermute | solution.py:27
  89.8 0.6 slice_bitcast_fusion
  90.4 0.6 slice_bitcast_fusion.1
  (26 shorter events, 0.1 us)
Async XLA Ops:
  0.6 6.4 %copy-start.3 = (bf16[2048,128]{1,0:T(8,128)(2,1)S(1)}, bf16[2048,128]{1,0:T(8,128)(2,1)}, u32[]{:S(2)}) copy-start(bf16[2048,128]{1,0:T(8,128)(2,1)} %param.8) | copy-start | bytes 1572868
  0.6 5.0 %copy-start.6 = (s32[64]{0:T(128)S(1)}, s32[64]{0:T(128)}, u32[]{:S(2)}) copy-start(s32[64]{0:T(128)} %param.13) | copy-start | bytes 772
  2.4 3.9 %copy-start.4 = (s32[2048]{0:T(1024)S(1)}, s32[2048]{0:T(1024)}, u32[]{:S(2)}) copy-start(s32[2048]{0:T(1024)} %param.12) | copy-start | bytes 24580
  2.4 11.9 %collective-permute-start = (bf16[64,2176]{1,0:T(8,128)(2,1)}, bf16[64,2176]{1,0:T(8,128)(2,1)S(1)}, u32[]{:S(2)}, u32[]{:S(2)}) collective-permute-start(bf16[64,2176]{1,0:T(8,128)(2,1)} %shard_map.85.packed), channel_id=1, source_target_pairs={{0,1},{1,0},{2,3},{3,2},{4,5},{5,4},{6,7},{7,6},{8,9},{9,8},{10,11... | collective-permute-start | bytes 835592 | tf_op jit(solution)/shard_map/ppermute | solution.py:27
  7.0 7.3 %copy-start = (bf16[64,2176]{1,0:T(8,128)(2,1)S(1)}, bf16[64,2176]{1,0:T(8,128)(2,1)}, u32[]{:S(2)}) copy-start(bf16[64,2176]{1,0:T(8,128)(2,1)} %shard_map.85.packed) | copy-start | bytes 835588
  7.3 19.6 %collective-permute-start.7 = (bf16[2048,128]{1,0:T(8,128)(2,1)S(1)}, bf16[2048,128]{1,0:T(8,128)(2,1)S(1)}, u32[]{:S(2)}, u32[]{:S(2)}) collective-permute-start(bf16[2048,128]{1,0:T(8,128)(2,1)S(1)} %broadcast_multiply_fusion.mb), channel_id=1, source_target_pairs={{0,126},{1,127},{2,0},{3,1},{4,2},{5,3},{6,4},{7,5},{8,6},{9,7},{1... | collective-permute-start | bytes 1572872 | tf_op jit(solution)/shard_map/ppermute | solution.py:27
  12.9 14.1 %collective-permute-start.5 = (bf16[2048,128]{1,0:T(8,128)(2,1)S(1)}, bf16[2048,128]{1,0:T(8,128)(2,1)S(1)}, u32[]{:S(2)}, u32[]{:S(2)}) collective-permute-start(bf16[2048,128]{1,0:T(8,128)(2,1)S(1)} %broadcast_multiply_fusion.mb), channel_id=1, source_target_pairs={{0,2},{1,3},{2,4},{3,5},{4,6},{5,7},{6,8},{7,9},{8,10},{9,11},{10,... | collective-permute-start | bytes 1572872 | tf_op jit(solution)/shard_map/ppermute | solution.py:27
  13.6 0.7 copy-start.5
  14.6 0.6 copy-start.1
  15.2 13.8 %collective-permute-start.8 = (bf16[128,2048]{1,0:T(8,128)(2,1)S(1)}, bf16[128,2048]{1,0:T(8,128)(2,1)S(1)}, u32[]{:S(2)}, u32[]{:S(2)}) collective-permute-start(bf16[128,2048]{1,0:T(8,128)(2,1)S(1)} %get-tuple-element.47.sb), channel_id=1, source_target_pairs={{0,126},{1,127},{2,0},{3,1},{4,2},{5,3},{6,4},{7,5},{8,6},{9,7},{1... | collective-permute-start | bytes 1572872 | tf_op jit(solution)/shard_map/ppermute | solution.py:27
  21.1 0.8 copy-start.2
  21.2 14.6 %collective-permute-start.6 = (bf16[128,2048]{1,0:T(8,128)(2,1)S(1)}, bf16[128,2048]{1,0:T(8,128)(2,1)S(1)}, u32[]{:S(2)}, u32[]{:S(2)}) collective-permute-start(bf16[128,2048]{1,0:T(8,128)(2,1)S(1)} %get-tuple-element.47.sb), channel_id=1, source_target_pairs={{0,2},{1,3},{2,4},{3,5},{4,6},{5,7},{6,8},{7,9},{8,10},{9,11},{10,... | collective-permute-start | bytes 1572872 | tf_op jit(solution)/shard_map/ppermute | solution.py:27
  26.8 13.8 %collective-permute-start.3 = (bf16[2048,128]{1,0:T(8,128)(2,1)S(1)}, bf16[2048,128]{1,0:T(8,128)(2,1)S(1)}, u32[]{:S(2)}, u32[]{:S(2)}) collective-permute-start(bf16[2048,128]{1,0:T(8,128)(2,1)S(1)} %broadcast_multiply_fusion.mb), channel_id=1, source_target_pairs={{0,124},{1,125},{2,126},{3,127},{4,0},{5,1},{6,2},{7,3},{8,4},{9,5... | collective-permute-start | bytes 1572872 | tf_op jit(solution)/shard_map/ppermute | solution.py:27
  26.9 20.4 %collective-permute-start.4 = (bf16[128,2048]{1,0:T(8,128)(2,1)S(1)}, bf16[128,2048]{1,0:T(8,128)(2,1)S(1)}, u32[]{:S(2)}, u32[]{:S(2)}) collective-permute-start(bf16[128,2048]{1,0:T(8,128)(2,1)S(1)} %get-tuple-element.47.sb), channel_id=1, source_target_pairs={{0,124},{1,125},{2,126},{3,127},{4,0},{5,1},{6,2},{7,3},{8,4},{9,5... | collective-permute-start | bytes 1572872 | tf_op jit(solution)/shard_map/ppermute | solution.py:27
  27.0 25.1 %collective-permute-start.1 = (bf16[2048,128]{1,0:T(8,128)(2,1)S(1)}, bf16[2048,128]{1,0:T(8,128)(2,1)S(1)}, u32[]{:S(2)}, u32[]{:S(2)}) collective-permute-start(bf16[2048,128]{1,0:T(8,128)(2,1)S(1)} %broadcast_multiply_fusion.mb), channel_id=1, source_target_pairs={{0,4},{1,5},{2,6},{3,7},{4,8},{5,9},{6,10},{7,11},{8,12},{9,13},{1... | collective-permute-start | bytes 1572872 | tf_op jit(solution)/shard_map/ppermute | solution.py:27
  29.0 23.9 %collective-permute-start.2 = (bf16[128,2048]{1,0:T(8,128)(2,1)S(1)}, bf16[128,2048]{1,0:T(8,128)(2,1)S(1)}, u32[]{:S(2)}, u32[]{:S(2)}) collective-permute-start(bf16[128,2048]{1,0:T(8,128)(2,1)S(1)} %get-tuple-element.47.sb), channel_id=1, source_target_pairs={{0,4},{1,5},{2,6},{3,7},{4,8},{5,9},{6,10},{7,11},{8,12},{9,13},{1... | collective-permute-start | bytes 1572872 | tf_op jit(solution)/shard_map/ppermute | solution.py:27
  58.4 4.4 %collective-permute-start.10 = (f32[144,128]{1,0:T(8,128)S(1)}, f32[144,128]{1,0:T(8,128)S(1)}, u32[]{:S(2)}, u32[]{:S(2)}) collective-permute-start(f32[144,128]{1,0:T(8,128)S(1)} %get-tuple-element.60), channel_id=1, source_target_pairs={{0,64},{1,65},{2,66},{3,67},{4,68},{5,69},{6,70},{7,71},{8,72},{9,... | collective-permute-start | bytes 221192 | tf_op jit(solution)/shard_map/ppermute | solution.py:27
  62.8 5.6 %collective-permute-start.11 = (f32[72,128]{1,0:T(8,128)S(1)}, f32[72,128]{1,0:T(8,128)S(1)}, u32[]{:S(2)}, u32[]{:S(2)}) collective-permute-start(f32[72,128]{1,0:T(8,128)S(1)} %slice.33), channel_id=1, source_target_pairs={{0,65},{1,64},{2,67},{3,66},{4,69},{5,68},{6,71},{7,70},{8,73},{9,... | collective-permute-start | bytes 110600 | tf_op jit(solution)/shard_map/ppermute | solution.py:27
  68.4 3.0 %collective-permute-start.12 = (f32[72,128]{1,0:T(8,128)S(1)}, f32[72,128]{1,0:T(8,128)S(1)}, u32[]{:S(2)}, u32[]{:S(2)}) collective-permute-start(f32[72,128]{1,0:T(8,128)S(1)} %slice_add_fusion), channel_id=1, source_target_pairs={{0,2},{1,3},{2,0},{3,1},{4,6},{5,7},{6,4},{7,5},{8,10},{9,11},{10,... | collective-permute-start | bytes 110600 | tf_op jit(solution)/shard_map/ppermute | solution.py:27
  70.0 15.8 %collective-permute-start.9 = (bf16[64,1024]{1,0:T(8,128)(2,1)S(1)}, bf16[64,1024]{1,0:T(8,128)(2,1)S(1)}, u32[]{:S(2)}, u32[]{:S(2)}) collective-permute-start(bf16[64,1024]{1,0:T(8,128)(2,1)S(1)} %get-tuple-element.59), channel_id=1, source_target_pairs={{0,1},{1,0},{2,3},{3,2},{4,5},{5,4},{6,7},{7,6},{8,9},{9,8},{10,11... | collective-permute-start | bytes 393224 | tf_op jit(solution)/shard_map/ppermute | solution.py:27
  71.4 4.0 %collective-permute-start.13 = (f32[72,128]{1,0:T(8,128)S(1)}, f32[72,128]{1,0:T(8,128)S(1)}, u32[]{:S(2)}, u32[]{:S(2)}) collective-permute-start(f32[72,128]{1,0:T(8,128)S(1)} %add.39), channel_id=1, source_target_pairs={{0,4},{1,5},{2,6},{3,7},{4,0},{5,1},{6,2},{7,3},{8,12},{9,13},{10,... | collective-permute-start | bytes 110600 | tf_op jit(solution)/shard_map/ppermute | solution.py:27
  75.5 5.2 %collective-permute-start.14 = (f32[72,128]{1,0:T(8,128)S(1)}, f32[72,128]{1,0:T(8,128)S(1)}, u32[]{:S(2)}, u32[]{:S(2)}) collective-permute-start(f32[72,128]{1,0:T(8,128)S(1)} %add.40), channel_id=1, source_target_pairs={{0,12},{1,13},{2,14},{3,15},{4,8},{5,9},{6,10},{7,11},{8,4},{9,5},... | collective-permute-start | bytes 110600 | tf_op jit(solution)/shard_map/ppermute | solution.py:27
  80.7 4.0 %collective-permute-start.15 = (f32[72,128]{1,0:T(8,128)S(1)}, f32[72,128]{1,0:T(8,128)S(1)}, u32[]{:S(2)}, u32[]{:S(2)}) collective-permute-start(f32[72,128]{1,0:T(8,128)S(1)} %add.41), channel_id=1, source_target_pairs={{0,16},{1,17},{2,18},{3,19},{4,20},{5,21},{6,22},{7,23},{8,24},{9,... | collective-permute-start | bytes 110600 | tf_op jit(solution)/shard_map/ppermute | solution.py:27
  84.6 5.2 %collective-permute-start.16 = (f32[72,128]{1,0:T(8,128)S(1)}, f32[72,128]{1,0:T(8,128)S(1)}, u32[]{:S(2)}, u32[]{:S(2)}) collective-permute-start(f32[72,128]{1,0:T(8,128)S(1)} %add.42), channel_id=1, source_target_pairs={{0,48},{1,49},{2,50},{3,51},{4,52},{5,53},{6,54},{7,55},{8,56},{9,... | collective-permute-start | bytes 110600 | tf_op jit(solution)/shard_map/ppermute | solution.py:27

commit v6 on v5

--- a/solution.py
+++ b/solution.py
@@ -13,8 +13,8 @@
 NT = (((1,), (1,)), ((), ()))
 F32 = jnp.float32
 BF16 = jnp.bfloat16
-ROW_TILE = 512
-COL_TILE = 1024
+ROW_TILE = 1024
+COL_TILE = 512
 
 
 def moved(x, target):

time: 91.2 us -> 91 us (level)
  transfers between devices with their start and end apart: 17 -> 17, of which waited for: 8 -> 8; matrix products, arithmetic and copies ran while one was open for 3% -> 3% of each run, Pallas kernels for 21% -> 22%
where the time goes in v6:
time: 91 us; the launch traced here: 90.8 us
  starting transfers between devices  30.3 us (33%)
  Pallas kernels  26.8 us (29%)
  waiting for transfers between devices  26.5 us (29%)
  local copies, waits for them, and re-layouts  3.19 us (4%)
  other arithmetic  2.46 us (3%)
  between operations  1.58 us (2%)
    ppermute x17, starting transfers between devices, moved(): return lax.ppermute(x, ('blk', 'feat'), route)  30.3 us
    ppermute x17, waiting for transfers between devices, moved(): return lax.ppermute(x, ('blk', 'feat'), route)  26.5 us
    pallas_call x5, Pallas kernels, call(): pl.pallas_call(body, out_shape=outs, in_specs=[vmem] * len(operands), out...  24.8 us
    unnamed x14, local copies, waits for them, and re-layouts  1.95 us
  transfers between devices with their start and end apart: 17, of which 8 were waited for; matrix products, arithmetic and copies ran while one was open for 3% of the time, Pallas kernels for 22%

profile of v6, /device:TPU:0, one launch (start us, length us, event | category | flops | bytes accessed | tf_op | source)
XLA Modules:
  0.0 90.8 jit_solution(5591579391037869482)
XLA Ops:
  0.7 1.7 %shard_map.85.packed = bf16[64,2176]{1,0:T(8,128)(2,1)} custom-call(bf16[64,2048]{1,0:T(8,128)(2,1)} %bitcast.14, bf16[64,128]{1,0:T(8,128)(2,1)} %bitcast.15), custom_call_target="tpu_custom_call" | custom-call | tf_op jit(solution)/shard_map/pallas_call | solution.py:223
  2.4 3.3 %collective-permute-start = (bf16[64,2176]{1,0:T(8,128)(2,1)}, bf16[64,2176]{1,0:T(8,128)(2,1)S(1)}, u32[]{:S(2)}, u32[]{:S(2)}) collective-permute-start(bf16[64,2176]{1,0:T(8,128)(2,1)} %shard_map.85.packed), channel_id=1, source_target_pairs={{0,1},{1,0},{2,3},{3,2},{4,5},{5,4},{6,7},{7,6},{8,9},{9,8},{10,11... | collective-permute-start | bytes 835592 | tf_op jit(solution)/shard_map/ppermute | solution.py:27
  5.7 0.6 fusion.3
  6.3 0.6 fusion.4
  7.0 0.3 broadcast_multiply_fusion.mb
  7.3 5.6 %collective-permute-start.7 = (bf16[2048,128]{1,0:T(8,128)(2,1)S(1)}, bf16[2048,128]{1,0:T(8,128)(2,1)S(1)}, u32[]{:S(2)}, u32[]{:S(2)}) collective-permute-start(bf16[2048,128]{1,0:T(8,128)(2,1)S(1)} %broadcast_multiply_fusion.mb), channel_id=1, source_target_pairs={{0,126},{1,127},{2,0},{3,1},{4,2},{5,3},{6,4},{7,5},{8,6},{9,7},{1... | collective-permute-start | bytes 1572872 | tf_op jit(solution)/shard_map/ppermute | solution.py:27
  12.9 0.0 collective-permute-start.5
  13.6 0.0 copy-start.5
  13.6 0.7 copy-done.5
  14.3 0.0 collective-permute-done.arrived
  14.3 0.2 shard_map.86
  14.6 0.0 copy-start.1
  14.6 0.6 copy-done.1
  15.2 6.0 %collective-permute-start.8 = (bf16[128,2048]{1,0:T(8,128)(2,1)S(1)}, bf16[128,2048]{1,0:T(8,128)(2,1)S(1)}, u32[]{:S(2)}, u32[]{:S(2)}) collective-permute-start(bf16[128,2048]{1,0:T(8,128)(2,1)S(1)} %get-tuple-element.47.sb), channel_id=1, source_target_pairs={{0,126},{1,127},{2,0},{3,1},{4,2},{5,3},{6,4},{7,5},{8,6},{9,7},{1... | collective-permute-start | bytes 1572872 | tf_op jit(solution)/shard_map/ppermute | solution.py:27
  21.2 0.1 collective-permute-start.6
  21.2 0.7 copy-done.2
  21.9 4.9 %shard_map.87 = (f32[1024,128]{1,0:T(8,128)S(1)}, f32[1024,32]{1,0:T(8,128)S(1)}, bf16[1024,64]{1,0:T(8,128)(2,1)S(1)}, bf16[1024,256]{1,0:T(8,128)(2,1)S(1)}) custom-call(bf16[1024,128]{1,0:T(8,128)(2,1)S(1)} %constant_dynamic-slice_fusion.ma, bf16[128,1024]{1,0:T(8,128)(2,1)S(1)} %get-tuple-element.38.sa, bf16[2048,128]{1,0:T(8,128)(2,1)S(1)} %broadcast_multiply_fusion.mb, ...), custom_call_target="tpu_custom_call" | custom-call | flops 2147483648 | bytes 1048576 | tf_op jit(solution)/shard_map/pallas_call | solution.py:185
  26.8 0.1 collective-permute-start.3
  26.9 0.0 collective-permute-done.7.mb
  26.9 0.1 collective-permute-start.4
  27.0 0.0 collective-permute-done.5.mb
  27.0 2.0 %collective-permute-start.1 = (bf16[2048,128]{1,0:T(8,128)(2,1)S(1)}, bf16[2048,128]{1,0:T(8,128)(2,1)S(1)}, u32[]{:S(2)}, u32[]{:S(2)}) collective-permute-start(bf16[2048,128]{1,0:T(8,128)(2,1)S(1)} %broadcast_multiply_fusion.mb), channel_id=1, source_target_pairs={{0,4},{1,5},{2,6},{3,7},{4,8},{5,9},{6,10},{7,11},{8,12},{9,13},{1... | collective-permute-start | bytes 1572872 | tf_op jit(solution)/shard_map/ppermute | solution.py:27
  29.0 0.0 collective-permute-done.8.sb
  29.0 1.9 %collective-permute-start.2 = (bf16[128,2048]{1,0:T(8,128)(2,1)S(1)}, bf16[128,2048]{1,0:T(8,128)(2,1)S(1)}, u32[]{:S(2)}, u32[]{:S(2)}) collective-permute-start(bf16[128,2048]{1,0:T(8,128)(2,1)S(1)} %get-tuple-element.47.sb), channel_id=1, source_target_pairs={{0,4},{1,5},{2,6},{3,7},{4,8},{5,9},{6,10},{7,11},{8,12},{9,13},{1... | collective-permute-start | bytes 1572872 | tf_op jit(solution)/shard_map/ppermute | solution.py:27
  31.0 4.8 %shard_map.88 = (f32[1024,128]{1,0:T(8,128)S(1)}, f32[1024,32]{1,0:T(8,128)S(1)}) custom-call(bf16[1024,64]{1,0:T(8,128)(2,1)S(1)} %get-tuple-element.42.near_dist, bf16[1024,256]{1,0:T(8,128)(2,1)S(1)} %get-tuple-element.43.near_mix, bf16[2048,128]{1,0:T(8,128)(2,1)S(1)} %collective-permute-done.7.mb, ...), custom_call_target="tpu_custom_call", output_to_operand_aliasing={{0}: (6, {}), {1}: (7, {})} | custom-call | flops 2147483648 | bytes 1048576 | tf_op jit(solution)/shard_map/pallas_call | solution.py:185
  35.8 0.0 collective-permute-done.6.sb
  35.8 4.8 %shard_map.89 = (f32[1024,128]{1,0:T(8,128)S(1)}, f32[1024,32]{1,0:T(8,128)S(1)}) custom-call(bf16[1024,64]{1,0:T(8,128)(2,1)S(1)} %get-tuple-element.42.near_dist, bf16[1024,256]{1,0:T(8,128)(2,1)S(1)} %get-tuple-element.43.near_mix, bf16[2048,128]{1,0:T(8,128)(2,1)S(1)} %collective-permute-done.5.mb, ...), custom_call_target="tpu_custom_call", output_to_operand_aliasing={{0}: (6, {}), {1}: (7, {})} | custom-call | flops 2147483648 | bytes 1048576 | tf_op jit(solution)/shard_map/pallas_call | solution.py:185
  40.6 0.0 collective-permute-done.3.mb
  40.6 6.7 %collective-permute-done.4.sb = bf16[128,2048]{1,0:T(8,128)(2,1)S(1)} collective-permute-done((bf16[128,2048]{1,0:T(8,128)(2,1)S(1)}, bf16[128,2048]{1,0:T(8,128)(2,1)S(1)}, u32[]{:S(2)}, u32[]{:S(2)}) %collective-permute-start.4) | collective-permute-done | bytes 524320 | tf_op jit(solution)/shard_map/ppermute | solution.py:27
  47.3 5.0 %shard_map.90 = (f32[1024,128]{1,0:T(8,128)S(1)}, f32[1024,32]{1,0:T(8,128)S(1)}) custom-call(bf16[1024,64]{1,0:T(8,128)(2,1)S(1)} %get-tuple-element.42.near_dist, bf16[1024,256]{1,0:T(8,128)(2,1)S(1)} %get-tuple-element.43.near_mix, bf16[2048,128]{1,0:T(8,128)(2,1)S(1)} %collective-permute-done.3.mb, ...), custom_call_target="tpu_custom_call", output_to_operand_aliasing={{0}: (6, {}), {1}: (7, {})} | custom-call | flops 2147483648 | bytes 1048576 | tf_op jit(solution)/shard_map/pallas_call | solution.py:185
  52.4 0.6 collective-permute-done.2.sb
  53.0 5.2 %shard_map.91 = (f32[144,128]{1,0:T(8,128)S(1)}, bf16[64,1024]{1,0:T(8,128)(2,1)S(1)}, bf16[64,1024]{1,0:T(8,128)(2,1)S(1)}) custom-call(bf16[1024,64]{1,0:T(8,128)(2,1)S(1)} %get-tuple-element.42.near_dist, bf16[1024,256]{1,0:T(8,128)(2,1)S(1)} %get-tuple-element.43.near_mix, bf16[2048,128]{1,0:T(8,128)(2,1)S(1)} %collective-permute-done.1.mb, ...), custom_call_target="tpu_custom_call" | custom-call | flops 2147483648 | bytes 1048576 | tf_op jit(solution)/shard_map/pallas_call | solution.py:185
  58.2 1.4 %collective-permute-start.10 = (f32[144,128]{1,0:T(8,128)S(1)}, f32[144,128]{1,0:T(8,128)S(1)}, u32[]{:S(2)}, u32[]{:S(2)}) collective-permute-start(f32[144,128]{1,0:T(8,128)S(1)} %get-tuple-element.60), channel_id=1, source_target_pairs={{0,64},{1,65},{2,66},{3,67},{4,68},{5,69},{6,70},{7,71},{8,72},{9,... | collective-permute-start | bytes 221192 | tf_op jit(solution)/shard_map/ppermute | solution.py:27
  59.6 3.0 %collective-permute-done.10 = f32[144,128]{1,0:T(8,128)S(1)} collective-permute-done((f32[144,128]{1,0:T(8,128)S(1)}, f32[144,128]{1,0:T(8,128)S(1)}, u32[]{:S(2)}, u32[]{:S(2)}) %collective-permute-start.10) | collective-permute-done | bytes 73760 | tf_op jit(solution)/shard_map/ppermute | solution.py:27
  62.6 3.6 %collective-permute-start.11 = (f32[72,128]{1,0:T(8,128)S(1)}, f32[72,128]{1,0:T(8,128)S(1)}, u32[]{:S(2)}, u32[]{:S(2)}) collective-permute-start(f32[72,128]{1,0:T(8,128)S(1)} %slice.33), channel_id=1, source_target_pairs={{0,65},{1,64},{2,67},{3,66},{4,69},{5,68},{6,71},{7,70},{8,73},{9,... | collective-permute-start | bytes 110600 | tf_op jit(solution)/shard_map/ppermute | solution.py:27
  66.3 1.9 %collective-permute-done.11 = f32[72,128]{1,0:T(8,128)S(1)} collective-permute-done((f32[72,128]{1,0:T(8,128)S(1)}, f32[72,128]{1,0:T(8,128)S(1)}, u32[]{:S(2)}, u32[]{:S(2)}) %collective-permute-start.11) | collective-permute-done | bytes 36896 | tf_op jit(solution)/shard_map/ppermute | solution.py:27
  68.2 1.6 %collective-permute-start.12 = (f32[72,128]{1,0:T(8,128)S(1)}, f32[72,128]{1,0:T(8,128)S(1)}, u32[]{:S(2)}, u32[]{:S(2)}) collective-permute-start(f32[72,128]{1,0:T(8,128)S(1)} %slice_add_fusion), channel_id=1, source_target_pairs={{0,2},{1,3},{2,0},{3,1},{4,6},{5,7},{6,4},{7,5},{8,10},{9,11},{10,... | collective-permute-start | bytes 110600 | tf_op jit(solution)/shard_map/ppermute | solution.py:27
  69.8 1.4 %collective-permute-start.9 = (bf16[64,1024]{1,0:T(8,128)(2,1)S(1)}, bf16[64,1024]{1,0:T(8,128)(2,1)S(1)}, u32[]{:S(2)}, u32[]{:S(2)}) collective-permute-start(bf16[64,1024]{1,0:T(8,128)(2,1)S(1)} %get-tuple-element.59), channel_id=1, source_target_pairs={{0,1},{1,0},{2,3},{3,2},{4,5},{5,4},{6,7},{7,6},{8,9},{9,8},{10,11... | collective-permute-start | bytes 393224 | tf_op jit(solution)/shard_map/ppermute | solution.py:27
  71.3 0.1 collective-permute-start.13
  71.3 3.9 %collective-permute-done.13 = f32[72,128]{1,0:T(8,128)S(1)} collective-permute-done((f32[72,128]{1,0:T(8,128)S(1)}, f32[72,128]{1,0:T(8,128)S(1)}, u32[]{:S(2)}, u32[]{:S(2)}) %collective-permute-start.13) | collective-permute-done | bytes 36896 | tf_op jit(solution)/shard_map/ppermute | solution.py:27
  75.3 1.7 %collective-permute-start.14 = (f32[72,128]{1,0:T(8,128)S(1)}, f32[72,128]{1,0:T(8,128)S(1)}, u32[]{:S(2)}, u32[]{:S(2)}) collective-permute-start(f32[72,128]{1,0:T(8,128)S(1)} %add.40), channel_id=1, source_target_pairs={{0,12},{1,13},{2,14},{3,15},{4,8},{5,9},{6,10},{7,11},{8,4},{9,5},... | collective-permute-start | bytes 110600 | tf_op jit(solution)/shard_map/ppermute | solution.py:27
  77.0 3.4 %collective-permute-done.14 = f32[72,128]{1,0:T(8,128)S(1)} collective-permute-done((f32[72,128]{1,0:T(8,128)S(1)}, f32[72,128]{1,0:T(8,128)S(1)}, u32[]{:S(2)}, u32[]{:S(2)}) %collective-permute-start.14) | collective-permute-done | bytes 36896 | tf_op jit(solution)/shard_map/ppermute | solution.py:27
  80.5 3.9 %collective-permute-done.15 = f32[72,128]{1,0:T(8,128)S(1)} collective-permute-done((f32[72,128]{1,0:T(8,128)S(1)}, f32[72,128]{1,0:T(8,128)S(1)}, u32[]{:S(2)}, u32[]{:S(2)}) %collective-permute-start.15) | collective-permute-done | bytes 36896 | tf_op jit(solution)/shard_map/ppermute | solution.py:27
  84.4 1.4 %collective-permute-start.16 = (f32[72,128]{1,0:T(8,128)S(1)}, f32[72,128]{1,0:T(8,128)S(1)}, u32[]{:S(2)}, u32[]{:S(2)}) collective-permute-start(f32[72,128]{1,0:T(8,128)S(1)} %add.42), channel_id=1, source_target_pairs={{0,48},{1,49},{2,50},{3,51},{4,52},{5,53},{6,54},{7,55},{8,56},{9,... | collective-permute-start | bytes 110600 | tf_op jit(solution)/shard_map/ppermute | solution.py:27
  85.9 0.8 fusion
  86.7 2.9 %collective-permute-done.16 = f32[72,128]{1,0:T(8,128)S(1)} collective-permute-done((f32[72,128]{1,0:T(8,128)S(1)}, f32[72,128]{1,0:T(8,128)S(1)}, u32[]{:S(2)}, u32[]{:S(2)}) %collective-permute-start.16) | collective-permute-done | bytes 36896 | tf_op jit(solution)/shard_map/ppermute | solution.py:27
  89.6 0.6 slice_bitcast_fusion
  90.2 0.6 slice_bitcast_fusion.1
  (26 shorter events, 0.1 us)
Async XLA Ops:
  0.6 6.4 %copy-start.3 = (bf16[2048,128]{1,0:T(8,128)(2,1)S(1)}, bf16[2048,128]{1,0:T(8,128)(2,1)}, u32[]{:S(2)}) copy-start(bf16[2048,128]{1,0:T(8,128)(2,1)} %param.8) | copy-start | bytes 1572868
  0.6 5.0 %copy-start.6 = (s32[64]{0:T(128)S(1)}, s32[64]{0:T(128)}, u32[]{:S(2)}) copy-start(s32[64]{0:T(128)} %param.13) | copy-start | bytes 772
  2.4 3.9 %copy-start.4 = (s32[2048]{0:T(1024)S(1)}, s32[2048]{0:T(1024)}, u32[]{:S(2)}) copy-start(s32[2048]{0:T(1024)} %param.12) | copy-start | bytes 24580
  2.4 11.9 %collective-permute-start = (bf16[64,2176]{1,0:T(8,128)(2,1)}, bf16[64,2176]{1,0:T(8,128)(2,1)S(1)}, u32[]{:S(2)}, u32[]{:S(2)}) collective-permute-start(bf16[64,2176]{1,0:T(8,128)(2,1)} %shard_map.85.packed), channel_id=1, source_target_pairs={{0,1},{1,0},{2,3},{3,2},{4,5},{5,4},{6,7},{7,6},{8,9},{9,8},{10,11... | collective-permute-start | bytes 835592 | tf_op jit(solution)/shard_map/ppermute | solution.py:27
  7.0 7.3 %copy-start = (bf16[64,2176]{1,0:T(8,128)(2,1)S(1)}, bf16[64,2176]{1,0:T(8,128)(2,1)}, u32[]{:S(2)}) copy-start(bf16[64,2176]{1,0:T(8,128)(2,1)} %shard_map.85.packed) | copy-start | bytes 835588
  7.3 19.6 %collective-permute-start.7 = (bf16[2048,128]{1,0:T(8,128)(2,1)S(1)}, bf16[2048,128]{1,0:T(8,128)(2,1)S(1)}, u32[]{:S(2)}, u32[]{:S(2)}) collective-permute-start(bf16[2048,128]{1,0:T(8,128)(2,1)S(1)} %broadcast_multiply_fusion.mb), channel_id=1, source_target_pairs={{0,126},{1,127},{2,0},{3,1},{4,2},{5,3},{6,4},{7,5},{8,6},{9,7},{1... | collective-permute-start | bytes 1572872 | tf_op jit(solution)/shard_map/ppermute | solution.py:27
  12.9 14.1 %collective-permute-start.5 = (bf16[2048,128]{1,0:T(8,128)(2,1)S(1)}, bf16[2048,128]{1,0:T(8,128)(2,1)S(1)}, u32[]{:S(2)}, u32[]{:S(2)}) collective-permute-start(bf16[2048,128]{1,0:T(8,128)(2,1)S(1)} %broadcast_multiply_fusion.mb), channel_id=1, source_target_pairs={{0,2},{1,3},{2,4},{3,5},{4,6},{5,7},{6,8},{7,9},{8,10},{9,11},{10,... | collective-permute-start | bytes 1572872 | tf_op jit(solution)/shard_map/ppermute | solution.py:27
  13.6 0.7 copy-start.5
  14.6 0.6 copy-start.1
  15.2 13.9 %collective-permute-start.8 = (bf16[128,2048]{1,0:T(8,128)(2,1)S(1)}, bf16[128,2048]{1,0:T(8,128)(2,1)S(1)}, u32[]{:S(2)}, u32[]{:S(2)}) collective-permute-start(bf16[128,2048]{1,0:T(8,128)(2,1)S(1)} %get-tuple-element.47.sb), channel_id=1, source_target_pairs={{0,126},{1,127},{2,0},{3,1},{4,2},{5,3},{6,4},{7,5},{8,6},{9,7},{1... | collective-permute-start | bytes 1572872 | tf_op jit(solution)/shard_map/ppermute | solution.py:27
  21.1 0.8 copy-start.2
  21.2 14.6 %collective-permute-start.6 = (bf16[128,2048]{1,0:T(8,128)(2,1)S(1)}, bf16[128,2048]{1,0:T(8,128)(2,1)S(1)}, u32[]{:S(2)}, u32[]{:S(2)}) collective-permute-start(bf16[128,2048]{1,0:T(8,128)(2,1)S(1)} %get-tuple-element.47.sb), channel_id=1, source_target_pairs={{0,2},{1,3},{2,4},{3,5},{4,6},{5,7},{6,8},{7,9},{8,10},{9,11},{10,... | collective-permute-start | bytes 1572872 | tf_op jit(solution)/shard_map/ppermute | solution.py:27
  26.8 13.8 %collective-permute-start.3 = (bf16[2048,128]{1,0:T(8,128)(2,1)S(1)}, bf16[2048,128]{1,0:T(8,128)(2,1)S(1)}, u32[]{:S(2)}, u32[]{:S(2)}) collective-permute-start(bf16[2048,128]{1,0:T(8,128)(2,1)S(1)} %broadcast_multiply_fusion.mb), channel_id=1, source_target_pairs={{0,124},{1,125},{2,126},{3,127},{4,0},{5,1},{6,2},{7,3},{8,4},{9,5... | collective-permute-start | bytes 1572872 | tf_op jit(solution)/shard_map/ppermute | solution.py:27
  26.9 20.4 %collective-permute-start.4 = (bf16[128,2048]{1,0:T(8,128)(2,1)S(1)}, bf16[128,2048]{1,0:T(8,128)(2,1)S(1)}, u32[]{:S(2)}, u32[]{:S(2)}) collective-permute-start(bf16[128,2048]{1,0:T(8,128)(2,1)S(1)} %get-tuple-element.47.sb), channel_id=1, source_target_pairs={{0,124},{1,125},{2,126},{3,127},{4,0},{5,1},{6,2},{7,3},{8,4},{9,5... | collective-permute-start | bytes 1572872 | tf_op jit(solution)/shard_map/ppermute | solution.py:27
  27.0 25.3 %collective-permute-start.1 = (bf16[2048,128]{1,0:T(8,128)(2,1)S(1)}, bf16[2048,128]{1,0:T(8,128)(2,1)S(1)}, u32[]{:S(2)}, u32[]{:S(2)}) collective-permute-start(bf16[2048,128]{1,0:T(8,128)(2,1)S(1)} %broadcast_multiply_fusion.mb), channel_id=1, source_target_pairs={{0,4},{1,5},{2,6},{3,7},{4,8},{5,9},{6,10},{7,11},{8,12},{9,13},{1... | collective-permute-start | bytes 1572872 | tf_op jit(solution)/shard_map/ppermute | solution.py:27
  29.0 23.9 %collective-permute-start.2 = (bf16[128,2048]{1,0:T(8,128)(2,1)S(1)}, bf16[128,2048]{1,0:T(8,128)(2,1)S(1)}, u32[]{:S(2)}, u32[]{:S(2)}) collective-permute-start(bf16[128,2048]{1,0:T(8,128)(2,1)S(1)} %get-tuple-element.47.sb), channel_id=1, source_target_pairs={{0,4},{1,5},{2,6},{3,7},{4,8},{5,9},{6,10},{7,11},{8,12},{9,13},{1... | collective-permute-start | bytes 1572872 | tf_op jit(solution)/shard_map/ppermute | solution.py:27
  58.2 4.4 %collective-permute-start.10 = (f32[144,128]{1,0:T(8,128)S(1)}, f32[144,128]{1,0:T(8,128)S(1)}, u32[]{:S(2)}, u32[]{:S(2)}) collective-permute-start(f32[144,128]{1,0:T(8,128)S(1)} %get-tuple-element.60), channel_id=1, source_target_pairs={{0,64},{1,65},{2,66},{3,67},{4,68},{5,69},{6,70},{7,71},{8,72},{9,... | collective-permute-start | bytes 221192 | tf_op jit(solution)/shard_map/ppermute | solution.py:27
  62.6 5.6 %collective-permute-start.11 = (f32[72,128]{1,0:T(8,128)S(1)}, f32[72,128]{1,0:T(8,128)S(1)}, u32[]{:S(2)}, u32[]{:S(2)}) collective-permute-start(f32[72,128]{1,0:T(8,128)S(1)} %slice.33), channel_id=1, source_target_pairs={{0,65},{1,64},{2,67},{3,66},{4,69},{5,68},{6,71},{7,70},{8,73},{9,... | collective-permute-start | bytes 110600 | tf_op jit(solution)/shard_map/ppermute | solution.py:27
  68.2 3.0 %collective-permute-start.12 = (f32[72,128]{1,0:T(8,128)S(1)}, f32[72,128]{1,0:T(8,128)S(1)}, u32[]{:S(2)}, u32[]{:S(2)}) collective-permute-start(f32[72,128]{1,0:T(8,128)S(1)} %slice_add_fusion), channel_id=1, source_target_pairs={{0,2},{1,3},{2,0},{3,1},{4,6},{5,7},{6,4},{7,5},{8,10},{9,11},{10,... | collective-permute-start | bytes 110600 | tf_op jit(solution)/shard_map/ppermute | solution.py:27
  69.8 16.1 %collective-permute-start.9 = (bf16[64,1024]{1,0:T(8,128)(2,1)S(1)}, bf16[64,1024]{1,0:T(8,128)(2,1)S(1)}, u32[]{:S(2)}, u32[]{:S(2)}) collective-permute-start(bf16[64,1024]{1,0:T(8,128)(2,1)S(1)} %get-tuple-element.59), channel_id=1, source_target_pairs={{0,1},{1,0},{2,3},{3,2},{4,5},{5,4},{6,7},{7,6},{8,9},{9,8},{10,11... | collective-permute-start | bytes 393224 | tf_op jit(solution)/shard_map/ppermute | solution.py:27
  71.3 4.0 %collective-permute-start.13 = (f32[72,128]{1,0:T(8,128)S(1)}, f32[72,128]{1,0:T(8,128)S(1)}, u32[]{:S(2)}, u32[]{:S(2)}) collective-permute-start(f32[72,128]{1,0:T(8,128)S(1)} %add.39), channel_id=1, source_target_pairs={{0,4},{1,5},{2,6},{3,7},{4,0},{5,1},{6,2},{7,3},{8,12},{9,13},{10,... | collective-permute-start | bytes 110600 | tf_op jit(solution)/shard_map/ppermute | solution.py:27
  75.3 5.2 %collective-permute-start.14 = (f32[72,128]{1,0:T(8,128)S(1)}, f32[72,128]{1,0:T(8,128)S(1)}, u32[]{:S(2)}, u32[]{:S(2)}) collective-permute-start(f32[72,128]{1,0:T(8,128)S(1)} %add.40), channel_id=1, source_target_pairs={{0,12},{1,13},{2,14},{3,15},{4,8},{5,9},{6,10},{7,11},{8,4},{9,5},... | collective-permute-start | bytes 110600 | tf_op jit(solution)/shard_map/ppermute | solution.py:27
  80.5 4.0 %collective-permute-start.15 = (f32[72,128]{1,0:T(8,128)S(1)}, f32[72,128]{1,0:T(8,128)S(1)}, u32[]{:S(2)}, u32[]{:S(2)}) collective-permute-start(f32[72,128]{1,0:T(8,128)S(1)} %add.41), channel_id=1, source_target_pairs={{0,16},{1,17},{2,18},{3,19},{4,20},{5,21},{6,22},{7,23},{8,24},{9,... | collective-permute-start | bytes 110600 | tf_op jit(solution)/shard_map/ppermute | solution.py:27
  84.4 5.2 %collective-permute-start.16 = (f32[72,128]{1,0:T(8,128)S(1)}, f32[72,128]{1,0:T(8,128)S(1)}, u32[]{:S(2)}, u32[]{:S(2)}) collective-permute-start(f32[72,128]{1,0:T(8,128)S(1)} %add.42), channel_id=1, source_target_pairs={{0,48},{1,49},{2,50},{3,51},{4,52},{5,53},{6,54},{7,55},{8,56},{9,... | collective-permute-start | bytes 110600 | tf_op jit(solution)/shard_map/ppermute | solution.py:27

commit v7 on v6

--- a/solution.py
+++ b/solution.py
@@ -14,7 +14,7 @@
 F32 = jnp.float32
 BF16 = jnp.bfloat16
 ROW_TILE = 1024
-COL_TILE = 512
+COL_TILE = 1024
 
 
 def moved(x, target):

time: 91 us -> 91 us (level)
  no operation moved by 1% of the time
where the time goes in v7:
time: 91 us; the launch traced here: 90.8 us
  starting transfers between devices  30.6 us (34%)
  Pallas kernels  27.1 us (30%)
  waiting for transfers between devices  25.9 us (28%)
  local copies, waits for them, and re-layouts  3.19 us (4%)
  other arithmetic  2.46 us (3%)
  between operations  1.56 us (2%)
    ppermute x17, starting transfers between devices, moved(): return lax.ppermute(x, ('blk', 'feat'), route)  30.6 us
    ppermute x17, waiting for transfers between devices, moved(): return lax.ppermute(x, ('blk', 'feat'), route)  25.9 us
    pallas_call x5, Pallas kernels, call(): pl.pallas_call(body, out_shape=outs, in_specs=[vmem] * len(operands), out...  25.1 us
    unnamed x14, local copies, waits for them, and re-layouts  1.95 us
  transfers between devices with their start and end apart: 17, of which 8 were waited for; matrix products, arithmetic and copies ran while one was open for 3% of the time, Pallas kernels for 22%

profile of v7, /device:TPU:0, one launch (start us, length us, event | category | flops | bytes accessed | tf_op | source)
XLA Modules:
  0.0 90.8 jit_solution(10091478212850798083)
XLA Ops:
  0.7 1.7 %shard_map.85.packed = bf16[64,2176]{1,0:T(8,128)(2,1)} custom-call(bf16[64,2048]{1,0:T(8,128)(2,1)} %bitcast.14, bf16[64,128]{1,0:T(8,128)(2,1)} %bitcast.15), custom_call_target="tpu_custom_call" | custom-call | tf_op jit(solution)/shard_map/pallas_call | solution.py:223
  2.4 3.3 %collective-permute-start = (bf16[64,2176]{1,0:T(8,128)(2,1)}, bf16[64,2176]{1,0:T(8,128)(2,1)S(1)}, u32[]{:S(2)}, u32[]{:S(2)}) collective-permute-start(bf16[64,2176]{1,0:T(8,128)(2,1)} %shard_map.85.packed), channel_id=1, source_target_pairs={{0,1},{1,0},{2,3},{3,2},{4,5},{5,4},{6,7},{7,6},{8,9},{9,8},{10,11... | collective-permute-start | bytes 835592 | tf_op jit(solution)/shard_map/ppermute | solution.py:27
  5.7 0.6 fusion.3
  6.3 0.6 fusion.4
  7.0 0.3 broadcast_multiply_fusion.mb
  7.3 5.6 %collective-permute-start.7 = (bf16[2048,128]{1,0:T(8,128)(2,1)S(1)}, bf16[2048,128]{1,0:T(8,128)(2,1)S(1)}, u32[]{:S(2)}, u32[]{:S(2)}) collective-permute-start(bf16[2048,128]{1,0:T(8,128)(2,1)S(1)} %broadcast_multiply_fusion.mb), channel_id=1, source_target_pairs={{0,126},{1,127},{2,0},{3,1},{4,2},{5,3},{6,4},{7,5},{8,6},{9,7},{1... | collective-permute-start | bytes 1572872 | tf_op jit(solution)/shard_map/ppermute | solution.py:27
  12.9 0.0 collective-permute-start.5
  13.6 0.0 copy-start.5
  13.6 0.7 copy-done.5
  14.3 0.2 shard_map.86
  14.6 0.0 copy-start.1
  14.6 0.6 copy-done.1
  15.2 6.0 %collective-permute-start.8 = (bf16[128,2048]{1,0:T(8,128)(2,1)S(1)}, bf16[128,2048]{1,0:T(8,128)(2,1)S(1)}, u32[]{:S(2)}, u32[]{:S(2)}) collective-permute-start(bf16[128,2048]{1,0:T(8,128)(2,1)S(1)} %get-tuple-element.47.sb), channel_id=1, source_target_pairs={{0,126},{1,127},{2,0},{3,1},{4,2},{5,3},{6,4},{7,5},{8,6},{9,7},{1... | collective-permute-start | bytes 1572872 | tf_op jit(solution)/shard_map/ppermute | solution.py:27
  21.2 0.1 collective-permute-start.6
  21.2 0.7 copy-done.2
  21.9 4.9 %shard_map.87 = (f32[1024,128]{1,0:T(8,128)S(1)}, f32[1024,32]{1,0:T(8,128)S(1)}, bf16[1024,64]{1,0:T(8,128)(2,1)S(1)}, bf16[1024,256]{1,0:T(8,128)(2,1)S(1)}) custom-call(bf16[1024,128]{1,0:T(8,128)(2,1)S(1)} %constant_dynamic-slice_fusion.ma, bf16[128,1024]{1,0:T(8,128)(2,1)S(1)} %get-tuple-element.38.sa, bf16[2048,128]{1,0:T(8,128)(2,1)S(1)} %broadcast_multiply_fusion.mb, ...), custom_call_target="tpu_custom_call" | custom-call | flops 2147483648 | bytes 1048576 | tf_op jit(solution)/shard_map/pallas_call | solution.py:185
  26.8 0.1 collective-permute-start.3
  26.9 0.0 collective-permute-done.7.mb
  26.9 0.1 collective-permute-start.4
  27.0 0.0 collective-permute-done.5.mb
  27.0 2.0 %collective-permute-start.1 = (bf16[2048,128]{1,0:T(8,128)(2,1)S(1)}, bf16[2048,128]{1,0:T(8,128)(2,1)S(1)}, u32[]{:S(2)}, u32[]{:S(2)}) collective-permute-start(bf16[2048,128]{1,0:T(8,128)(2,1)S(1)} %broadcast_multiply_fusion.mb), channel_id=1, source_target_pairs={{0,4},{1,5},{2,6},{3,7},{4,8},{5,9},{6,10},{7,11},{8,12},{9,13},{1... | collective-permute-start | bytes 1572872 | tf_op jit(solution)/shard_map/ppermute | solution.py:27
  29.0 0.0 collective-permute-done.8.sb
  29.0 1.9 %collective-permute-start.2 = (bf16[128,2048]{1,0:T(8,128)(2,1)S(1)}, bf16[128,2048]{1,0:T(8,128)(2,1)S(1)}, u32[]{:S(2)}, u32[]{:S(2)}) collective-permute-start(bf16[128,2048]{1,0:T(8,128)(2,1)S(1)} %get-tuple-element.47.sb), channel_id=1, source_target_pairs={{0,4},{1,5},{2,6},{3,7},{4,8},{5,9},{6,10},{7,11},{8,12},{9,13},{1... | collective-permute-start | bytes 1572872 | tf_op jit(solution)/shard_map/ppermute | solution.py:27
  31.0 4.9 %shard_map.88 = (f32[1024,128]{1,0:T(8,128)S(1)}, f32[1024,32]{1,0:T(8,128)S(1)}) custom-call(bf16[1024,64]{1,0:T(8,128)(2,1)S(1)} %get-tuple-element.42.near_dist, bf16[1024,256]{1,0:T(8,128)(2,1)S(1)} %get-tuple-element.43.near_mix, bf16[2048,128]{1,0:T(8,128)(2,1)S(1)} %collective-permute-done.7.mb, ...), custom_call_target="tpu_custom_call", output_to_operand_aliasing={{0}: (6, {}), {1}: (7, {})} | custom-call | flops 2147483648 | bytes 1048576 | tf_op jit(solution)/shard_map/pallas_call | solution.py:185
  35.9 0.0 collective-permute-done.6.sb
  35.9 4.9 %shard_map.89 = (f32[1024,128]{1,0:T(8,128)S(1)}, f32[1024,32]{1,0:T(8,128)S(1)}) custom-call(bf16[1024,64]{1,0:T(8,128)(2,1)S(1)} %get-tuple-element.42.near_dist, bf16[1024,256]{1,0:T(8,128)(2,1)S(1)} %get-tuple-element.43.near_mix, bf16[2048,128]{1,0:T(8,128)(2,1)S(1)} %collective-permute-done.5.mb, ...), custom_call_target="tpu_custom_call", output_to_operand_aliasing={{0}: (6, {}), {1}: (7, {})} | custom-call | flops 2147483648 | bytes 1048576 | tf_op jit(solution)/shard_map/pallas_call | solution.py:185
  40.8 6.5 %collective-permute-done.4.sb = bf16[128,2048]{1,0:T(8,128)(2,1)S(1)} collective-permute-done((bf16[128,2048]{1,0:T(8,128)(2,1)S(1)}, bf16[128,2048]{1,0:T(8,128)(2,1)S(1)}, u32[]{:S(2)}, u32[]{:S(2)}) %collective-permute-start.4) | collective-permute-done | bytes 524320 | tf_op jit(solution)/shard_map/ppermute | solution.py:27
  47.3 5.2 %shard_map.90 = (f32[1024,128]{1,0:T(8,128)S(1)}, f32[1024,32]{1,0:T(8,128)S(1)}) custom-call(bf16[1024,64]{1,0:T(8,128)(2,1)S(1)} %get-tuple-element.42.near_dist, bf16[1024,256]{1,0:T(8,128)(2,1)S(1)} %get-tuple-element.43.near_mix, bf16[2048,128]{1,0:T(8,128)(2,1)S(1)} %collective-permute-done.3.mb, ...), custom_call_target="tpu_custom_call", output_to_operand_aliasing={{0}: (6, {}), {1}: (7, {})} | custom-call | flops 2147483648 | bytes 1048576 | tf_op jit(solution)/shard_map/pallas_call | solution.py:185
  52.5 0.5 collective-permute-done.2.sb
  52.9 5.2 %shard_map.91 = (f32[144,128]{1,0:T(8,128)S(1)}, bf16[64,1024]{1,0:T(8,128)(2,1)S(1)}, bf16[64,1024]{1,0:T(8,128)(2,1)S(1)}) custom-call(bf16[1024,64]{1,0:T(8,128)(2,1)S(1)} %get-tuple-element.42.near_dist, bf16[1024,256]{1,0:T(8,128)(2,1)S(1)} %get-tuple-element.43.near_mix, bf16[2048,128]{1,0:T(8,128)(2,1)S(1)} %collective-permute-done.1.mb, ...), custom_call_target="tpu_custom_call" | custom-call | flops 2147483648 | bytes 1048576 | tf_op jit(solution)/shard_map/pallas_call | solution.py:185
  58.2 1.4 %collective-permute-start.10 = (f32[144,128]{1,0:T(8,128)S(1)}, f32[144,128]{1,0:T(8,128)S(1)}, u32[]{:S(2)}, u32[]{:S(2)}) collective-permute-start(f32[144,128]{1,0:T(8,128)S(1)} %get-tuple-element.60), channel_id=1, source_target_pairs={{0,64},{1,65},{2,66},{3,67},{4,68},{5,69},{6,70},{7,71},{8,72},{9,... | collective-permute-start | bytes 221192 | tf_op jit(solution)/shard_map/ppermute | solution.py:27
  59.6 3.0 %collective-permute-done.10 = f32[144,128]{1,0:T(8,128)S(1)} collective-permute-done((f32[144,128]{1,0:T(8,128)S(1)}, f32[144,128]{1,0:T(8,128)S(1)}, u32[]{:S(2)}, u32[]{:S(2)}) %collective-permute-start.10) | collective-permute-done | bytes 73760 | tf_op jit(solution)/shard_map/ppermute | solution.py:27
  62.6 3.6 %collective-permute-start.11 = (f32[72,128]{1,0:T(8,128)S(1)}, f32[72,128]{1,0:T(8,128)S(1)}, u32[]{:S(2)}, u32[]{:S(2)}) collective-permute-start(f32[72,128]{1,0:T(8,128)S(1)} %slice.33), channel_id=1, source_target_pairs={{0,65},{1,64},{2,67},{3,66},{4,69},{5,68},{6,71},{7,70},{8,73},{9,... | collective-permute-start | bytes 110600 | tf_op jit(solution)/shard_map/ppermute | solution.py:27
  66.3 1.9 %collective-permute-done.11 = f32[72,128]{1,0:T(8,128)S(1)} collective-permute-done((f32[72,128]{1,0:T(8,128)S(1)}, f32[72,128]{1,0:T(8,128)S(1)}, u32[]{:S(2)}, u32[]{:S(2)}) %collective-permute-start.11) | collective-permute-done | bytes 36896 | tf_op jit(solution)/shard_map/ppermute | solution.py:27
  68.2 1.6 %collective-permute-start.12 = (f32[72,128]{1,0:T(8,128)S(1)}, f32[72,128]{1,0:T(8,128)S(1)}, u32[]{:S(2)}, u32[]{:S(2)}) collective-permute-start(f32[72,128]{1,0:T(8,128)S(1)} %slice_add_fusion), channel_id=1, source_target_pairs={{0,2},{1,3},{2,0},{3,1},{4,6},{5,7},{6,4},{7,5},{8,10},{9,11},{10,... | collective-permute-start | bytes 110600 | tf_op jit(solution)/shard_map/ppermute | solution.py:27
  69.8 1.4 %collective-permute-start.9 = (bf16[64,1024]{1,0:T(8,128)(2,1)S(1)}, bf16[64,1024]{1,0:T(8,128)(2,1)S(1)}, u32[]{:S(2)}, u32[]{:S(2)}) collective-permute-start(bf16[64,1024]{1,0:T(8,128)(2,1)S(1)} %get-tuple-element.59), channel_id=1, source_target_pairs={{0,1},{1,0},{2,3},{3,2},{4,5},{5,4},{6,7},{7,6},{8,9},{9,8},{10,11... | collective-permute-start | bytes 393224 | tf_op jit(solution)/shard_map/ppermute | solution.py:27
  71.2 0.1 collective-permute-start.13
  71.3 3.9 %collective-permute-done.13 = f32[72,128]{1,0:T(8,128)S(1)} collective-permute-done((f32[72,128]{1,0:T(8,128)S(1)}, f32[72,128]{1,0:T(8,128)S(1)}, u32[]{:S(2)}, u32[]{:S(2)}) %collective-permute-start.13) | collective-permute-done | bytes 36896 | tf_op jit(solution)/shard_map/ppermute | solution.py:27
  75.3 1.8 %collective-permute-start.14 = (f32[72,128]{1,0:T(8,128)S(1)}, f32[72,128]{1,0:T(8,128)S(1)}, u32[]{:S(2)}, u32[]{:S(2)}) collective-permute-start(f32[72,128]{1,0:T(8,128)S(1)} %add.40), channel_id=1, source_target_pairs={{0,12},{1,13},{2,14},{3,15},{4,8},{5,9},{6,10},{7,11},{8,4},{9,5},... | collective-permute-start | bytes 110600 | tf_op jit(solution)/shard_map/ppermute | solution.py:27
  77.1 3.3 %collective-permute-done.14 = f32[72,128]{1,0:T(8,128)S(1)} collective-permute-done((f32[72,128]{1,0:T(8,128)S(1)}, f32[72,128]{1,0:T(8,128)S(1)}, u32[]{:S(2)}, u32[]{:S(2)}) %collective-permute-start.14) | collective-permute-done | bytes 36896 | tf_op jit(solution)/shard_map/ppermute | solution.py:27
  80.5 0.1 collective-permute-start.15
  80.6 3.9 %collective-permute-done.15 = f32[72,128]{1,0:T(8,128)S(1)} collective-permute-done((f32[72,128]{1,0:T(8,128)S(1)}, f32[72,128]{1,0:T(8,128)S(1)}, u32[]{:S(2)}, u32[]{:S(2)}) %collective-permute-start.15) | collective-permute-done | bytes 36896 | tf_op jit(solution)/shard_map/ppermute | solution.py:27
  84.4 1.5 %collective-permute-start.16 = (f32[72,128]{1,0:T(8,128)S(1)}, f32[72,128]{1,0:T(8,128)S(1)}, u32[]{:S(2)}, u32[]{:S(2)}) collective-permute-start(f32[72,128]{1,0:T(8,128)S(1)} %add.42), channel_id=1, source_target_pairs={{0,48},{1,49},{2,50},{3,51},{4,52},{5,53},{6,54},{7,55},{8,56},{9,... | collective-permute-start | bytes 110600 | tf_op jit(solution)/shard_map/ppermute | solution.py:27
  86.0 0.0 collective-permute-done.9
  86.0 0.8 fusion
  86.8 2.8 %collective-permute-done.16 = f32[72,128]{1,0:T(8,128)S(1)} collective-permute-done((f32[72,128]{1,0:T(8,128)S(1)}, f32[72,128]{1,0:T(8,128)S(1)}, u32[]{:S(2)}, u32[]{:S(2)}) %collective-permute-start.16) | collective-permute-done | bytes 36896 | tf_op jit(solution)/shard_map/ppermute | solution.py:27
  89.6 0.6 slice_bitcast_fusion
  90.2 0.6 slice_bitcast_fusion.1
  (26 shorter events, 0.1 us)
Async XLA Ops:
  0.6 6.4 %copy-start.3 = (bf16[2048,128]{1,0:T(8,128)(2,1)S(1)}, bf16[2048,128]{1,0:T(8,128)(2,1)}, u32[]{:S(2)}) copy-start(bf16[2048,128]{1,0:T(8,128)(2,1)} %param.8) | copy-start | bytes 1572868
  0.6 5.0 %copy-start.6 = (s32[64]{0:T(128)S(1)}, s32[64]{0:T(128)}, u32[]{:S(2)}) copy-start(s32[64]{0:T(128)} %param.13) | copy-start | bytes 772
  2.4 3.9 %copy-start.4 = (s32[2048]{0:T(1024)S(1)}, s32[2048]{0:T(1024)}, u32[]{:S(2)}) copy-start(s32[2048]{0:T(1024)} %param.12) | copy-start | bytes 24580
  2.4 11.9 %collective-permute-start = (bf16[64,2176]{1,0:T(8,128)(2,1)}, bf16[64,2176]{1,0:T(8,128)(2,1)S(1)}, u32[]{:S(2)}, u32[]{:S(2)}) collective-permute-start(bf16[64,2176]{1,0:T(8,128)(2,1)} %shard_map.85.packed), channel_id=1, source_target_pairs={{0,1},{1,0},{2,3},{3,2},{4,5},{5,4},{6,7},{7,6},{8,9},{9,8},{10,11... | collective-permute-start | bytes 835592 | tf_op jit(solution)/shard_map/ppermute | solution.py:27
  7.0 7.3 %copy-start = (bf16[64,2176]{1,0:T(8,128)(2,1)S(1)}, bf16[64,2176]{1,0:T(8,128)(2,1)}, u32[]{:S(2)}) copy-start(bf16[64,2176]{1,0:T(8,128)(2,1)} %shard_map.85.packed) | copy-start | bytes 835588
  7.3 19.6 %collective-permute-start.7 = (bf16[2048,128]{1,0:T(8,128)(2,1)S(1)}, bf16[2048,128]{1,0:T(8,128)(2,1)S(1)}, u32[]{:S(2)}, u32[]{:S(2)}) collective-permute-start(bf16[2048,128]{1,0:T(8,128)(2,1)S(1)} %broadcast_multiply_fusion.mb), channel_id=1, source_target_pairs={{0,126},{1,127},{2,0},{3,1},{4,2},{5,3},{6,4},{7,5},{8,6},{9,7},{1... | collective-permute-start | bytes 1572872 | tf_op jit(solution)/shard_map/ppermute | solution.py:27
  12.9 14.1 %collective-permute-start.5 = (bf16[2048,128]{1,0:T(8,128)(2,1)S(1)}, bf16[2048,128]{1,0:T(8,128)(2,1)S(1)}, u32[]{:S(2)}, u32[]{:S(2)}) collective-permute-start(bf16[2048,128]{1,0:T(8,128)(2,1)S(1)} %broadcast_multiply_fusion.mb), channel_id=1, source_target_pairs={{0,2},{1,3},{2,4},{3,5},{4,6},{5,7},{6,8},{7,9},{8,10},{9,11},{10,... | collective-permute-start | bytes 1572872 | tf_op jit(solution)/shard_map/ppermute | solution.py:27
  13.6 0.7 copy-start.5
  14.6 0.6 copy-start.1
  15.2 13.8 %collective-permute-start.8 = (bf16[128,2048]{1,0:T(8,128)(2,1)S(1)}, bf16[128,2048]{1,0:T(8,128)(2,1)S(1)}, u32[]{:S(2)}, u32[]{:S(2)}) collective-permute-start(bf16[128,2048]{1,0:T(8,128)(2,1)S(1)} %get-tuple-element.47.sb), channel_id=1, source_target_pairs={{0,126},{1,127},{2,0},{3,1},{4,2},{5,3},{6,4},{7,5},{8,6},{9,7},{1... | collective-permute-start | bytes 1572872 | tf_op jit(solution)/shard_map/ppermute | solution.py:27
  21.1 0.8 copy-start.2
  21.2 14.7 %collective-permute-start.6 = (bf16[128,2048]{1,0:T(8,128)(2,1)S(1)}, bf16[128,2048]{1,0:T(8,128)(2,1)S(1)}, u32[]{:S(2)}, u32[]{:S(2)}) collective-permute-start(bf16[128,2048]{1,0:T(8,128)(2,1)S(1)} %get-tuple-element.47.sb), channel_id=1, source_target_pairs={{0,2},{1,3},{2,4},{3,5},{4,6},{5,7},{6,8},{7,9},{8,10},{9,11},{10,... | collective-permute-start | bytes 1572872 | tf_op jit(solution)/shard_map/ppermute | solution.py:27
  26.8 14.0 %collective-permute-start.3 = (bf16[2048,128]{1,0:T(8,128)(2,1)S(1)}, bf16[2048,128]{1,0:T(8,128)(2,1)S(1)}, u32[]{:S(2)}, u32[]{:S(2)}) collective-permute-start(bf16[2048,128]{1,0:T(8,128)(2,1)S(1)} %broadcast_multiply_fusion.mb), channel_id=1, source_target_pairs={{0,124},{1,125},{2,126},{3,127},{4,0},{5,1},{6,2},{7,3},{8,4},{9,5... | collective-permute-start | bytes 1572872 | tf_op jit(solution)/shard_map/ppermute | solution.py:27
  26.9 20.4 %collective-permute-start.4 = (bf16[128,2048]{1,0:T(8,128)(2,1)S(1)}, bf16[128,2048]{1,0:T(8,128)(2,1)S(1)}, u32[]{:S(2)}, u32[]{:S(2)}) collective-permute-start(bf16[128,2048]{1,0:T(8,128)(2,1)S(1)} %get-tuple-element.47.sb), channel_id=1, source_target_pairs={{0,124},{1,125},{2,126},{3,127},{4,0},{5,1},{6,2},{7,3},{8,4},{9,5... | collective-permute-start | bytes 1572872 | tf_op jit(solution)/shard_map/ppermute | solution.py:27
  27.0 25.4 %collective-permute-start.1 = (bf16[2048,128]{1,0:T(8,128)(2,1)S(1)}, bf16[2048,128]{1,0:T(8,128)(2,1)S(1)}, u32[]{:S(2)}, u32[]{:S(2)}) collective-permute-start(bf16[2048,128]{1,0:T(8,128)(2,1)S(1)} %broadcast_multiply_fusion.mb), channel_id=1, source_target_pairs={{0,4},{1,5},{2,6},{3,7},{4,8},{5,9},{6,10},{7,11},{8,12},{9,13},{1... | collective-permute-start | bytes 1572872 | tf_op jit(solution)/shard_map/ppermute | solution.py:27
  29.0 23.9 %collective-permute-start.2 = (bf16[128,2048]{1,0:T(8,128)(2,1)S(1)}, bf16[128,2048]{1,0:T(8,128)(2,1)S(1)}, u32[]{:S(2)}, u32[]{:S(2)}) collective-permute-start(bf16[128,2048]{1,0:T(8,128)(2,1)S(1)} %get-tuple-element.47.sb), channel_id=1, source_target_pairs={{0,4},{1,5},{2,6},{3,7},{4,8},{5,9},{6,10},{7,11},{8,12},{9,13},{1... | collective-permute-start | bytes 1572872 | tf_op jit(solution)/shard_map/ppermute | solution.py:27
  58.2 4.4 %collective-permute-start.10 = (f32[144,128]{1,0:T(8,128)S(1)}, f32[144,128]{1,0:T(8,128)S(1)}, u32[]{:S(2)}, u32[]{:S(2)}) collective-permute-start(f32[144,128]{1,0:T(8,128)S(1)} %get-tuple-element.60), channel_id=1, source_target_pairs={{0,64},{1,65},{2,66},{3,67},{4,68},{5,69},{6,70},{7,71},{8,72},{9,... | collective-permute-start | bytes 221192 | tf_op jit(solution)/shard_map/ppermute | solution.py:27
  62.6 5.6 %collective-permute-start.11 = (f32[72,128]{1,0:T(8,128)S(1)}, f32[72,128]{1,0:T(8,128)S(1)}, u32[]{:S(2)}, u32[]{:S(2)}) collective-permute-start(f32[72,128]{1,0:T(8,128)S(1)} %slice.33), channel_id=1, source_target_pairs={{0,65},{1,64},{2,67},{3,66},{4,69},{5,68},{6,71},{7,70},{8,73},{9,... | collective-permute-start | bytes 110600 | tf_op jit(solution)/shard_map/ppermute | solution.py:27
  68.2 3.0 %collective-permute-start.12 = (f32[72,128]{1,0:T(8,128)S(1)}, f32[72,128]{1,0:T(8,128)S(1)}, u32[]{:S(2)}, u32[]{:S(2)}) collective-permute-start(f32[72,128]{1,0:T(8,128)S(1)} %slice_add_fusion), channel_id=1, source_target_pairs={{0,2},{1,3},{2,0},{3,1},{4,6},{5,7},{6,4},{7,5},{8,10},{9,11},{10,... | collective-permute-start | bytes 110600 | tf_op jit(solution)/shard_map/ppermute | solution.py:27
  69.8 16.2 %collective-permute-start.9 = (bf16[64,1024]{1,0:T(8,128)(2,1)S(1)}, bf16[64,1024]{1,0:T(8,128)(2,1)S(1)}, u32[]{:S(2)}, u32[]{:S(2)}) collective-permute-start(bf16[64,1024]{1,0:T(8,128)(2,1)S(1)} %get-tuple-element.59), channel_id=1, source_target_pairs={{0,1},{1,0},{2,3},{3,2},{4,5},{5,4},{6,7},{7,6},{8,9},{9,8},{10,11... | collective-permute-start | bytes 393224 | tf_op jit(solution)/shard_map/ppermute | solution.py:27
  71.2 4.0 %collective-permute-start.13 = (f32[72,128]{1,0:T(8,128)S(1)}, f32[72,128]{1,0:T(8,128)S(1)}, u32[]{:S(2)}, u32[]{:S(2)}) collective-permute-start(f32[72,128]{1,0:T(8,128)S(1)} %add.39), channel_id=1, source_target_pairs={{0,4},{1,5},{2,6},{3,7},{4,0},{5,1},{6,2},{7,3},{8,12},{9,13},{10,... | collective-permute-start | bytes 110600 | tf_op jit(solution)/shard_map/ppermute | solution.py:27
  75.3 5.2 %collective-permute-start.14 = (f32[72,128]{1,0:T(8,128)S(1)}, f32[72,128]{1,0:T(8,128)S(1)}, u32[]{:S(2)}, u32[]{:S(2)}) collective-permute-start(f32[72,128]{1,0:T(8,128)S(1)} %add.40), channel_id=1, source_target_pairs={{0,12},{1,13},{2,14},{3,15},{4,8},{5,9},{6,10},{7,11},{8,4},{9,5},... | collective-permute-start | bytes 110600 | tf_op jit(solution)/shard_map/ppermute | solution.py:27
  80.5 4.0 %collective-permute-start.15 = (f32[72,128]{1,0:T(8,128)S(1)}, f32[72,128]{1,0:T(8,128)S(1)}, u32[]{:S(2)}, u32[]{:S(2)}) collective-permute-start(f32[72,128]{1,0:T(8,128)S(1)} %add.41), channel_id=1, source_target_pairs={{0,16},{1,17},{2,18},{3,19},{4,20},{5,21},{6,22},{7,23},{8,24},{9,... | collective-permute-start | bytes 110600 | tf_op jit(solution)/shard_map/ppermute | solution.py:27
  84.4 5.2 %collective-permute-start.16 = (f32[72,128]{1,0:T(8,128)S(1)}, f32[72,128]{1,0:T(8,128)S(1)}, u32[]{:S(2)}, u32[]{:S(2)}) collective-permute-start(f32[72,128]{1,0:T(8,128)S(1)} %add.42), channel_id=1, source_target_pairs={{0,48},{1,49},{2,50},{3,51},{4,52},{5,53},{6,54},{7,55},{8,56},{9,... | collective-permute-start | bytes 110600 | tf_op jit(solution)/shard_map/ppermute | solution.py:27
